TPU v7x, 32 devices: a whole 2x2x4 slice. The times are simulated.
32 devices in a mesh: gz: 2 (over core), gy: 8 (over z, y), gx: 2 (over x).
Axes of the slice: x: 2, y: 2, z: 4, core: 2. Of those that a mesh axis runs over, the one named last changes fastest.
Arguments:
- fixed: bfloat16 [32, 512, 256], P('gz', 'gy', 'gx'), may hold values from -6 to 6
- moving: bfloat16 [32, 512, 256], P('gz', 'gy', 'gx'), may hold values from -6 to 6
- owners: int32 [2, 8, 2, 256, 1], P('gz', 'gy', 'gx'), may hold values from 0 to 15; in each aligned block of 256 rows (0 to 255, 256 to 511, ..., all dimensions but the last counted through in order) at most 32 rows name the same one
- block_ids: int32 [2, 8, 2, 256], P('gz', 'gy', 'gx'), may hold values from 0 to 127
- counts: int32 [2, 8, 2, 128], P('gz', 'gy', 'gx'), may hold values from 1 to 2
- mix_yx: bfloat16 [2, 8, 2, 256, 128, 128], P('gz', 'gy', 'gx')
- mix_z: float32 [2, 8, 2, 256, 8, 8], P('gz', 'gy', 'gx')
Outputs:
- warped: float32 [32, 512, 256], P('gz', 'gy', 'gx')
- force: float32 [3, 32, 512, 256], P(None, 'gz', 'gy', 'gx')
Inputs may be any that keep to these rules, and one draw needn't show every extreme that they name: `owners`: owner o names the device with the same gz index, gy index o // 2 and gx index o % 2; within one device's 256 requests no owner is named more than 32 times.
All inputs are finite; a program needn't handle non-finite values.
Results may differ from a plain program's by a relative error of at most 0.00035.
Values may be sent and summed in bfloat16 or wider, within the bound.
No kernel may reach another device: no remote copies, remote signals or barrier semaphores. Data moves between devices by JAX's collectives and lax.ppermute only.
A program may use at most 128 MiB of HBM per device.

v0:
```python
import jax
import jax.numpy as jnp
from jax import lax
from jax.sharding import PartitionSpec as P

VZ = 8
VY = 8
VX = 16
NBZ = 2
NBY = 8
NBX = 8
SOURCES = 2
RAD = 4
BV = 128
BLOCKS = 128
SLOTS = 256


def padded_2(block, sides, width):
    for axis, dim in sides:
        count = lax.axis_size(axis)
        forward = [(i, i + 1) for i in range(count - 1)]
        backward = [(target, source) for source, target in forward]
        low = lax.ppermute(
            lax.slice_in_dim(block, block.shape[dim] - width, None, axis=dim), axis, forward
        )
        high = lax.ppermute(lax.slice_in_dim(block, 0, width, axis=dim), axis, backward)
        block = jnp.concatenate([low, block, high], axis=dim)
    return block


def box_along(padded, axis):
    length = padded.shape[axis] - 2 * RAD
    total = lax.slice_in_dim(padded, 0, length, axis=axis)
    for shift in range(1, 2 * RAD + 1):
        total = total + lax.slice_in_dim(padded, shift, shift + length, axis=axis)
    return total


def to_blocks(brick):
    return (
        brick.reshape(NBZ, VZ, NBY, VY, NBX, VX)
        .transpose(0, 2, 4, 1, 3, 5)
        .reshape(NBZ * NBY * NBX, VZ, VY * VX)
    )


def from_blocks(blocks):
    return (
        blocks.reshape(NBZ, NBY, NBX, VZ, VY, VX)
        .transpose(0, 3, 1, 4, 2, 5)
        .reshape(NBZ * VZ, NBY * VY, NBX * VX)
    )


def per_device(fixed, moving, owners, block_ids, counts, mix_yx, mix_z):
    rows_gy = lax.axis_size("gy")
    cols_gx = lax.axis_size("gx")
    groups = rows_gy * cols_gx
    capacity = max(2, 2 * SLOTS // groups)
    owner = owners.reshape(-1)
    ident = block_ids.reshape(-1)
    used = counts.reshape(-1)
    slot_pos = jnp.arange(SLOTS, dtype=jnp.int32)
    earlier = (owner[:, None] == owner[None, :]) & (slot_pos[None, :] < slot_pos[:, None])
    rank = jnp.sum(earlier.astype(jnp.int32), axis=1)
    flat = owner * capacity + rank
    table = flat[:, None] == jnp.arange(groups * capacity, dtype=jnp.int32)[None, :]
    request = jnp.sum(jnp.where(table, ident[:, None], 0), axis=0).reshape(groups, capacity)
    mblocks = to_blocks(moving)
    picked = jnp.take(
        mblocks,
        lax.all_to_all(request, ("gy", "gx"), split_axis=0, concat_axis=0, tiled=True),
        axis=0,
    )
    received = lax.all_to_all(picked, ("gy", "gx"), split_axis=0, concat_axis=0, tiled=True)
    source = jnp.take(received.reshape(groups * capacity, VZ, BV), flat, axis=0)
    weights_yx = mix_yx.reshape(SLOTS, BV, BV)
    weights_z = mix_z.reshape(SLOTS, VZ, VZ)
    inplane = jnp.einsum("szc,scd->szd", source, weights_yx, preferred_element_type=jnp.float32)
    resampled = jnp.einsum("szy,syd->szd", weights_z, inplane, precision=lax.Precision.HIGHEST)
    keep = slot_pos % SOURCES < used[slot_pos // SOURCES]
    resampled = jnp.where(keep[:, None, None], resampled, jnp.float32(0.0))
    warped = from_blocks(resampled.reshape(BLOCKS, SOURCES, VZ, BV).sum(axis=1))
    image = fixed.astype(jnp.float32)
    fields = jnp.stack([image, warped, image * image, warped * warped, image * warped])
    padded = padded_2(fields, (("gz", 1),), RAD)
    sums = box_along(padded, 1)
    padded = padded_2(sums, (("gy", 2),), RAD)
    sums = box_along(padded, 2)
    padded = padded_2(sums, (("gx", 3),), RAD)
    sums = box_along(padded, 3)
    wpad = padded_2(warped, (("gz", 0), ("gy", 1), ("gx", 2)), 1)
    count = float((2 * RAD + 1) ** 3)
    mean_f = sums[0] / count
    mean_w = sums[1] / count
    cov = sums[4] / count - mean_f * mean_w
    var_f = sums[2] / count - mean_f * mean_f
    var_w = sums[3] / count - mean_w * mean_w
    deriv = (
        2.0
        * cov
        / ((var_f + 1e-05) * (var_w + 1e-05))
        * (image - mean_f - cov / (var_w + 1e-05) * (warped - mean_w))
    )
    slope_z = (wpad[2:, 1:-1, 1:-1] - wpad[:-2, 1:-1, 1:-1]) * 0.5
    slope_y = (wpad[1:-1, 2:, 1:-1] - wpad[1:-1, :-2, 1:-1]) * 0.5
    slope_x = (wpad[1:-1, 1:-1, 2:] - wpad[1:-1, 1:-1, :-2]) * 0.5
    force = jnp.stack([deriv * slope_z, deriv * slope_y, deriv * slope_x])
    return (warped, force)


def solution(mesh):
    return jax.shard_map(
        per_device,
        mesh=mesh,
        in_specs=(
            P("gz", "gy", "gx"),
            P("gz", "gy", "gx"),
            P("gz", "gy", "gx", None, None),
            P("gz", "gy", "gx", None),
            P("gz", "gy", "gx", None),
            P("gz", "gy", "gx", None, None, None),
            P("gz", "gy", "gx", None, None, None),
        ),
        out_specs=(P("gz", "gy", "gx"), P(None, "gz", "gy", "gx")),
        check_vma=False,
    )
```

profile of v0, /device:TPU:14, one launch (start us, length us, event | category | flops | bytes accessed | tf_op | source)
XLA Modules:
  0.0 164.7 jit_solution(679567138018058009)
XLA Ops:
  3.8 7.1 %all-to-all-start = ((s32[16,1,32]{2,1,0:T(1,128)}), s32[16,1,32]{2,1,0:T(1,128)S(1)}, u32[]{:S(2)}, u32[]{:S(2)}) async-start(s32[16,1,32]{2,1,0:T(1,128)} %all_to_all.13), calls=%async_computation | async-start | bytes 16384 | tf_op jit(solution)/shard_map/all_to_all | solution.py:73
  10.9 3.4 %reshape.192 = bf16[2,8,8,8,8,16]{5,4,3,2,1,0:T(8,128)(2,1)} reshape(bf16[16,64,128]{2,1,0:T(8,128)(2,1)} %param.8) | data formatting | bytes 524288 | tf_op jit(solution)/shard_map/reshape | solution.py:42
  14.4 2.2 %copy.41 = bf16[2,8,8,8,8,16]{5,3,1,4,2,0:T(8,128)(2,1)S(1)} copy(bf16[2,8,8,8,8,16]{5,4,3,2,1,0:T(8,128)(2,1)} %reshape.192) | data formatting | bytes 524288 | tf_op jit(solution)/shard_map/reshape | solution.py:42
  18.1 1.8 %gather_fusion.1 = bf16[512,8,128]{2,1,0:T(8,128)(2,1)S(1)} fusion(bf16[128,8,128]{2,1,0:T(8,128)(2,1)S(1)} %reshape.193, s32[1024]{0:T(1024)S(1)} %get-tuple-element.21), kind=kCustom, calls=%fused_computation.1 | custom fusion | bytes 2099200 | tf_op jit(solution)/shard_map/jit(_take)/gather | solution.py:71
  21.4 6.9 %all-to-all-start.1 = ((bf16[16,32,8,128]{3,2,1,0:T(8,128)(2,1)}), bf16[16,32,8,128]{3,2,1,0:T(8,128)(2,1)}, u32[]{:S(2)}, u32[]{:S(2)}) async-start(bf16[16,32,8,128]{3,2,1,0:T(8,128)(2,1)} %broadcast_select_fusion), calls=%async_computation.1 | async-start | bytes 2097152 | tf_op jit(solution)/shard_map/all_to_all | solution.py:76
  29.7 1.9 %gather_fusion = s32[256]{0:T(256)S(1)} fusion(s32[128]{0:T(128)S(1)} %bitcast.93, s32[1024]{0:T(1024)S(1)} %get-tuple-element.22), kind=kCustom, calls=%fused_computation | custom fusion | bytes 3072 | tf_op jit(solution)/shard_map/gather | solution.py:82
  31.6 20.7 %all-to-all-done.1 = bf16[16,32,8,128]{3,2,1,0:T(8,128)(2,1)} async-done(((bf16[16,32,8,128]{3,2,1,0:T(8,128)(2,1)}), bf16[16,32,8,128]{3,2,1,0:T(8,128)(2,1)}, u32[]{:S(2)}, u32[]{:S(2)}) %all-to-all-start.1) | async-done | bytes 1048608 | tf_op jit(solution)/shard_map/all_to_all | solution.py:76
  52.3 2.0 %gather_fusion.2 = bf16[256,8,128]{2,1,0:T(8,128)(2,1)S(1)} fusion(bf16[512,8,128]{2,1,0:T(8,128)(2,1)} %bitcast.8, s32[1024]{0:T(1024)S(1)} %pad_clamp_fusion), kind=kCustom, calls=%fused_computation.2 | custom fusion | bytes 1049600 | tf_op jit(solution)/shard_map/jit(_take)/gather | solution.py:77
  54.4 4.8 %fusion = f32[256,8,128]{2,1,0:T(8,128)S(1)} fusion(bf16[1,1,1,256,128,128]{5,4,3,2,1,0:T(8,128)(2,1)} %param.12, bf16[256,8,128]{2,1,0:T(8,128)(2,1)S(1)} %gather_fusion.2, pred[256]{0:T(512)(128)(4,1)S(1)} %get-tuple-element.4), kind=kOutput, calls=%fused_computation.3 | convolution fusion | flops 67371008 | bytes 9961728 | tf_op jit(solution)/shard_map/szc,scd->szd/dot_general | solution.py:80
  59.1 1.9 %bitcast_reduce_fusion = f32[128,8,128]{2,1,0:T(8,128)S(1)} fusion(f32[256,8,128]{2,1,0:T(8,128)S(1)} %fusion, f32[256,8,8]{2,1,0:T(8,128)S(1)} %copy-done.3, pred[256]{0:T(512)(128)(4,1)S(1)} %fusion.79), kind=kOutput, calls=%fused_computation.92 | convolution fusion | flops 25559040 | bytes 1638656 | tf_op jit(solution)/shard_map/szy,syd->szd/dot_general | solution.py:81
  61.0 2.6 %reshape.198 = f32[2,8,8,8,8,16]{5,4,3,2,1,0:T(8,128)} reshape(f32[128,8,128]{2,1,0:T(8,128)S(1)} %bitcast_reduce_fusion) | data formatting | bytes 1048576 | tf_op jit(solution)/shard_map/reshape | solution.py:50
  63.6 6.6 %copy.30 = f32[2,8,8,8,8,16]{5,4,3,2,1,0:T(8,128)} copy(f32[2,8,8,8,8,16]{5,3,1,4,2,0:T(8,128)} %bitcast.94) | data formatting | bytes 1048576 | tf_op jit(solution)/shard_map/transpose | solution.py:51
  70.2 3.9 %stack_reshape.3 = f32[1,16,64,128]{3,2,1,0:T(8,128)} reshape(f32[2,8,8,8,8,16]{5,4,3,2,1,0:T(8,128)} %copy.30) | data formatting | bytes 1048576 | tf_op jit(solution)/shard_map/stack;reshape | solution.py:86
  74.2 3.2 %reshape.199 = f32[16,64,128]{2,1,0:T(8,128)S(1)} reshape(f32[2,8,8,8,8,16]{5,4,3,2,1,0:T(8,128)} %copy.30) | data formatting | bytes 1048576 | tf_op jit(solution)/shard_map/reshape | solution.py:52
  83.0 2.3 %collective-permute-done.1 = f32[5,4,64,128]{3,2,1,0:T(8,128)S(1)} collective-permute-done((f32[5,4,64,128]{3,2,1,0:T(8,128)S(1)}, f32[5,4,64,128]{3,2,1,0:T(8,128)S(1)}, u32[]{:S(2)}, u32[]{:S(2)}) %collective-permute-start.1) | collective-permute-done | bytes 655392 | tf_op jit(solution)/shard_map/ppermute | solution.py:27
  85.3 2.9 %fusion.18 = f32[5,16,64,128]{3,2,1,0:T(8,128)S(1)} fusion(f32[5,16,64,128]{3,2,1,0:T(8,128)S(1)} %fusion.48, f32[5,4,64,128]{3,2,1,0:T(8,128)S(1)} %collective-permute-done.1, f32[5,4,64,128]{3,2,1,0:T(8,128)S(1)} %collective-permute-done), kind=kLoop, calls=%fused_computation.57 | loop fusion | flops 10485760 | bytes 6553600 | tf_op jit(solution)/shard_map/add | solution.py:36
  88.3 3.5 %collective-permute-start.2 = (f32[5,16,4,128]{3,2,1,0:T(4,128)S(1)}, f32[5,16,4,128]{3,2,1,0:T(4,128)S(1)}, u32[]{:S(2)}, u32[]{:S(2)}) collective-permute-start(f32[5,16,4,128]{3,2,1,0:T(4,128)S(1)} %get-tuple-element.8), channel_id=1, source_target_pairs={{0,2},{2,4},{4,6},{6,8},{8,10},{10,12},{12,14},{1,3},{3,5},{5,7},{... | collective-permute-start | bytes 491528 | tf_op jit(solution)/shard_map/ppermute | solution.py:24
  91.8 2.4 %collective-permute-start.3 = (f32[5,16,4,128]{3,2,1,0:T(4,128)S(1)}, f32[5,16,4,128]{3,2,1,0:T(4,128)S(1)}, u32[]{:S(2)}, u32[]{:S(2)}) collective-permute-start(f32[5,16,4,128]{3,2,1,0:T(4,128)S(1)} %get-tuple-element.9), channel_id=1, source_target_pairs={{2,0},{4,2},{6,4},{8,6},{10,8},{12,10},{14,12},{3,1},{5,3},{7,5},{... | collective-permute-start | bytes 491528 | tf_op jit(solution)/shard_map/ppermute | solution.py:27
  97.2 3.3 %collective-permute-done.3 = f32[5,16,4,128]{3,2,1,0:T(4,128)S(1)} collective-permute-done((f32[5,16,4,128]{3,2,1,0:T(4,128)S(1)}, f32[5,16,4,128]{3,2,1,0:T(4,128)S(1)}, u32[]{:S(2)}, u32[]{:S(2)}) %collective-permute-start.3) | collective-permute-done | bytes 163872 | tf_op jit(solution)/shard_map/ppermute | solution.py:27
  100.6 2.8 %fusion.4 = f32[5,16,64,128]{3,2,1,0:T(8,128)S(1)} fusion(f32[5,16,64,128]{3,2,1,0:T(8,128)S(1)} %fusion.18, f32[5,16,4,128]{3,2,1,0:T(4,128)S(1)} %collective-permute-done.3, f32[5,16,4,128]{3,2,1,0:T(4,128)S(1)} %collective-permute-done.2), kind=kLoop, calls=%fused_computation.43 | loop fusion | flops 10485760 | bytes 5570560 | tf_op jit(solution)/shard_map/add | solution.py:36
  103.3 3.2 %fusion.82 = (f32[5,16,64,4]{3,2,1,0:T(8,128)}, f32[5,16,64,4]{3,2,1,0:T(8,128)}) fusion(f32[5,16,64,128]{3,2,1,0:T(8,128)S(1)} %fusion.4), kind=kLoop, calls=%fused_computation.177 | loop fusion | bytes 327680 | tf_op jit(solution)/shard_map/slice | solution.py:25
  106.6 3.3 %copy.32 = f32[5,16,64,4]{2,1,3,0:T(8,128)} copy(f32[5,16,64,4]{3,2,1,0:T(8,128)} %get-tuple-element.6) | data formatting | bytes 163840 | tf_op jit(solution)/shard_map/slice | solution.py:25
  111.1 3.3 %copy.34 = f32[5,16,64,4]{2,1,3,0:T(8,128)} copy(f32[5,16,64,4]{3,2,1,0:T(8,128)} %get-tuple-element.7) | data formatting | bytes 163840 | tf_op jit(solution)/shard_map/slice | solution.py:27
  114.4 5.9 %collective-permute-start.5 = (f32[5,16,64,4]{2,1,3,0:T(8,128)}, f32[5,16,64,4]{2,1,3,0:T(8,128)}, u32[]{:S(2)}, u32[]{:S(2)}) collective-permute-start(f32[5,16,64,4]{2,1,3,0:T(8,128)} %copy.34), channel_id=1, source_target_pairs={{1,0},{3,2},{5,4},{7,6},{9,8},{11,10},{13,12},{15,14},{17,16},{19,... | collective-permute-start | bytes 245768 | tf_op jit(solution)/shard_map/ppermute | solution.py:27
  120.9 3.3 %copy.33 = f32[5,16,64,4]{3,2,1,0:T(8,128)} copy(f32[5,16,64,4]{2,1,3,0:T(8,128)} %collective-permute-done.4) | data formatting | bytes 163840 | tf_op jit(solution)/shard_map/ppermute | solution.py:24
  124.1 3.3 %copy.35 = f32[5,16,64,4]{3,2,1,0:T(8,128)} copy(f32[5,16,64,4]{2,1,3,0:T(8,128)} %collective-permute-done.5) | data formatting | bytes 163840 | tf_op jit(solution)/shard_map/ppermute | solution.py:27
  127.4 15.2 %fusion.32 = f32[5,16,64,128]{3,2,1,0:T(8,128)S(1)} fusion(f32[5,16,64,128]{3,2,1,0:T(8,128)S(1)} %fusion.4, f32[5,16,64,4]{3,2,1,0:T(8,128)} %copy.35, f32[5,16,64,4]{3,2,1,0:T(8,128)} %copy.33), kind=kLoop, calls=%fused_computation.71 | loop fusion | flops 10485760 | bytes 5406720 | tf_op jit(solution)/shard_map/add | solution.py:36
  144.0 3.0 %collective-permute-start.8 = (f32[18,1,128]{2,1,0:T(1,128)S(1)}, f32[18,1,128]{2,1,0:T(1,128)S(1)}, u32[]{:S(2)}, u32[]{:S(2)}) collective-permute-start(f32[18,1,128]{2,1,0:T(1,128)S(1)} %get-tuple-element.17), channel_id=1, source_target_pairs={{2,0},{4,2},{6,4},{8,6},{10,8},{12,10},{14,12},{3,1},{5,3},{7,5},{... | collective-permute-start | bytes 27656 | tf_op jit(solution)/shard_map/ppermute | solution.py:27
  147.0 3.7 %collective-permute-start.9 = (f32[18,1,128]{2,1,0:T(1,128)S(1)}, f32[18,1,128]{2,1,0:T(1,128)S(1)}, u32[]{:S(2)}, u32[]{:S(2)}) collective-permute-start(f32[18,1,128]{2,1,0:T(1,128)S(1)} %get-tuple-element.16), channel_id=1, source_target_pairs={{0,2},{2,4},{4,6},{6,8},{8,10},{10,12},{12,14},{1,3},{3,5},{5,7},{... | collective-permute-start | bytes 27656 | tf_op jit(solution)/shard_map/ppermute | solution.py:24
  150.8 1.8 %collective-permute-done.9 = f32[18,1,128]{2,1,0:T(1,128)S(1)} collective-permute-done((f32[18,1,128]{2,1,0:T(1,128)S(1)}, f32[18,1,128]{2,1,0:T(1,128)S(1)}, u32[]{:S(2)}, u32[]{:S(2)}) %collective-permute-start.9) | collective-permute-done | bytes 9248 | tf_op jit(solution)/shard_map/ppermute | solution.py:24
  153.2 3.5 %collective-permute-start.10 = (f32[18,66,1]{1,2,0:T(1,128)S(1)}, f32[18,66,1]{1,2,0:T(1,128)S(1)}, u32[]{:S(2)}, u32[]{:S(2)}) collective-permute-start(f32[18,66,1]{1,2,0:T(1,128)S(1)} %copy.36), channel_id=1, source_target_pairs={{1,0},{3,2},{5,4},{7,6},{9,8},{11,10},{13,12},{15,14},{17,16},{19,... | collective-permute-start | bytes 14264 | tf_op jit(solution)/shard_map/ppermute | solution.py:27
  158.6 3.9 %collective-permute-done.11 = f32[18,66,1]{1,2,0:T(1,128)S(1)} collective-permute-done((f32[18,66,1]{1,2,0:T(1,128)S(1)}, f32[18,66,1]{1,2,0:T(1,128)S(1)}, u32[]{:S(2)}, u32[]{:S(2)}) %collective-permute-start.11) | collective-permute-done | bytes 4784 | tf_op jit(solution)/shard_map/ppermute | solution.py:24
  (70 shorter events, 24.0 us)
Async XLA Ops:
  0.6 29.1 %copy-start = (s32[1,1,1,128]{3,2,1,0:T(1,128)S(1)}, s32[1,1,1,128]{3,2,1,0:T(1,128)}, u32[]{:S(2)}) copy-start(s32[1,1,1,128]{3,2,1,0:T(1,128)} %param.11) | copy-start | bytes 1540
  3.8 14.2 %all-to-all-start = ((s32[16,1,32]{2,1,0:T(1,128)}), s32[16,1,32]{2,1,0:T(1,128)S(1)}, u32[]{:S(2)}, u32[]{:S(2)}) async-start(s32[16,1,32]{2,1,0:T(1,128)} %all_to_all.13), calls=%async_computation | async-start | bytes 16384 | tf_op jit(solution)/shard_map/all_to_all | solution.py:73
  19.9 8.5 %copy-start.8 = (f32[1,1,1,256,8,8]{3,5,4,2,1,0:T(8,128)S(1)}, f32[1,1,1,256,8,8]{3,5,4,2,1,0:T(8,128)}, u32[]{:S(2)}) copy-start(f32[1,1,1,256,8,8]{3,5,4,2,1,0:T(8,128)} %param.13) | copy-start | bytes 196612
  19.9 9.7 %copy-start.9 = (s32[1,1,1,256,1]{3,4,2,1,0:T(1,128)S(1)}, s32[1,1,1,256,1]{3,4,2,1,0:T(1,128)}, u32[]{:S(2)}) copy-start(s32[1,1,1,256,1]{3,4,2,1,0:T(1,128)} %param.9) | copy-start | bytes 3076
  19.9 9.7 %copy-start.2 = (bf16[16,64,128]{2,1,0:T(8,128)(2,1)S(1)}, bf16[16,64,128]{2,1,0:T(8,128)(2,1)}, u32[]{:S(2)}) copy-start(bf16[16,64,128]{2,1,0:T(8,128)(2,1)} %param.7) | copy-start | bytes 786436
  21.4 30.9 %all-to-all-start.1 = ((bf16[16,32,8,128]{3,2,1,0:T(8,128)(2,1)}), bf16[16,32,8,128]{3,2,1,0:T(8,128)(2,1)}, u32[]{:S(2)}, u32[]{:S(2)}) async-start(bf16[16,32,8,128]{3,2,1,0:T(8,128)(2,1)} %broadcast_select_fusion), calls=%async_computation.1 | async-start | bytes 2097152 | tf_op jit(solution)/shard_map/all_to_all | solution.py:76
  54.3 4.8 %copy-start.3 = (f32[256,8,8]{2,1,0:T(8,128)S(1)}, f32[256,8,8]{2,1,0:T(8,128)}, u32[]{:S(2)}) copy-start(f32[256,8,8]{2,1,0:T(8,128)} %copy.29) | copy-start | bytes 196612
  77.4 65.3 %copy-start.1 = (f32[16,64,128]{2,1,0:T(8,128)}, f32[16,64,128]{2,1,0:T(8,128)S(1)}, u32[]{:S(2)}) copy-start(f32[16,64,128]{2,1,0:T(8,128)S(1)} %reshape.199) | copy-start | bytes 1572868
  80.0 3.0 %collective-permute-start = (f32[5,4,64,128]{3,2,1,0:T(8,128)S(1)}, f32[5,4,64,128]{3,2,1,0:T(8,128)S(1)}, u32[]{:S(2)}, u32[]{:S(2)}) collective-permute-start(f32[5,4,64,128]{3,2,1,0:T(8,128)S(1)} %get-tuple-element.10), channel_id=1, source_target_pairs={{0,16},{1,17},{2,18},{3,19},{4,20},{5,21},{6,22},{7,23},{8,24},{9,... | collective-permute-start | bytes 1966088 | tf_op jit(solution)/shard_map/ppermute | solution.py:24
  81.3 4.0 %collective-permute-start.1 = (f32[5,4,64,128]{3,2,1,0:T(8,128)S(1)}, f32[5,4,64,128]{3,2,1,0:T(8,128)S(1)}, u32[]{:S(2)}, u32[]{:S(2)}) collective-permute-start(f32[5,4,64,128]{3,2,1,0:T(8,128)S(1)} %get-tuple-element.11), channel_id=1, source_target_pairs={{16,0},{17,1},{18,2},{19,3},{20,4},{21,5},{22,6},{23,7},{24,8},{25... | collective-permute-start | bytes 1966088 | tf_op jit(solution)/shard_map/ppermute | solution.py:27
  88.3 8.9 %collective-permute-start.2 = (f32[5,16,4,128]{3,2,1,0:T(4,128)S(1)}, f32[5,16,4,128]{3,2,1,0:T(4,128)S(1)}, u32[]{:S(2)}, u32[]{:S(2)}) collective-permute-start(f32[5,16,4,128]{3,2,1,0:T(4,128)S(1)} %get-tuple-element.8), channel_id=1, source_target_pairs={{0,2},{2,4},{4,6},{6,8},{8,10},{10,12},{12,14},{1,3},{3,5},{5,7},{... | collective-permute-start | bytes 491528 | tf_op jit(solution)/shard_map/ppermute | solution.py:24
  91.8 8.8 %collective-permute-start.3 = (f32[5,16,4,128]{3,2,1,0:T(4,128)S(1)}, f32[5,16,4,128]{3,2,1,0:T(4,128)S(1)}, u32[]{:S(2)}, u32[]{:S(2)}) collective-permute-start(f32[5,16,4,128]{3,2,1,0:T(4,128)S(1)} %get-tuple-element.9), channel_id=1, source_target_pairs={{2,0},{4,2},{6,4},{8,6},{10,8},{12,10},{14,12},{3,1},{5,3},{7,5},{... | collective-permute-start | bytes 491528 | tf_op jit(solution)/shard_map/ppermute | solution.py:27
  94.2 26.0 %collective-permute-start.7 = (f32[1,64,128]{2,1,0:T(8,128)S(1)}, f32[1,64,128]{2,1,0:T(8,128)S(1)}, u32[]{:S(2)}, u32[]{:S(2)}) collective-permute-start(f32[1,64,128]{2,1,0:T(8,128)S(1)} %get-tuple-element.20), channel_id=1, source_target_pairs={{0,16},{1,17},{2,18},{3,19},{4,20},{5,21},{6,22},{7,23},{8,24},{9,... | collective-permute-start | bytes 98312 | tf_op jit(solution)/shard_map/ppermute | solution.py:24
  95.7 47.0 %collective-permute-start.6 = (f32[1,64,128]{2,1,0:T(8,128)S(1)}, f32[1,64,128]{2,1,0:T(8,128)S(1)}, u32[]{:S(2)}, u32[]{:S(2)}) collective-permute-start(f32[1,64,128]{2,1,0:T(8,128)S(1)} %get-tuple-element.19), channel_id=1, source_target_pairs={{16,0},{17,1},{18,2},{19,3},{20,4},{21,5},{22,6},{23,7},{24,8},{25... | collective-permute-start | bytes 98312 | tf_op jit(solution)/shard_map/ppermute | solution.py:27
  109.8 11.0 %collective-permute-start.4 = (f32[5,16,64,4]{2,1,3,0:T(8,128)}, f32[5,16,64,4]{2,1,3,0:T(8,128)}, u32[]{:S(2)}, u32[]{:S(2)}) collective-permute-start(f32[5,16,64,4]{2,1,3,0:T(8,128)} %copy.32), channel_id=1, source_target_pairs={{0,1},{2,3},{4,5},{6,7},{8,9},{10,11},{12,13},{14,15},{16,17},{18,... | collective-permute-start | bytes 245768 | tf_op jit(solution)/shard_map/ppermute | solution.py:24
  114.4 9.8 %collective-permute-start.5 = (f32[5,16,64,4]{2,1,3,0:T(8,128)}, f32[5,16,64,4]{2,1,3,0:T(8,128)}, u32[]{:S(2)}, u32[]{:S(2)}) collective-permute-start(f32[5,16,64,4]{2,1,3,0:T(8,128)} %copy.34), channel_id=1, source_target_pairs={{1,0},{3,2},{5,4},{7,6},{9,8},{11,10},{13,12},{15,14},{17,16},{19,... | collective-permute-start | bytes 245768 | tf_op jit(solution)/shard_map/ppermute | solution.py:27
  127.4 15.3 %copy-start.4 = (f32[18,64,128]{2,1,0:T(8,128)S(1)}, f32[18,64,128]{2,1,0:T(8,128)}, u32[]{:S(2)}) copy-start(f32[18,64,128]{2,1,0:T(8,128)} %constant_dynamic-update-slice_fusion.3) | copy-start | bytes 1769476
  144.0 8.9 %copy-start.5 = (f32[18,64,128]{2,1,0:T(8,128)}, f32[18,64,128]{2,1,0:T(8,128)S(1)}, u32[]{:S(2)}) copy-start(f32[18,64,128]{2,1,0:T(8,128)S(1)} %constant_dynamic-update-slice_fusion.1) | copy-start | bytes 1769476
  144.0 6.8 %collective-permute-start.8 = (f32[18,1,128]{2,1,0:T(1,128)S(1)}, f32[18,1,128]{2,1,0:T(1,128)S(1)}, u32[]{:S(2)}, u32[]{:S(2)}) collective-permute-start(f32[18,1,128]{2,1,0:T(1,128)S(1)} %get-tuple-element.17), channel_id=1, source_target_pairs={{2,0},{4,2},{6,4},{8,6},{10,8},{12,10},{14,12},{3,1},{5,3},{7,5},{... | collective-permute-start | bytes 27656 | tf_op jit(solution)/shard_map/ppermute | solution.py:27
  147.0 5.6 %collective-permute-start.9 = (f32[18,1,128]{2,1,0:T(1,128)S(1)}, f32[18,1,128]{2,1,0:T(1,128)S(1)}, u32[]{:S(2)}, u32[]{:S(2)}) collective-permute-start(f32[18,1,128]{2,1,0:T(1,128)S(1)} %get-tuple-element.16), channel_id=1, source_target_pairs={{0,2},{2,4},{4,6},{6,8},{8,10},{10,12},{12,14},{1,3},{3,5},{5,7},{... | collective-permute-start | bytes 27656 | tf_op jit(solution)/shard_map/ppermute | solution.py:24
  152.7 10.2 %copy-start.7 = (f32[16,64,128]{2,1,0:T(8,128)S(1)}, f32[16,64,128]{2,1,0:T(8,128)}, u32[]{:S(2)}) copy-start(f32[16,64,128]{2,1,0:T(8,128)} %get-tuple-element.3) | copy-start | bytes 1572868
  152.9 10.0 %copy-start.6 = (f32[18,64,128]{2,1,0:T(8,128)S(1)}, f32[18,64,128]{2,1,0:T(8,128)}, u32[]{:S(2)}) copy-start(f32[18,64,128]{2,1,0:T(8,128)} %copy-done.5) | copy-start | bytes 1769476
  153.2 5.1 %collective-permute-start.10 = (f32[18,66,1]{1,2,0:T(1,128)S(1)}, f32[18,66,1]{1,2,0:T(1,128)S(1)}, u32[]{:S(2)}, u32[]{:S(2)}) collective-permute-start(f32[18,66,1]{1,2,0:T(1,128)S(1)} %copy.36), channel_id=1, source_target_pairs={{1,0},{3,2},{5,4},{7,6},{9,8},{11,10},{13,12},{15,14},{17,16},{19,... | collective-permute-start | bytes 14264 | tf_op jit(solution)/shard_map/ppermute | solution.py:27
  157.0 5.6 %collective-permute-start.11 = (f32[18,66,1]{1,2,0:T(1,128)S(1)}, f32[18,66,1]{1,2,0:T(1,128)S(1)}, u32[]{:S(2)}, u32[]{:S(2)}) collective-permute-start(f32[18,66,1]{1,2,0:T(1,128)S(1)} %copy.38), channel_id=1, source_target_pairs={{0,1},{2,3},{4,5},{6,7},{8,9},{10,11},{12,13},{14,15},{16,17},{18,... | collective-permute-start | bytes 14264 | tf_op jit(solution)/shard_map/ppermute | solution.py:24
where the time goes:
time: 167 us; the launch traced here: 165 us
  local copies, waits for them, and re-layouts  51 us (31%)
  starting transfers between devices  44.2 us (26%)
  waiting for transfers between devices  32.4 us (19%)
  other arithmetic  29.3 us (18%)
  matrix products  6.66 us (4%)
    add x3, other arithmetic, box_along(): total = total + lax.slice_in_dim(padded, shift, shift + length, axis=axis)  20.9 us
    all_to_all x1, waiting for transfers between devices, per_device(): lax.all_to_all(picked, ('gy', 'gx'), split_axis=0, concat_axis=0, tiled=T...  20.7 us
    ppermute x6, starting transfers between devices, padded_2(): lax.ppermute(lax.slice_in_dim(block, 0, width, axis=dim), axis, backward)  17.6 us
    ppermute x6, starting transfers between devices, padded_2(): lax.ppermute(lax.slice_in_dim(block, block.shape[dim] - width, None, axis...  12.6 us
    all_to_all x1, starting transfers between devices, per_device(): lax.all_to_all(request, ('gy', 'gx'), split_axis=0, concat_axis=0, tiled=...  7.14 us
    slice x6, local copies, waits for them, and re-layouts, padded_2(): lax.slice_in_dim(block, block.shape[dim] - width, None, axis=dim)  6.92 us
    all_to_all x1, starting transfers between devices, per_device(): lax.all_to_all(picked, ('gy', 'gx'), split_axis=0, concat_axis=0, tiled=T...  6.92 us
    transpose x1, local copies, waits for them, and re-layouts, from_blocks(): return blocks.reshape(NBZ, NBY, NBX, VZ, VY, VX).transpose(0, 3, 1, 4, 2,...  6.63 us
  transfers between devices with their start and end apart: 14, of which 6 were waited for; matrix products, arithmetic and copies ran while one was open for 28% of the time, Pallas kernels for 0%

commit v1 on v0

v1 whole, which is shorter than its diff:
```python
import jax
import jax.numpy as jnp
from jax import lax
from jax.experimental import pallas as pl
from jax.experimental.pallas import tpu as pltpu
from jax.sharding import PartitionSpec as P

VZ = 8
VY = 8
VX = 16
NBZ = 2
NBY = 8
NBX = 8
SOURCES = 2
RAD = 4
BV = VY * VX
BLOCKS = NBZ * NBY * NBX
SLOTS = BLOCKS * SOURCES
NZ = NBZ * VZ
NY = NBY * VY
NX = NBX * VX
GROUPS = NBZ * NBY
PER = NBX * SOURCES
ROWS = PER * VZ
BRICKS = ("gy", "gx")
F32 = jnp.float32
BF16 = jnp.bfloat16

VMEM = pl.BlockSpec(memory_space=pltpu.VMEM)
SMEM = pl.BlockSpec(memory_space=pltpu.SMEM)


def iota(shape, dim):
    return lax.broadcasted_iota(jnp.int32, shape, dim)


def pieces(value, count):
    parts = []
    for _ in range(count - 1):
        part = value.astype(BF16)
        parts.append(part)
        value = value - part.astype(F32)
    parts.append(value.astype(BF16))
    return parts


def swap_chunks(rows):
    chunk = iota((VZ, BV), 1) // VX
    for k in (1, 2, 4):
        low = (chunk & k) == 0
        out = list(rows)
        for b in range(8):
            if b & k == 0:
                first, second = rows[b], rows[b + k]
                out[b] = jnp.where(low, first, pltpu.roll(second, k * VX, 1))
                out[b + k] = jnp.where(low, pltpu.roll(first, BV - k * VX, 1), second)
        rows = out
    return rows


def prepare_kernel(half_ref, moving_ref, owner_ref, ident_ref, blocks_ref, request_ref, flat_ref, wide):
    holders, _, width = request_ref.shape
    capacity = width // 2
    half = half_ref[0]
    owner = owner_ref[...]
    ident = ident_ref[...].astype(F32)
    groups = 2 * holders
    named = jnp.where(owner == iota((groups, SLOTS), 0), 1.0, 0.0)
    earlier = jnp.where(iota((SLOTS, SLOTS), 0) < iota((SLOTS, SLOTS), 1), 1.0, 0.0).astype(BF16)
    before = jnp.dot(named.astype(BF16), earlier, preferred_element_type=F32)
    rank = jnp.sum(named * before, axis=0, keepdims=True).astype(jnp.int32)
    upper = jnp.where(owner >= holders, 1, 0)
    holder = owner - upper * holders
    place = jnp.where(upper == half, 0, capacity) + rank
    flat_ref[...] = holder * width + place
    wanted = jnp.where(holder == iota((holders, SLOTS), 0), ident, 0.0).astype(BF16)
    at = jnp.where(place == iota((width, SLOTS), 0), 1.0, 0.0).astype(BF16)
    request = lax.dot_general(wanted, at, (((1,), (1,)), ((), ())), preferred_element_type=F32).astype(jnp.int32)
    for h in range(holders):
        request_ref[h] = request[h : h + 1, :]
    for z in range(NZ):
        wide[z * NY : (z + 1) * NY, :] = moving_ref[z].astype(F32)

    def group(g, _):
        start = (g // NBY) * (VZ * NY) + (g % NBY) * VY
        rows = [wide[pl.ds(start + y, VZ, stride=NY), :] for y in range(VY)]
        for x, block in enumerate(swap_chunks(rows)):
            blocks_ref[g * NBX + x] = block.astype(BF16)
        return 0

    lax.fori_loop(0, GROUPS, group, 0)


def prepare(half, moving, owner, ident, groups, capacity):
    holders = groups // 2
    return pl.pallas_call(
        prepare_kernel,
        out_shape=(
            jax.ShapeDtypeStruct((BLOCKS, VZ, BV), BF16),
            jax.ShapeDtypeStruct((holders, 1, 2 * capacity), jnp.int32),
            jax.ShapeDtypeStruct((1, SLOTS), jnp.int32),
        ),
        in_specs=[SMEM, VMEM, VMEM, VMEM],
        out_specs=(VMEM, VMEM, VMEM),
        scratch_shapes=[pltpu.VMEM((NZ * NY, NX), F32)],
        name="prepare",
    )(half, moving, owner, ident)


def pick_kernel(capacity, request_ref, near_ref, far_ref, out_ref):
    width = 2 * capacity

    def holder(h, _):
        for k in range(width):
            source = near_ref if k < capacity else far_ref
            out_ref[h * width + k] = source[request_ref[h * width + k]]
        return 0

    lax.fori_loop(0, out_ref.shape[0] // width, holder, 0)


def pick(request, near, far, capacity):
    return pl.pallas_call(
        lambda *refs: pick_kernel(capacity, *refs),
        out_shape=jax.ShapeDtypeStruct((request.shape[0], VZ, BV), BF16),
        in_specs=[SMEM, VMEM, VMEM],
        out_specs=VMEM,
        name="pick",
    )(request, near, far)


def spread_kernel(mix_ref, out_ref):
    pick_lane = jnp.where(iota((VZ, ROWS), 1) % VZ == iota((VZ, ROWS), 0), 1.0, 0.0).astype(BF16)
    same = iota((ROWS, ROWS), 0) // VZ == iota((ROWS, ROWS), 1) // VZ

    def group(g, _):
        weights = mix_ref[pl.ds(pl.multiple_of(g * ROWS, ROWS), ROWS), :]
        for k, part in enumerate(pieces(weights, 3)):
            tiled = jnp.dot(part, pick_lane, preferred_element_type=F32)
            out_ref[g, k * ROWS : (k + 1) * ROWS, :] = jnp.where(same, tiled, 0.0).astype(BF16)
        return 0

    lax.fori_loop(0, GROUPS, group, 0)


def spread(mix_z):
    return pl.pallas_call(
        spread_kernel,
        out_shape=jax.ShapeDtypeStruct((GROUPS, 3 * ROWS, ROWS), BF16),
        in_specs=[VMEM],
        out_specs=VMEM,
        name="spread",
    )(mix_z)


STEP = 2


def mix_kernel(flat_ref, received_ref, spread_ref, mix_ref, warped_ref, source):
    step = pl.program_id(0)
    for q in range(STEP):
        g = step * STEP + q
        for i in range(PER):
            source[i * VZ : (i + 1) * VZ, :] = received_ref[flat_ref[g * PER + i]].astype(F32)
        parts = jnp.dot(spread_ref[q], source[...].astype(BF16), preferred_element_type=F32)
        mixed = parts[:ROWS] + parts[ROWS : 2 * ROWS] + parts[2 * ROWS :]
        high = mixed.astype(BF16).astype(F32)
        low = mixed - high
        rows = []
        for j in range(NBX):
            a = slice(2 * j * VZ, (2 * j + 1) * VZ)
            b = slice((2 * j + 1) * VZ, (2 * j + 2) * VZ)
            left = jnp.concatenate(
                [jnp.concatenate([high[a], high[b]], 1), jnp.concatenate([low[a], low[b]], 1)], 0
            ).astype(BF16)
            right = mix_ref[q * PER + 2 * j : q * PER + 2 * j + 2].reshape(2 * BV, BV)
            both = jnp.dot(left, right, preferred_element_type=F32)
            rows.append(both[:VZ] + both[VZ:])
        start = (g // NBY) * (VZ * NY) + (g % NBY) * VY
        for y, row in enumerate(swap_chunks(rows)):
            warped_ref[pl.ds(start + y, VZ, stride=NY), :] = row


def mix(flat, received, spread_z, mix_yx):
    return pl.pallas_call(
        mix_kernel,
        grid_spec=pltpu.PrefetchScalarGridSpec(
            num_scalar_prefetch=1,
            grid=(GROUPS // STEP,),
            in_specs=[
                pl.BlockSpec(received.shape, lambda i, f: (0, 0, 0)),
                pl.BlockSpec((STEP, 3 * ROWS, ROWS), lambda i, f: (i, 0, 0)),
                pl.BlockSpec((STEP * PER, BV, BV), lambda i, f: (i, 0, 0)),
            ],
            out_specs=pl.BlockSpec((NZ * NY, NX), lambda i, f: (0, 0)),
            scratch_shapes=[pltpu.VMEM((ROWS, BV), F32)],
        ),
        out_shape=jax.ShapeDtypeStruct((NZ * NY, NX), F32),
        name="mix",
    )(flat, received, spread_z, mix_yx)


def fetch_and_mix(moving, owners, block_ids, counts, mix_yx, mix_z):
    rows_gy = lax.axis_size("gy")
    groups = rows_gy * lax.axis_size("gx")
    holders = groups // 2
    capacity = max(2, 2 * SLOTS // groups)
    halves = [list(range(holders)), list(range(holders, groups))]
    half = (lax.axis_index("gy") >= rows_gy // 2).astype(jnp.int32).reshape(1)
    near, request, flat = prepare(half, moving, owners.reshape(1, SLOTS), block_ids.reshape(1, SLOTS), groups, capacity)
    far = lax.ppermute(near, "gy", [(i, (i + rows_gy // 2) % rows_gy) for i in range(rows_gy)])
    request = lax.all_to_all(request, BRICKS, split_axis=0, concat_axis=0, tiled=True, axis_index_groups=halves)
    picked = pick(request.reshape(-1), near, far, capacity).reshape(holders, 2 * capacity, VZ, BV)
    received = lax.all_to_all(picked, BRICKS, split_axis=0, concat_axis=0, tiled=True, axis_index_groups=halves)
    slot_pos = jnp.arange(SLOTS, dtype=jnp.int32)
    keep = slot_pos % SOURCES < jnp.repeat(counts.reshape(-1), SOURCES)
    weights_z = jnp.where(keep[:, None, None], mix_z.reshape(SLOTS, VZ, VZ), 0.0).reshape(SLOTS * VZ, VZ)
    warped = mix(
        flat.reshape(-1),
        received.reshape(groups * capacity, VZ, BV),
        spread(weights_z),
        mix_yx.reshape(SLOTS, BV, BV),
    )
    return warped.reshape(NZ, NY, NX)


def padded_2(block, sides, width):
    for axis, dim in sides:
        count = lax.axis_size(axis)
        forward = [(i, i + 1) for i in range(count - 1)]
        backward = [(target, source) for source, target in forward]
        low = lax.ppermute(
            lax.slice_in_dim(block, block.shape[dim] - width, None, axis=dim), axis, forward
        )
        high = lax.ppermute(lax.slice_in_dim(block, 0, width, axis=dim), axis, backward)
        block = jnp.concatenate([low, block, high], axis=dim)
    return block


def box_along(padded, axis):
    length = padded.shape[axis] - 2 * RAD
    total = lax.slice_in_dim(padded, 0, length, axis=axis)
    for shift in range(1, 2 * RAD + 1):
        total = total + lax.slice_in_dim(padded, shift, shift + length, axis=axis)
    return total


def per_device(fixed, moving, owners, block_ids, counts, mix_yx, mix_z):
    warped = fetch_and_mix(moving, owners, block_ids, counts, mix_yx, mix_z)
    image = fixed.astype(jnp.float32)
    fields = jnp.stack([image, warped, image * image, warped * warped, image * warped])
    padded = padded_2(fields, (("gz", 1),), RAD)
    sums = box_along(padded, 1)
    padded = padded_2(sums, (("gy", 2),), RAD)
    sums = box_along(padded, 2)
    padded = padded_2(sums, (("gx", 3),), RAD)
    sums = box_along(padded, 3)
    wpad = padded_2(warped, (("gz", 0), ("gy", 1), ("gx", 2)), 1)
    count = float((2 * RAD + 1) ** 3)
    mean_f = sums[0] / count
    mean_w = sums[1] / count
    cov = sums[4] / count - mean_f * mean_w
    var_f = sums[2] / count - mean_f * mean_f
    var_w = sums[3] / count - mean_w * mean_w
    deriv = (
        2.0
        * cov
        / ((var_f + 1e-05) * (var_w + 1e-05))
        * (image - mean_f - cov / (var_w + 1e-05) * (warped - mean_w))
    )
    slope_z = (wpad[2:, 1:-1, 1:-1] - wpad[:-2, 1:-1, 1:-1]) * 0.5
    slope_y = (wpad[1:-1, 2:, 1:-1] - wpad[1:-1, :-2, 1:-1]) * 0.5
    slope_x = (wpad[1:-1, 1:-1, 2:] - wpad[1:-1, 1:-1, :-2]) * 0.5
    force = jnp.stack([deriv * slope_z, deriv * slope_y, deriv * slope_x])
    return (warped, force)


def solution(mesh):
    return jax.shard_map(
        per_device,
        mesh=mesh,
        in_specs=(
            P("gz", "gy", "gx"),
            P("gz", "gy", "gx"),
            P("gz", "gy", "gx", None, None),
            P("gz", "gy", "gx", None),
            P("gz", "gy", "gx", None),
            P("gz", "gy", "gx", None, None, None),
            P("gz", "gy", "gx", None, None, None),
        ),
        out_specs=(P("gz", "gy", "gx"), P(None, "gz", "gy", "gx")),
        check_vma=False,
    )
```

time: 167 us -> 144 us (0.86)
  Pallas kernels: 0 us -> 24.6 us
  local copies, waits for them, and re-layouts: 51 us -> 28.7 us
  waiting for transfers between devices: 32.4 us -> 15.4 us
  blocking collectives: 0 us -> 7.35 us
  matrix products: 6.66 us -> 0 us
  starting transfers between devices: 44.2 us -> 38.7 us
  other arithmetic: 29.3 us -> 27.4 us
    pallas_call x0 -> x4, Pallas kernels: none -> 24.6 us  [the longest x1 11.3 us: mix(): pl.pallas_call(mix_kernel, grid_spec=pltpu.PrefetchScalarGridSpec(num_sca...]
    all_to_all x2 -> x1, waiting for transfers between devices: 20.7 us -> 5.72 us  [fetch_and_mix(): lax.all_to_all(picked, BRICKS, split_axis=0, concat_axis=0, tiled=True, a...]
    reshape x6 -> x2, local copies, waits for them, and re-layouts: 14.1 us -> 0.81 us  [the longest x1 0.66 us: fetch_and_mix(): request.reshape(-1)]
    all_to_all x2 -> x1, starting transfers between devices: 14.1 us -> 5.37 us  [fetch_and_mix(): lax.all_to_all(picked, BRICKS, split_axis=0, concat_axis=0, tiled=True, a...]
    all_to_all x0 -> x1, blocking collectives: none -> 7.35 us  [fetch_and_mix(): lax.all_to_all(request, BRICKS, split_axis=0, concat_axis=0, tiled=True,...]
    dot_general x2 -> x0, matrix products: 6.66 us -> none  [the longest x1 4.79 us: per_device(): jnp.einsum('szc,scd->szd', source, weights_yx, preferred_element_type=jnp...]
    transpose x1 -> x0, local copies, waits for them, and re-layouts: 6.63 us -> none  [from_blocks(): return blocks.reshape(NBZ, NBY, NBX, VZ, VY, VX).transpose(0, 3, 1, 4, 2,...]
    gather x3 -> x0, local copies, waits for them, and re-layouts: 5.72 us -> none  [the longest x1 2.05 us: per_device(): source = jnp.take(received.reshape(groups * capacity, VZ, BV), flat, axis=0)]
  transfers between devices with their start and end apart: 14 -> 14, of which waited for: 6 -> 4; matrix products, arithmetic and copies ran while one was open for 28% -> 16% of each run, Pallas kernels for 0% -> 3%
where the time goes in v1:
time: 144 us; the launch traced here: 143 us
  starting transfers between devices  38.7 us (27%)
  local copies, waits for them, and re-layouts  28.7 us (20%)
  other arithmetic  27.4 us (19%)
  Pallas kernels  24.6 us (17%)
  waiting for transfers between devices  15.4 us (11%)
  blocking collectives  7.35 us (5%)
    add x3, other arithmetic, box_along(): total = total + lax.slice_in_dim(padded, shift, shift + length, axis=axis)  20.8 us
    ppermute x6, starting transfers between devices, padded_2(): lax.ppermute(lax.slice_in_dim(block, block.shape[dim] - width, None, axis...  17.1 us
    ppermute x6, starting transfers between devices, padded_2(): lax.ppermute(lax.slice_in_dim(block, 0, width, axis=dim), axis, backward)  13.6 us
    pallas_call x1, Pallas kernels, mix(): pl.pallas_call(mix_kernel, grid_spec=pltpu.PrefetchScalarGridSpec(num_sca...  11.3 us
    all_to_all x1, blocking collectives, fetch_and_mix(): lax.all_to_all(request, BRICKS, split_axis=0, concat_axis=0, tiled=True,...  7.35 us
    slice x5, local copies, waits for them, and re-layouts, padded_2(): lax.slice_in_dim(block, block.shape[dim] - width, None, axis=dim)  6.64 us
    slice x4, local copies, waits for them, and re-layouts, padded_2(): lax.slice_in_dim(block, 0, width, axis=dim)  5.85 us
    pallas_call x1, Pallas kernels, prepare(): pl.pallas_call(prepare_kernel, out_shape=(jax.ShapeDtypeStruct((BLOCKS, V...  5.84 us
  transfers between devices with their start and end apart: 14, of which 4 were waited for; matrix products, arithmetic and copies ran while one was open for 16% of the time, Pallas kernels for 3%

profile of v1, /device:TPU:14, one launch (start us, length us, event | category | flops | bytes accessed | tf_op | source)
XLA Modules:
  0.0 143.1 jit_solution(10462616184110445501)
XLA Ops:
  0.7 5.8 %prepare.1 = (bf16[128,8,128]{2,1,0:T(8,128)(2,1)}, s32[8,1,64]{2,1,0:T(1,128)}, s32[1,256]{1,0:T(1,128)}) custom-call(s32[1]{0:T(128)} %bitcast.half_ref, bf16[16,64,128]{2,1,0:T(8,128)(2,1)} %moving_ref.1, s32[1,256]{1,0:T(1,128)} %bitcast.84, s32[1,256]{1,0:T(1,128)} %bitcast.85), custom_call_target="tpu_custom_call" | custom-call | tf_op jit(solution)/shard_map/prepare/pallas_call | solution.py:96
  6.5 2.6 %collective-permute-start = (bf16[128,8,128]{2,1,0:T(8,128)(2,1)}, bf16[128,8,128]{2,1,0:T(8,128)(2,1)S(1)}, u32[]{:S(2)}, u32[]{:S(2)}) collective-permute-start(bf16[128,8,128]{2,1,0:T(8,128)(2,1)} %get-tuple-element.7.refs_1_), channel_id=1, source_target_pairs={{0,8},{2,10},{4,12},{6,14},{8,0},{10,2},{12,4},{14,6},{1,9},{3,11}... | collective-permute-start | bytes 786440 | tf_op jit(solution)/shard_map/ppermute | solution.py:211
  9.1 7.3 %all_to_all.10 = s32[8,1,64]{2,1,0:T(1,128)S(1)} all-to-all(s32[8,1,64]{2,1,0:T(1,128)} %get-tuple-element.6), channel_id=1, replica_groups={{0,1,2,3,4,5,6,7},{8,9,10,11,12,13,14,15},{16,17,18,19,20,21,22,23},{24..., dimensions={0} | all-to-all | bytes 4096 | tf_op jit(solution)/shard_map/all_to_all | solution.py:212
  18.3 2.2 %collective-permute-done.refs_2_ = bf16[128,8,128]{2,1,0:T(8,128)(2,1)S(1)} collective-permute-done((bf16[128,8,128]{2,1,0:T(8,128)(2,1)}, bf16[128,8,128]{2,1,0:T(8,128)(2,1)S(1)}, u32[]{:S(2)}, u32[]{:S(2)}) %collective-permute-start) | collective-permute-done | bytes 262176 | tf_op jit(solution)/shard_map/ppermute | solution.py:211
  21.2 2.6 %pick.1 = bf16[512,8,128]{2,1,0:T(8,128)(2,1)} custom-call(s32[512]{0:T(512)} %reshape.86.refs_0_, bf16[128,8,128]{2,1,0:T(8,128)(2,1)} %get-tuple-element.7.refs_1_, bf16[128,8,128]{2,1,0:T(8,128)(2,1)} %copy-done.4), custom_call_target="tpu_custom_call" | custom-call | tf_op jit(solution)/shard_map/pick/pallas_call | solution.py:123
  23.7 5.4 %all-to-all-start.1 = ((bf16[8,64,8,128]{3,2,1,0:T(8,128)(2,1)}), bf16[8,64,8,128]{3,2,1,0:T(8,128)(2,1)}, u32[]{:S(2)}, u32[]{:S(2)}) async-start(bf16[8,64,8,128]{3,2,1,0:T(8,128)(2,1)} %bitcast.83), calls=%async_computation.1 | async-start | bytes 2097152 | tf_op jit(solution)/shard_map/all_to_all | solution.py:214
  30.0 1.3 bitcast_select_fusion.mix_ref
  31.4 4.8 %spread.1.spread_ref = bf16[16,384,128]{2,1,0:T(8,128)(2,1)} custom-call(f32[2048,8]{1,0:T(8,128)} %bitcast_select_fusion.mix_ref), custom_call_target="tpu_custom_call" | custom-call | tf_op jit(solution)/shard_map/spread/pallas_call | solution.py:147
  36.2 5.7 %all-to-all-done.1 = bf16[8,64,8,128]{3,2,1,0:T(8,128)(2,1)} async-done(((bf16[8,64,8,128]{3,2,1,0:T(8,128)(2,1)}), bf16[8,64,8,128]{3,2,1,0:T(8,128)(2,1)}, u32[]{:S(2)}, u32[]{:S(2)}) %all-to-all-start.1) | async-done | bytes 1048608 | tf_op jit(solution)/shard_map/all_to_all | solution.py:214
  42.0 11.3 %mix.1 = f32[1024,128]{1,0:T(8,128)} custom-call(s32[256]{0:T(256)} %bitcast.86, bf16[512,8,128]{2,1,0:T(8,128)(2,1)} %bitcast.5.received_ref, bf16[16,384,128]{2,1,0:T(8,128)(2,1)} %spread.1.spread_ref, bf16[256,128,128]{2,1,0:T(8,128)(2,1)} %bitcast.82), custom_call_target="tpu_custom_call" | custom-call | tf_op jit(solution)/shard_map/mix/pallas_call | solution.py:185
  55.8 2.0 %collective-permute-start.1 = (f32[5,4,64,128]{3,2,1,0:T(8,128)S(1)}, f32[5,4,64,128]{3,2,1,0:T(8,128)S(1)}, u32[]{:S(2)}, u32[]{:S(2)}) collective-permute-start(f32[5,4,64,128]{3,2,1,0:T(8,128)S(1)} %get-tuple-element.16), channel_id=1, source_target_pairs={{0,16},{1,17},{2,18},{3,19},{4,20},{5,21},{6,22},{7,23},{8,24},{9,... | collective-permute-start | bytes 1966088 | tf_op jit(solution)/shard_map/ppermute | solution.py:232
  60.4 3.1 %collective-permute-start.8 = (f32[1,64,128]{2,1,0:T(8,128)S(1)}, f32[1,64,128]{2,1,0:T(8,128)S(1)}, u32[]{:S(2)}, u32[]{:S(2)}) collective-permute-start(f32[1,64,128]{2,1,0:T(8,128)S(1)} %get-tuple-element.23), channel_id=1, source_target_pairs={{0,16},{1,17},{2,18},{3,19},{4,20},{5,21},{6,22},{7,23},{8,24},{9,... | collective-permute-start | bytes 98312 | tf_op jit(solution)/shard_map/ppermute | solution.py:232
  63.4 3.0 %fusion.16 = f32[5,16,64,128]{3,2,1,0:T(8,128)S(1)} fusion(f32[5,16,64,128]{3,2,1,0:T(8,128)S(1)} %fusion.46, f32[5,4,64,128]{3,2,1,0:T(8,128)S(1)} %collective-permute-done.2, f32[5,4,64,128]{3,2,1,0:T(8,128)S(1)} %collective-permute-done.1), kind=kLoop, calls=%fused_computation.52 | loop fusion | flops 10485760 | bytes 6553600 | tf_op jit(solution)/shard_map/add | solution.py:244
  66.5 4.5 %collective-permute-start.3 = (f32[5,16,4,128]{3,1,2,0:T(8,128)S(1)}, f32[5,16,4,128]{3,1,2,0:T(8,128)S(1)}, u32[]{:S(2)}, u32[]{:S(2)}) collective-permute-start(f32[5,16,4,128]{3,1,2,0:T(8,128)S(1)} %copy.31), channel_id=1, source_target_pairs={{0,2},{2,4},{4,6},{6,8},{8,10},{10,12},{12,14},{1,3},{3,5},{5,7},{... | collective-permute-start | bytes 491528 | tf_op jit(solution)/shard_map/ppermute | solution.py:232
  71.0 1.9 %collective-permute-start.4 = (f32[5,16,4,128]{3,1,2,0:T(8,128)S(1)}, f32[5,16,4,128]{3,1,2,0:T(8,128)S(1)}, u32[]{:S(2)}, u32[]{:S(2)}) collective-permute-start(f32[5,16,4,128]{3,1,2,0:T(8,128)S(1)} %copy.33), channel_id=1, source_target_pairs={{2,0},{4,2},{6,4},{8,6},{10,8},{12,10},{14,12},{3,1},{5,3},{7,5},{... | collective-permute-start | bytes 491528 | tf_op jit(solution)/shard_map/ppermute | solution.py:235
  73.0 4.8 %collective-permute-start.10 = (f32[18,1,128]{2,1,0:T(1,128)S(1)}, f32[18,1,128]{2,1,0:T(1,128)S(1)}, u32[]{:S(2)}, u32[]{:S(2)}) collective-permute-start(f32[18,1,128]{2,1,0:T(1,128)S(1)} %get-tuple-element.20), channel_id=1, source_target_pairs={{0,2},{2,4},{4,6},{6,8},{8,10},{10,12},{12,14},{1,3},{3,5},{5,7},{... | collective-permute-start | bytes 27656 | tf_op jit(solution)/shard_map/ppermute | solution.py:232
  77.8 1.9 %collective-permute-start.9 = (f32[18,1,128]{2,1,0:T(1,128)S(1)}, f32[18,1,128]{2,1,0:T(1,128)S(1)}, u32[]{:S(2)}, u32[]{:S(2)}) collective-permute-start(f32[18,1,128]{2,1,0:T(1,128)S(1)} %get-tuple-element.21), channel_id=1, source_target_pairs={{2,0},{4,2},{6,4},{8,6},{10,8},{12,10},{14,12},{3,1},{5,3},{7,5},{... | collective-permute-start | bytes 27656 | tf_op jit(solution)/shard_map/ppermute | solution.py:235
  79.8 4.5 %collective-permute-done.9 = f32[18,1,128]{2,1,0:T(1,128)S(1)} collective-permute-done((f32[18,1,128]{2,1,0:T(1,128)S(1)}, f32[18,1,128]{2,1,0:T(1,128)S(1)}, u32[]{:S(2)}, u32[]{:S(2)}) %collective-permute-start.9) | collective-permute-done | bytes 9248 | tf_op jit(solution)/shard_map/ppermute | solution.py:235
  85.3 2.8 %fusion.2 = f32[5,16,64,128]{3,2,1,0:T(8,128)S(1)} fusion(f32[5,16,64,128]{3,2,1,0:T(8,128)S(1)} %fusion.16, f32[5,16,4,128]{3,2,1,0:T(4,128)S(1)} %copy.34, f32[5,16,4,128]{3,2,1,0:T(4,128)S(1)} %copy.32), kind=kLoop, calls=%fused_computation.38 | loop fusion | flops 10485760 | bytes 5570560 | tf_op jit(solution)/shard_map/add | solution.py:244
  88.1 3.2 %fusion.75 = (f32[5,16,64,4]{3,2,1,0:T(8,128)}, f32[5,16,64,4]{3,2,1,0:T(8,128)}) fusion(f32[5,16,64,128]{3,2,1,0:T(8,128)S(1)} %fusion.2), kind=kLoop, calls=%fused_computation.154 | loop fusion | bytes 327680 | tf_op jit(solution)/shard_map/slice | solution.py:233
  91.4 3.2 %copy.35 = f32[5,16,64,4]{2,1,3,0:T(8,128)} copy(f32[5,16,64,4]{3,2,1,0:T(8,128)} %get-tuple-element.12) | data formatting | bytes 163840 | tf_op jit(solution)/shard_map/slice | solution.py:233
  95.9 3.3 %copy.37 = f32[5,16,64,4]{2,1,3,0:T(8,128)} copy(f32[5,16,64,4]{3,2,1,0:T(8,128)} %get-tuple-element.13) | data formatting | bytes 163840 | tf_op jit(solution)/shard_map/slice | solution.py:235
  99.2 5.9 %collective-permute-start.6 = (f32[5,16,64,4]{2,1,3,0:T(8,128)}, f32[5,16,64,4]{2,1,3,0:T(8,128)}, u32[]{:S(2)}, u32[]{:S(2)}) collective-permute-start(f32[5,16,64,4]{2,1,3,0:T(8,128)} %copy.37), channel_id=1, source_target_pairs={{1,0},{3,2},{5,4},{7,6},{9,8},{11,10},{13,12},{15,14},{17,16},{19,... | collective-permute-start | bytes 245768 | tf_op jit(solution)/shard_map/ppermute | solution.py:235
  105.0 2.6 %fusion.78 = (f32[18,66,1]{2,1,0:T(8,128)}, f32[18,66,1]{2,1,0:T(8,128)}) fusion(f32[18,66,128]{2,1,0:T(8,128)} %pad_maximum_fusion.7), kind=kLoop, calls=%fused_computation.157 | loop fusion | bytes 19008 | tf_op jit(solution)/shard_map/slice | solution.py:235
  107.6 1.3 copy.43
  109.0 1.3 collective-permute-start.11
  110.3 1.3 copy.44
  111.6 1.5 %collective-permute-start.12 = (f32[18,66,1]{1,2,0:T(1,128)S(1)}, f32[18,66,1]{1,2,0:T(1,128)S(1)}, u32[]{:S(2)}, u32[]{:S(2)}) collective-permute-start(f32[18,66,1]{1,2,0:T(1,128)S(1)} %copy.44), channel_id=1, source_target_pairs={{0,1},{2,3},{4,5},{6,7},{8,9},{10,11},{12,13},{14,15},{16,17},{18,... | collective-permute-start | bytes 14264 | tf_op jit(solution)/shard_map/ppermute | solution.py:232
  114.3 2.9 %collective-permute-done.12 = f32[18,66,1]{1,2,0:T(1,128)S(1)} collective-permute-done((f32[18,66,1]{1,2,0:T(1,128)S(1)}, f32[18,66,1]{1,2,0:T(1,128)S(1)}, u32[]{:S(2)}, u32[]{:S(2)}) %collective-permute-start.12) | collective-permute-done | bytes 4784 | tf_op jit(solution)/shard_map/ppermute | solution.py:232
  118.4 3.3 %copy.36 = f32[5,16,64,4]{3,2,1,0:T(8,128)} copy(f32[5,16,64,4]{2,1,3,0:T(8,128)} %collective-permute-done.5) | data formatting | bytes 163840 | tf_op jit(solution)/shard_map/ppermute | solution.py:232
  121.6 3.3 %copy.38 = f32[5,16,64,4]{3,2,1,0:T(8,128)} copy(f32[5,16,64,4]{2,1,3,0:T(8,128)} %collective-permute-done.6) | data formatting | bytes 163840 | tf_op jit(solution)/shard_map/ppermute | solution.py:235
  124.9 15.1 %fusion.30 = f32[5,16,64,128]{3,2,1,0:T(8,128)S(1)} fusion(f32[5,16,64,128]{3,2,1,0:T(8,128)S(1)} %fusion.2, f32[5,16,64,4]{3,2,1,0:T(8,128)} %copy.38, f32[5,16,64,4]{3,2,1,0:T(8,128)} %copy.36), kind=kLoop, calls=%fused_computation.66 | loop fusion | flops 10485760 | bytes 5406720 | tf_op jit(solution)/shard_map/add | solution.py:244
  (56 shorter events, 16.3 us)
Async XLA Ops:
  0.6 28.5 %copy-start.5 = (f32[1,1,1,256,8,8]{3,5,4,2,1,0:T(8,128)S(1)}, f32[1,1,1,256,8,8]{3,5,4,2,1,0:T(8,128)}, u32[]{:S(2)}) copy-start(f32[1,1,1,256,8,8]{3,5,4,2,1,0:T(8,128)} %param.13) | copy-start | bytes 196612
  0.6 28.9 %copy-start.6 = (s32[1,1,1,128]{3,2,1,0:T(1,128)S(1)}, s32[1,1,1,128]{3,2,1,0:T(1,128)}, u32[]{:S(2)}) copy-start(s32[1,1,1,128]{3,2,1,0:T(1,128)} %param.11) | copy-start | bytes 1540
  6.5 14.0 %collective-permute-start = (bf16[128,8,128]{2,1,0:T(8,128)(2,1)}, bf16[128,8,128]{2,1,0:T(8,128)(2,1)S(1)}, u32[]{:S(2)}, u32[]{:S(2)}) collective-permute-start(bf16[128,8,128]{2,1,0:T(8,128)(2,1)} %get-tuple-element.7.refs_1_), channel_id=1, source_target_pairs={{0,8},{2,10},{4,12},{6,14},{8,0},{10,2},{12,4},{14,6},{1,9},{3,11}... | collective-permute-start | bytes 786440 | tf_op jit(solution)/shard_map/ppermute | solution.py:211
  20.5 0.7 copy-start.4
  23.7 18.2 %all-to-all-start.1 = ((bf16[8,64,8,128]{3,2,1,0:T(8,128)(2,1)}), bf16[8,64,8,128]{3,2,1,0:T(8,128)(2,1)}, u32[]{:S(2)}, u32[]{:S(2)}) async-start(bf16[8,64,8,128]{3,2,1,0:T(8,128)(2,1)} %bitcast.83), calls=%async_computation.1 | async-start | bytes 2097152 | tf_op jit(solution)/shard_map/all_to_all | solution.py:214
  29.5 6.7 %copy-start.1 = (bf16[16,64,128]{2,1,0:T(8,128)(2,1)S(1)}, bf16[16,64,128]{2,1,0:T(8,128)(2,1)}, u32[]{:S(2)}) copy-start(bf16[16,64,128]{2,1,0:T(8,128)(2,1)} %param.7) | copy-start | bytes 786436
  53.3 2.3 %copy-start = (f32[1024,128]{1,0:T(8,128)S(1)}, f32[1024,128]{1,0:T(8,128)}, u32[]{:S(2)}) copy-start(f32[1024,128]{1,0:T(8,128)} %mix.1) | copy-start | bytes 1572868
  55.8 7.7 %collective-permute-start.1 = (f32[5,4,64,128]{3,2,1,0:T(8,128)S(1)}, f32[5,4,64,128]{3,2,1,0:T(8,128)S(1)}, u32[]{:S(2)}, u32[]{:S(2)}) collective-permute-start(f32[5,4,64,128]{3,2,1,0:T(8,128)S(1)} %get-tuple-element.16), channel_id=1, source_target_pairs={{0,16},{1,17},{2,18},{3,19},{4,20},{5,21},{6,22},{7,23},{8,24},{9,... | collective-permute-start | bytes 1966088 | tf_op jit(solution)/shard_map/ppermute | solution.py:232
  57.7 5.7 %collective-permute-start.2 = (f32[5,4,64,128]{3,2,1,0:T(8,128)S(1)}, f32[5,4,64,128]{3,2,1,0:T(8,128)S(1)}, u32[]{:S(2)}, u32[]{:S(2)}) collective-permute-start(f32[5,4,64,128]{3,2,1,0:T(8,128)S(1)} %get-tuple-element.17), channel_id=1, source_target_pairs={{16,0},{17,1},{18,2},{19,3},{20,4},{21,5},{22,6},{23,7},{24,8},{25... | collective-permute-start | bytes 1966088 | tf_op jit(solution)/shard_map/ppermute | solution.py:235
  59.1 13.9 %collective-permute-start.7 = (f32[1,64,128]{2,1,0:T(8,128)S(1)}, f32[1,64,128]{2,1,0:T(8,128)S(1)}, u32[]{:S(2)}, u32[]{:S(2)}) collective-permute-start(f32[1,64,128]{2,1,0:T(8,128)S(1)} %get-tuple-element.22), channel_id=1, source_target_pairs={{16,0},{17,1},{18,2},{19,3},{20,4},{21,5},{22,6},{23,7},{24,8},{25... | collective-permute-start | bytes 98312 | tf_op jit(solution)/shard_map/ppermute | solution.py:235
  60.4 12.6 %collective-permute-start.8 = (f32[1,64,128]{2,1,0:T(8,128)S(1)}, f32[1,64,128]{2,1,0:T(8,128)S(1)}, u32[]{:S(2)}, u32[]{:S(2)}) collective-permute-start(f32[1,64,128]{2,1,0:T(8,128)S(1)} %get-tuple-element.23), channel_id=1, source_target_pairs={{0,16},{1,17},{2,18},{3,19},{4,20},{5,21},{6,22},{7,23},{8,24},{9,... | collective-permute-start | bytes 98312 | tf_op jit(solution)/shard_map/ppermute | solution.py:232
  66.5 18.7 %collective-permute-start.3 = (f32[5,16,4,128]{3,1,2,0:T(8,128)S(1)}, f32[5,16,4,128]{3,1,2,0:T(8,128)S(1)}, u32[]{:S(2)}, u32[]{:S(2)}) collective-permute-start(f32[5,16,4,128]{3,1,2,0:T(8,128)S(1)} %copy.31), channel_id=1, source_target_pairs={{0,2},{2,4},{4,6},{6,8},{8,10},{10,12},{12,14},{1,3},{3,5},{5,7},{... | collective-permute-start | bytes 491528 | tf_op jit(solution)/shard_map/ppermute | solution.py:232
  71.0 14.2 %collective-permute-start.4 = (f32[5,16,4,128]{3,1,2,0:T(8,128)S(1)}, f32[5,16,4,128]{3,1,2,0:T(8,128)S(1)}, u32[]{:S(2)}, u32[]{:S(2)}) collective-permute-start(f32[5,16,4,128]{3,1,2,0:T(8,128)S(1)} %copy.33), channel_id=1, source_target_pairs={{2,0},{4,2},{6,4},{8,6},{10,8},{12,10},{14,12},{3,1},{5,3},{7,5},{... | collective-permute-start | bytes 491528 | tf_op jit(solution)/shard_map/ppermute | solution.py:235
  73.0 6.8 %collective-permute-start.10 = (f32[18,1,128]{2,1,0:T(1,128)S(1)}, f32[18,1,128]{2,1,0:T(1,128)S(1)}, u32[]{:S(2)}, u32[]{:S(2)}) collective-permute-start(f32[18,1,128]{2,1,0:T(1,128)S(1)} %get-tuple-element.20), channel_id=1, source_target_pairs={{0,2},{2,4},{4,6},{6,8},{8,10},{10,12},{12,14},{1,3},{3,5},{5,7},{... | collective-permute-start | bytes 27656 | tf_op jit(solution)/shard_map/ppermute | solution.py:232
  77.8 6.5 %collective-permute-start.9 = (f32[18,1,128]{2,1,0:T(1,128)S(1)}, f32[18,1,128]{2,1,0:T(1,128)S(1)}, u32[]{:S(2)}, u32[]{:S(2)}) collective-permute-start(f32[18,1,128]{2,1,0:T(1,128)S(1)} %get-tuple-element.21), channel_id=1, source_target_pairs={{2,0},{4,2},{6,4},{8,6},{10,8},{12,10},{14,12},{3,1},{5,3},{7,5},{... | collective-permute-start | bytes 27656 | tf_op jit(solution)/shard_map/ppermute | solution.py:235
  94.6 23.7 %collective-permute-start.5 = (f32[5,16,64,4]{2,1,3,0:T(8,128)}, f32[5,16,64,4]{2,1,3,0:T(8,128)}, u32[]{:S(2)}, u32[]{:S(2)}) collective-permute-start(f32[5,16,64,4]{2,1,3,0:T(8,128)} %copy.35), channel_id=1, source_target_pairs={{0,1},{2,3},{4,5},{6,7},{8,9},{10,11},{12,13},{14,15},{16,17},{18,... | collective-permute-start | bytes 245768 | tf_op jit(solution)/shard_map/ppermute | solution.py:232
  99.2 22.5 %collective-permute-start.6 = (f32[5,16,64,4]{2,1,3,0:T(8,128)}, f32[5,16,64,4]{2,1,3,0:T(8,128)}, u32[]{:S(2)}, u32[]{:S(2)}) collective-permute-start(f32[5,16,64,4]{2,1,3,0:T(8,128)} %copy.37), channel_id=1, source_target_pairs={{1,0},{3,2},{5,4},{7,6},{9,8},{11,10},{13,12},{15,14},{17,16},{19,... | collective-permute-start | bytes 245768 | tf_op jit(solution)/shard_map/ppermute | solution.py:235
  109.0 4.2 %collective-permute-start.11 = (f32[18,66,1]{1,2,0:T(1,128)S(1)}, f32[18,66,1]{1,2,0:T(1,128)S(1)}, u32[]{:S(2)}, u32[]{:S(2)}) collective-permute-start(f32[18,66,1]{1,2,0:T(1,128)S(1)} %copy.43), channel_id=1, source_target_pairs={{1,0},{3,2},{5,4},{7,6},{9,8},{11,10},{13,12},{15,14},{17,16},{19,... | collective-permute-start | bytes 14264 | tf_op jit(solution)/shard_map/ppermute | solution.py:235
  111.6 5.6 %collective-permute-start.12 = (f32[18,66,1]{1,2,0:T(1,128)S(1)}, f32[18,66,1]{1,2,0:T(1,128)S(1)}, u32[]{:S(2)}, u32[]{:S(2)}) collective-permute-start(f32[18,66,1]{1,2,0:T(1,128)S(1)} %copy.44), channel_id=1, source_target_pairs={{0,1},{2,3},{4,5},{6,7},{8,9},{10,11},{12,13},{14,15},{16,17},{18,... | collective-permute-start | bytes 14264 | tf_op jit(solution)/shard_map/ppermute | solution.py:232
  140.0 1.1 copy-start.2
  140.0 1.3 copy-start.3

commit v2 on v1

--- a/solution.py
+++ b/solution.py
@@ -156,7 +156,7 @@
 STEP = 2
 
 
-def mix_kernel(flat_ref, received_ref, spread_ref, mix_ref, warped_ref, source):
+def mix_kernel(flat_ref, place_ref, received_ref, spread_ref, mix_ref, warped_ref, side_ref, source):
     step = pl.program_id(0)
     for q in range(STEP):
         g = step * STEP + q
@@ -180,27 +180,38 @@
         for y, row in enumerate(swap_chunks(rows)):
             warped_ref[pl.ds(start + y, VZ, stride=NY), :] = row
 
-
-def mix(flat, received, spread_z, mix_yx):
+    @pl.when(step == pl.num_programs(0) - 1)
+    def _():
+        first = jnp.where(place_ref[0] == 0, (NZ - RAD) * NY, 0)
+        side_ref[...] = warped_ref[pl.ds(pl.multiple_of(first, NY), RAD * NY), :]
+
+
+def mix(flat, place, received, spread_z, mix_yx):
     return pl.pallas_call(
         mix_kernel,
         grid_spec=pltpu.PrefetchScalarGridSpec(
-            num_scalar_prefetch=1,
+            num_scalar_prefetch=2,
             grid=(GROUPS // STEP,),
             in_specs=[
-                pl.BlockSpec(received.shape, lambda i, f: (0, 0, 0)),
-                pl.BlockSpec((STEP, 3 * ROWS, ROWS), lambda i, f: (i, 0, 0)),
-                pl.BlockSpec((STEP * PER, BV, BV), lambda i, f: (i, 0, 0)),
+                pl.BlockSpec(received.shape, lambda i, f, p: (0, 0, 0)),
+                pl.BlockSpec((STEP, 3 * ROWS, ROWS), lambda i, f, p: (i, 0, 0)),
+                pl.BlockSpec((STEP * PER, BV, BV), lambda i, f, p: (i, 0, 0)),
             ],
-            out_specs=pl.BlockSpec((NZ * NY, NX), lambda i, f: (0, 0)),
+            out_specs=(
+                pl.BlockSpec((NZ * NY, NX), lambda i, f, p: (0, 0)),
+                pl.BlockSpec((RAD * NY, NX), lambda i, f, p: (0, 0)),
+            ),
             scratch_shapes=[pltpu.VMEM((ROWS, BV), F32)],
         ),
-        out_shape=jax.ShapeDtypeStruct((NZ * NY, NX), F32),
+        out_shape=(
+            jax.ShapeDtypeStruct((NZ * NY, NX), F32),
+            jax.ShapeDtypeStruct((RAD * NY, NX), F32),
+        ),
         name="mix",
-    )(flat, received, spread_z, mix_yx)
-
-
-def fetch_and_mix(moving, owners, block_ids, counts, mix_yx, mix_z):
+    )(flat, place, received, spread_z, mix_yx)
+
+
+def fetch_and_mix(place, moving, owners, block_ids, counts, mix_yx, mix_z):
     rows_gy = lax.axis_size("gy")
     groups = rows_gy * lax.axis_size("gx")
     holders = groups // 2
@@ -215,64 +226,281 @@
     slot_pos = jnp.arange(SLOTS, dtype=jnp.int32)
     keep = slot_pos % SOURCES < jnp.repeat(counts.reshape(-1), SOURCES)
     weights_z = jnp.where(keep[:, None, None], mix_z.reshape(SLOTS, VZ, VZ), 0.0).reshape(SLOTS * VZ, VZ)
-    warped = mix(
+    return mix(
         flat.reshape(-1),
+        place,
         received.reshape(groups * capacity, VZ, BV),
         spread(weights_z),
         mix_yx.reshape(SLOTS, BV, BV),
     )
-    return warped.reshape(NZ, NY, NX)
-
-
-def padded_2(block, sides, width):
-    for axis, dim in sides:
-        count = lax.axis_size(axis)
-        forward = [(i, i + 1) for i in range(count - 1)]
-        backward = [(target, source) for source, target in forward]
-        low = lax.ppermute(
-            lax.slice_in_dim(block, block.shape[dim] - width, None, axis=dim), axis, forward
-        )
-        high = lax.ppermute(lax.slice_in_dim(block, 0, width, axis=dim), axis, backward)
-        block = jnp.concatenate([low, block, high], axis=dim)
-    return block
-
-
-def box_along(padded, axis):
-    length = padded.shape[axis] - 2 * RAD
-    total = lax.slice_in_dim(padded, 0, length, axis=axis)
-    for shift in range(1, 2 * RAD + 1):
-        total = total + lax.slice_in_dim(padded, shift, shift + length, axis=axis)
+
+
+REACH = 2 * RAD
+EZ = NZ + REACH
+EY = NY + REACH
+COUNT = float((REACH + 1) ** 3)
+
+
+def ysend_kernel(has_odd, place_ref, own_ref, side_ref, *outs):
+    even = place_ref[1] == 0
+    for p in range(NZ + RAD):
+        source, start = (own_ref, p * NY) if p < NZ else (side_ref, (p - NZ) * NY)
+        first = source[start : start + VY, :][:RAD]
+        last = source[start + NY - VY : start + NY, :][VY - RAD :]
+        outs[0][p] = jnp.where(even, last, first)
+        if has_odd:
+            outs[1][p] = jnp.where(even, first, last)
+
+
+def ysend(place, own, side, has_odd):
+    shape = jax.ShapeDtypeStruct((NZ + RAD, RAD, NX), F32)
+    count = 2 if has_odd else 1
+    return pl.pallas_call(
+        lambda *refs: ysend_kernel(has_odd, *refs),
+        out_shape=(shape,) * count,
+        in_specs=[SMEM, VMEM, VMEM],
+        out_specs=(VMEM,) * count,
+        name="ysend",
+    )(place, own, side)
+
+
+def extend_kernel(y_count, x_count, place_ref, own_ref, side_ref, *refs):
+    y_refs, ext_ref, x_refs = refs[:y_count], refs[y_count], refs[y_count + 1 :]
+    low_z = place_ref[0] == 0
+    even_y = place_ref[1] == 0
+    even_x = place_ref[2] == 0
+    nothing = jnp.zeros((EY, NX), F32)
+    side_at = jnp.where(low_z, RAD + NZ, 0)
+    none_at = jnp.where(low_z, 0, RAD + NZ)
+    for p in range(NZ + RAD):
+        if p < NZ:
+            at, rows = RAD + p, own_ref[p * NY : (p + 1) * NY, :]
+        else:
+            at, rows = side_at + (p - NZ), side_ref[(p - NZ) * NY : (p - NZ + 1) * NY, :]
+            ext_ref[none_at + (p - NZ)] = nothing
+        first = y_refs[0][p]
+        second = y_refs[1][p] if y_count == 2 else jnp.zeros_like(first)
+        below = jnp.where(even_y, second, first)
+        above = jnp.where(even_y, first, second)
+        ext_ref[at] = jnp.concatenate([below, rows, above], 0)
+    slot = iota((VY, NX), 1) // RAD
+    for k in range(x_count):
+        lift = jnp.where(even_x, RAD, 0) if k == 0 else jnp.where(even_x, 0, RAD)
+        for q in range(EY // VY):
+            packed = jnp.zeros((VY, NX), F32)
+            for p in range(EZ):
+                rows = pltpu.roll(ext_ref[p, q * VY : (q + 1) * VY, :], lift + p * RAD, 1)
+                packed = jnp.where(slot == p, rows, packed)
+            x_refs[k][q * VY : (q + 1) * VY, :] = packed
+
+
+def extend(place, own, side, y_halos, x_count):
+    packed = jax.ShapeDtypeStruct((EY, NX), F32)
+    return pl.pallas_call(
+        lambda *refs: extend_kernel(len(y_halos), x_count, *refs),
+        out_shape=(jax.ShapeDtypeStruct((EZ, EY, NX), F32),) + (packed,) * x_count,
+        in_specs=[SMEM] + [VMEM] * (2 + len(y_halos)),
+        out_specs=(VMEM,) * (1 + x_count),
+        name="extend",
+    )(place, own, side, *y_halos)
+
+
+def window(parts, length):
+    two = [parts[i] + parts[i + 1] for i in range(len(parts) - 1)]
+    four = [two[i] + two[i + 2] for i in range(len(two) - 2)]
+    eight = [four[i] + four[i + 4] for i in range(len(four) - 4)]
+    return [eight[i] + parts[i + 8] for i in range(length)]
+
+
+def window_rows(value):
+    two = value + pltpu.roll(value, EY - 1, 0)
+    four = two + pltpu.roll(two, EY - 2, 0)
+    eight = four + pltpu.roll(four, EY - 4, 0)
+    return (eight + pltpu.roll(value, EY - 8, 0))[:NY]
+
+
+def split_dot(value, table):
+    total = None
+    for part in pieces(value, 3):
+        term = jnp.dot(part, table, preferred_element_type=F32)
+        total = term if total is None else total + term
     return total
 
 
+def brick_sums(kinds, fields, planes, out_ref):
+    for q in range(EY // VY):
+        for f, parts in enumerate(fields(q)):
+            for z, total in enumerate(window(parts, NZ)):
+                planes[f * NZ + z, q * VY : (q + 1) * VY, :] = total
+    near = jnp.where(jnp.abs(iota((NX, NX), 0) - iota((NX, NX), 1)) <= RAD, 1.0, 0.0).astype(BF16)
+
+    def one(i, _):
+        out_ref[i] = split_dot(window_rows(planes[i]), near)
+        return 0
+
+    lax.fori_loop(0, kinds * NZ, one, 0, unroll=2)
+
+
+def load_planes(ref, q):
+    return [ref[p, q * VY : (q + 1) * VY, :] for p in range(EZ)]
+
+
+def edge_table(right):
+    row, col = iota((NX, NX), 0), iota((NX, NX), 1)
+    plane, i = row // RAD, row % RAD
+    z, j = col // RAD, col % RAD
+    reach = jnp.where(right, j - i, i - j)
+    inside = (plane >= z) & (plane <= z + REACH) & (z < NZ) & (plane < EZ) & (reach >= 0)
+    return jnp.where(inside, 1.0, 0.0).astype(BF16)
+
+
+def edge_sums(fields, table):
+    return [split_dot(window_rows(field), table) for field in fields]
+
+
+def at_edge(right):
+    return iota((NY, NX), 1) // RAD == jnp.where(right, NX // RAD - 1, 0)
+
+
+def edge_part(sums, z, right, mask):
+    base = jnp.where(right, NX - RAD, 0)
+    return jnp.where(mask, pltpu.roll(sums, lax.rem(base + NX - RAD * z, NX), 1), 0.0)
+
+
+def side_is_right(place_ref, k):
+    even = place_ref[2] == 0
+    return even if k == 0 else jnp.logical_not(even)
+
+
+def fixed_sums_kernel(x_count, place_ref, ext_ref, *refs):
+    x_refs, out_ref, planes = refs[:x_count], refs[x_count], refs[x_count + 1]
+
+    def fields(q):
+        values = load_planes(ext_ref, q)
+        return [values, [v * v for v in values]]
+
+    brick_sums(2, fields, planes, out_ref)
+    for k in range(x_count):
+        right = side_is_right(place_ref, k)
+        halo = x_refs[k][...]
+        mask = at_edge(right)
+        for f, sums in enumerate(edge_sums([halo, halo * halo], edge_table(right))):
+            for z in range(NZ):
+                out_ref[f * NZ + z] += edge_part(sums, z, right, mask)
+
+
+def fixed_sums(place, ext, x_halos):
+    return pl.pallas_call(
+        lambda *refs: fixed_sums_kernel(len(x_halos), *refs),
+        out_shape=jax.ShapeDtypeStruct((2 * NZ, NY, NX), F32),
+        in_specs=[SMEM] + [VMEM] * (1 + len(x_halos)),
+        out_specs=VMEM,
+        scratch_shapes=[pltpu.VMEM((2 * NZ, EY, NX), F32)],
+        name="fixed_sums",
+    )(place, ext, *x_halos)
+
+
+def warped_sums_kernel(warped_ref, fixed_ref, out_ref, planes):
+    def fields(q):
+        w, f = load_planes(warped_ref, q), load_planes(fixed_ref, q)
+        return [w, [v * v for v in w], [u * v for u, v in zip(f, w)]]
+
+    brick_sums(3, fields, planes, out_ref)
+
+
+def warped_sums(warped_ext, fixed_ext):
+    return pl.pallas_call(
+        warped_sums_kernel,
+        out_shape=jax.ShapeDtypeStruct((3 * NZ, NY, NX), F32),
+        in_specs=[VMEM, VMEM],
+        out_specs=VMEM,
+        scratch_shapes=[pltpu.VMEM((3 * NZ, EY, NX), F32)],
+        name="warped_sums",
+    )(warped_ext, fixed_ext)
+
+
+def force_kernel(x_count, place_ref, sums_ref, fixed_sums_ref, fixed_ref, ext_ref, *refs):
+    warped_halos, fixed_halos = refs[:x_count], refs[x_count : 2 * x_count]
+    force_ref, edges = refs[2 * x_count], refs[2 * x_count + 1]
+    for k in range(x_count):
+        right = side_is_right(place_ref, k)
+        w, f = warped_halos[k][...], fixed_halos[k][...]
+        for i, sums in enumerate(edge_sums([w, w * w, f * w], edge_table(right))):
+            edges[4 * k + i] = sums
+        edges[4 * k + 3] = w[RAD : RAD + NY]
+    scale = 1.0 / COUNT
+    lane = iota((NY, NX), 1)
+
+    def plane(z, _):
+        sums = [sums_ref[f * NZ + z] for f in range(3)]
+        own = ext_ref[z + RAD, RAD : RAD + NY, :]
+        after = jnp.where(lane == NX - 1, 0.0, pltpu.roll(own, NX - 1, 1))
+        before = jnp.where(lane == 0, 0.0, pltpu.roll(own, 1, 1))
+        for k in range(x_count):
+            right = side_is_right(place_ref, k)
+            mask = at_edge(right)
+            sums = [total + edge_part(edges[4 * k + i], z, right, mask) for i, total in enumerate(sums)]
+            turn = jnp.where(right, NX - 1, NX + 1 - RAD) + NX - RAD * (z + RAD)
+            halo = pltpu.roll(edges[4 * k + 3], lax.rem(turn, NX), 1)
+            after = jnp.where(lane == jnp.where(right, NX - 1, -1), halo, after)
+            before = jnp.where(lane == jnp.where(right, -1, 0), halo, before)
+        mean_w = sums[0] * scale
+        mean_f = fixed_sums_ref[z] * scale
+        cov = sums[2] * scale - mean_f * mean_w
+        var_f = fixed_sums_ref[NZ + z] * scale - mean_f * mean_f + 1e-5
+        var_w = sums[1] * scale - mean_w * mean_w + 1e-5
+        image = fixed_ref[z].astype(F32)
+        deriv = 2.0 * cov / (var_f * var_w) * ((image - mean_f) - cov / var_w * (own - mean_w))
+        half = 0.5 * deriv
+        above, below = ext_ref[z + RAD + 1, RAD : RAD + NY, :], ext_ref[z + RAD - 1, RAD : RAD + NY, :]
+        force_ref[0, z] = half * (above - below)
+        force_ref[1, z] = half * (ext_ref[z + RAD, RAD + 1 : RAD + 1 + NY, :] - ext_ref[z + RAD, RAD - 1 : RAD - 1 + NY, :])
+        force_ref[2, z] = half * (after - before)
+        return 0
+
+    lax.fori_loop(0, NZ, plane, 0)
+
+
+def force_of(place, sums, sums_f, fixed, ext, warped_halos, fixed_halos):
+    count = len(warped_halos)
+    return pl.pallas_call(
+        lambda *refs: force_kernel(count, *refs),
+        out_shape=jax.ShapeDtypeStruct((3, NZ, NY, NX), F32),
+        in_specs=[SMEM] + [VMEM] * (4 + 2 * count),
+        out_specs=VMEM,
+        scratch_shapes=[pltpu.VMEM((4 * count, NY, NX), F32)],
+        name="force",
+    )(place, sums, sums_f, fixed, ext, *warped_halos, *fixed_halos)
+
+
+def pairings(size):
+    even = [(i, i ^ 1) for i in range(size) if (i ^ 1) < size]
+    odd = [(i, i + 1 if i % 2 else i - 1) for i in range(1, size)]
+    odd = [(i, j) for i, j in odd if j < size]
+    return [pairs for pairs in (even, odd) if pairs]
+
+
+def halos(place, own, side):
+    side = lax.ppermute(side, "gz", pairings(lax.axis_size("gz"))[0])
+    along_y = pairings(lax.axis_size("gy"))
+    sent = ysend(place, own, side, len(along_y) == 2)
+    received = [lax.ppermute(s, "gy", pairs) for s, pairs in reversed(list(zip(sent, along_y)))][::-1]
+    along_x = pairings(lax.axis_size("gx"))
+    ext, *columns = extend(place, own, side, received, len(along_x))
+    return ext, [lax.ppermute(c, "gx", pairs) for c, pairs in zip(columns, along_x)]
+
+
 def per_device(fixed, moving, owners, block_ids, counts, mix_yx, mix_z):
-    warped = fetch_and_mix(moving, owners, block_ids, counts, mix_yx, mix_z)
-    image = fixed.astype(jnp.float32)
-    fields = jnp.stack([image, warped, image * image, warped * warped, image * warped])
-    padded = padded_2(fields, (("gz", 1),), RAD)
-    sums = box_along(padded, 1)
-    padded = padded_2(sums, (("gy", 2),), RAD)
-    sums = box_along(padded, 2)
-    padded = padded_2(sums, (("gx", 3),), RAD)
-    sums = box_along(padded, 3)
-    wpad = padded_2(warped, (("gz", 0), ("gy", 1), ("gx", 2)), 1)
-    count = float((2 * RAD + 1) ** 3)
-    mean_f = sums[0] / count
-    mean_w = sums[1] / count
-    cov = sums[4] / count - mean_f * mean_w
-    var_f = sums[2] / count - mean_f * mean_f
-    var_w = sums[3] / count - mean_w * mean_w
-    deriv = (
-        2.0
-        * cov
-        / ((var_f + 1e-05) * (var_w + 1e-05))
-        * (image - mean_f - cov / (var_w + 1e-05) * (warped - mean_w))
-    )
-    slope_z = (wpad[2:, 1:-1, 1:-1] - wpad[:-2, 1:-1, 1:-1]) * 0.5
-    slope_y = (wpad[1:-1, 2:, 1:-1] - wpad[1:-1, :-2, 1:-1]) * 0.5
-    slope_x = (wpad[1:-1, 1:-1, 2:] - wpad[1:-1, 1:-1, :-2]) * 0.5
-    force = jnp.stack([deriv * slope_z, deriv * slope_y, deriv * slope_x])
-    return (warped, force)
+    place = jnp.stack([lax.axis_index("gz"), lax.axis_index("gy") % 2, lax.axis_index("gx") % 2]).astype(jnp.int32)
+    warped, side = fetch_and_mix(place, moving, owners, block_ids, counts, mix_yx, mix_z)
+    image = fixed.astype(F32).reshape(NZ * NY, NX)
+    start = jnp.where(place[0] == 0, (NZ - RAD) * NY, 0)
+    fixed_ext, fixed_columns = halos(place, image, lax.dynamic_slice_in_dim(image, start, RAD * NY, 0))
+    sums_f = fixed_sums(place, fixed_ext, fixed_columns)
+    ext, columns = halos(place, warped, side)
+    sums = warped_sums(ext, fixed_ext)
+    force = force_of(place, sums, sums_f, fixed, ext, columns, fixed_columns)
+    return warped.reshape(NZ, NY, NX), force
 
 
 def solution(mesh):

time: 144 us -> 100 us (0.69)
  Pallas kernels: 24.6 us -> 51.4 us
  other arithmetic: 27.4 us -> 2.63 us
  local copies, waits for them, and re-layouts: 28.7 us -> 8.72 us
  starting transfers between devices: 38.7 us -> 20.5 us
  waiting for transfers between devices: 15.4 us -> 7.42 us
    pallas_call x0 -> x7, Pallas kernels: none -> 26.8 us  [the longest x1 7.45 us: warped_sums(): pl.pallas_call(warped_sums_kernel, out_shape=jax.ShapeDtypeStruct((3 * NZ...]
    add x3 -> x0, other arithmetic: 20.8 us -> none  [box_along(): total = total + lax.slice_in_dim(padded, shift, shift + length, axis=axis)]
    ppermute x12 -> x8, starting transfers between devices: 30.7 us -> 12.7 us  [the longest x4 10.6 us: halos(): lax.ppermute(s, 'gy', pairs)]
    slice x9 -> x0, local copies, waits for them, and re-layouts: 12.5 us -> none  [the longest x5 6.64 us: padded_2(): lax.slice_in_dim(block, block.shape[dim] - width, None, axis=dim)]
    ppermute x6 -> x0, local copies, waits for them, and re-layouts: 9.02 us -> none  [the longest x3 4.54 us: padded_2(): lax.ppermute(lax.slice_in_dim(block, 0, width, axis=dim), axis, backward)]
    ppermute x12 -> x8, waiting for transfers between devices: 7.43 us -> 0.02 us  [the longest x4 0.01 us: halos(): lax.ppermute(s, 'gy', pairs)]
    another operation x5 -> x1, other arithmetic: 2.52 us -> 0.61 us  [per_device(): jnp.stack([lax.axis_index('gz'), lax.axis_index('gy') % 2, lax.axis_index...]
    unnamed x18 -> x29, local copies, waits for them, and re-layouts: 5.6 us -> 7.1 us
  transfers between devices with their start and end apart: 14 -> 10, of which waited for: 4 -> 2; matrix products, arithmetic and copies ran while one was open for 16% -> 5% of each run, Pallas kernels for 3% -> 38%
where the time goes in v2:
time: 100 us; the launch traced here: 98.9 us
  Pallas kernels  51.4 us (51%)
  starting transfers between devices  20.5 us (20%)
  local copies, waits for them, and re-layouts  8.72 us (9%)
  waiting for transfers between devices  7.42 us (7%)
  blocking collectives  7.35 us (7%)
  other arithmetic  2.63 us (3%)
    pallas_call x1, Pallas kernels, mix(): pl.pallas_call(mix_kernel, grid_spec=pltpu.PrefetchScalarGridSpec(num_sca...  11.4 us
    ppermute x4, starting transfers between devices, halos(): lax.ppermute(s, 'gy', pairs)  10.6 us
    pallas_call x1, Pallas kernels, warped_sums(): pl.pallas_call(warped_sums_kernel, out_shape=jax.ShapeDtypeStruct((3 * NZ...  7.45 us
    all_to_all x1, blocking collectives, fetch_and_mix(): lax.all_to_all(request, BRICKS, split_axis=0, concat_axis=0, tiled=True,...  7.35 us
    unnamed x29, local copies, waits for them, and re-layouts  7.1 us
    pallas_call x1, Pallas kernels, fixed_sums(): pl.pallas_call(lambda *refs: fixed_sums_kernel(len(x_halos), *refs), out_...  5.89 us
    pallas_call x1, Pallas kernels, prepare(): pl.pallas_call(prepare_kernel, out_shape=(jax.ShapeDtypeStruct((BLOCKS, V...  5.81 us
    pallas_call x1, Pallas kernels, force_of(): pl.pallas_call(lambda *refs: force_kernel(count, *refs), out_shape=jax.Sh...  5.49 us
  transfers between devices with their start and end apart: 10, of which 2 were waited for; matrix products, arithmetic and copies ran while one was open for 5% of the time, Pallas kernels for 38%

profile of v2, /device:TPU:14, one launch (start us, length us, event | category | flops | bytes accessed | tf_op | source)
XLA Modules:
  0.0 98.9 jit_solution(989614549678249983)
XLA Ops:
  0.6 5.8 %prepare.1 = (bf16[128,8,128]{2,1,0:T(8,128)(2,1)}, s32[8,1,64]{2,1,0:T(1,128)}, s32[1,256]{1,0:T(1,128)}) custom-call(s32[1]{0:T(128)} %bitcast.half_ref, bf16[16,64,128]{2,1,0:T(8,128)(2,1)} %moving_ref.1, s32[1,256]{1,0:T(1,128)} %bitcast.21, s32[1,256]{1,0:T(1,128)} %bitcast.22), custom_call_target="tpu_custom_call" | custom-call | tf_op jit(solution)/shard_map/prepare/pallas_call | solution.py:96
  6.5 2.6 %collective-permute-start = (bf16[128,8,128]{2,1,0:T(8,128)(2,1)}, bf16[128,8,128]{2,1,0:T(8,128)(2,1)S(1)}, u32[]{:S(2)}, u32[]{:S(2)}) collective-permute-start(bf16[128,8,128]{2,1,0:T(8,128)(2,1)} %get-tuple-element.17.refs_1_), channel_id=1, source_target_pairs={{0,8},{2,10},{4,12},{6,14},{8,0},{10,2},{12,4},{14,6},{1,9},{3,11}... | collective-permute-start | bytes 786440 | tf_op jit(solution)/shard_map/ppermute | solution.py:222
  9.0 7.3 %all_to_all.10 = s32[8,1,64]{2,1,0:T(1,128)S(1)} all-to-all(s32[8,1,64]{2,1,0:T(1,128)} %get-tuple-element.16), channel_id=1, replica_groups={{0,1,2,3,4,5,6,7},{8,9,10,11,12,13,14,15},{16,17,18,19,20,21,22,23},{24..., dimensions={0} | all-to-all | bytes 4096 | tf_op jit(solution)/shard_map/all_to_all | solution.py:223
  16.9 0.7 reduce.3
  17.6 0.6 reshape.69.refs_0_
  18.2 2.2 %collective-permute-done.refs_2_ = bf16[128,8,128]{2,1,0:T(8,128)(2,1)S(1)} collective-permute-done((bf16[128,8,128]{2,1,0:T(8,128)(2,1)}, bf16[128,8,128]{2,1,0:T(8,128)(2,1)S(1)}, u32[]{:S(2)}, u32[]{:S(2)}) %collective-permute-start) | collective-permute-done | bytes 262176 | tf_op jit(solution)/shard_map/ppermute | solution.py:222
  20.4 0.7 copy-done.5
  21.1 2.6 %pick.1 = bf16[512,8,128]{2,1,0:T(8,128)(2,1)} custom-call(s32[512]{0:T(512)} %reshape.69.refs_0_, bf16[128,8,128]{2,1,0:T(8,128)(2,1)} %get-tuple-element.17.refs_1_, bf16[128,8,128]{2,1,0:T(8,128)(2,1)} %copy-done.5), custom_call_target="tpu_custom_call" | custom-call | tf_op jit(solution)/shard_map/pick/pallas_call | solution.py:123
  23.8 5.2 %all-to-all-start.1 = ((bf16[8,64,8,128]{3,2,1,0:T(8,128)(2,1)}), bf16[8,64,8,128]{3,2,1,0:T(8,128)(2,1)S(1)}, u32[]{:S(2)}, u32[]{:S(2)}) async-start(bf16[8,64,8,128]{3,2,1,0:T(8,128)(2,1)} %bitcast.19), calls=%async_computation.1 | async-start | bytes 2097152 | tf_op jit(solution)/shard_map/all_to_all | solution.py:225
  30.1 1.3 %bitcast_select_fusion.mix_ref = f32[2048,8]{1,0:T(8,128)} fusion(f32[1,1,1,256,8,8]{5,4,3,2,1,0:T(8,128)S(1)} %copy.10, pred[2048]{0:T(1024)(128)(4,1)S(1)} %broadcast_in_dim.22), kind=kLoop, calls=%fused_computation | loop fusion | flops 16384 | bytes 133120 | tf_op jit(solution)/shard_map/jit(_where)/select_n | solution.py:228
  31.4 4.8 %spread.1.spread_ref = bf16[16,384,128]{2,1,0:T(8,128)(2,1)} custom-call(f32[2048,8]{1,0:T(8,128)} %bitcast_select_fusion.mix_ref), custom_call_target="tpu_custom_call" | custom-call | tf_op jit(solution)/shard_map/spread/pallas_call | solution.py:147
  36.2 0.6 pad_add_fusion.place_ref.refs_0_
  36.8 5.2 %all-to-all-done.1 = bf16[8,64,8,128]{3,2,1,0:T(8,128)(2,1)S(1)} async-done(((bf16[8,64,8,128]{3,2,1,0:T(8,128)(2,1)}), bf16[8,64,8,128]{3,2,1,0:T(8,128)(2,1)S(1)}, u32[]{:S(2)}, u32[]{:S(2)}) %all-to-all-start.1) | async-done | bytes 1048608 | tf_op jit(solution)/shard_map/all_to_all | solution.py:225
  42.0 1.0 %copy-done.1 = bf16[8,64,8,128]{3,2,1,0:T(8,128)(2,1)} copy-done((bf16[8,64,8,128]{3,2,1,0:T(8,128)(2,1)}, bf16[8,64,8,128]{3,2,1,0:T(8,128)(2,1)S(1)}, u32[]{:S(2)}) %copy-start.1) | copy-done | bytes 1048600
  43.0 11.4 %mix.1 = (f32[1024,128]{1,0:T(8,128)}, f32[256,128]{1,0:T(8,128)}) custom-call(s32[256]{0:T(256)} %bitcast.23, s32[3]{0:T(128)} %pad_add_fusion.place_ref.refs_0_, bf16[512,8,128]{2,1,0:T(8,128)(2,1)} %bitcast.18, bf16[16,384,128]{2,1,0:T(8,128)(2,1)} %spread.1.spread_ref, bf16[256,128,128]{2,1,0:T(8,128)(2,1)} %bitcast.17), custom_call_target="tpu_custom_call" | custom-call | tf_op jit(solution)/shard_map/mix/pallas_call | solution.py:190
  54.4 0.6 copy-done.3
  55.1 1.7 %ysend.3 = (f32[20,4,128]{2,1,0:T(4,128)}, f32[20,4,128]{2,1,0:T(4,128)}) custom-call(s32[3]{0:T(128)} %pad_add_fusion.place_ref.refs_0_, f32[1024,128]{1,0:T(8,128)} %copy-done, f32[256,128]{1,0:T(8,128)} %copy-done.3), custom_call_target="tpu_custom_call" | custom-call | tf_op jit(solution)/shard_map/ysend/pallas_call | solution.py:258
  56.8 0.8 collective-permute-start.5
  57.5 5.4 %collective-permute-start.6 = (f32[20,4,128]{2,1,0:T(4,128)}, f32[20,4,128]{2,1,0:T(4,128)S(1)}, u32[]{:S(2)}, u32[]{:S(2)}) collective-permute-start(f32[20,4,128]{2,1,0:T(4,128)} %get-tuple-element.24), channel_id=1, source_target_pairs={{2,4},{4,2},{6,8},{8,6},{10,12},{12,10},{3,5},{5,3},{7,9},{9,7},{1... | collective-permute-start | bytes 122888 | tf_op jit(solution)/shard_map/ppermute | solution.py:487
  63.0 0.7 copy-done.4
  63.6 1.7 %ysend.2 = (f32[20,4,128]{2,1,0:T(4,128)}, f32[20,4,128]{2,1,0:T(4,128)}) custom-call(s32[3]{0:T(128)} %pad_add_fusion.place_ref.refs_0_, f32[1024,128]{1,0:T(8,128)} %get-tuple-element.18.refs_1_, f32[256,128]{1,0:T(8,128)} %copy-done.4), custom_call_target="tpu_custom_call" | custom-call | tf_op jit(solution)/shard_map/ysend/pallas_call | solution.py:258
  65.4 4.4 %collective-permute-start.3 = (f32[20,4,128]{2,1,0:T(4,128)}, f32[20,4,128]{2,1,0:T(4,128)S(1)}, u32[]{:S(2)}, u32[]{:S(2)}) collective-permute-start(f32[20,4,128]{2,1,0:T(4,128)} %get-tuple-element.21), channel_id=1, source_target_pairs={{2,4},{4,2},{6,8},{8,6},{10,12},{12,10},{3,5},{5,3},{7,9},{9,7},{1... | collective-permute-start | bytes 122888 | tf_op jit(solution)/shard_map/ppermute | solution.py:487
  70.4 0.6 copy-done.11
  71.0 2.2 %extend.3 = (f32[24,72,128]{2,1,0:T(8,128)}, f32[72,128]{1,0:T(8,128)}) custom-call(s32[3]{0:T(128)} %pad_add_fusion.place_ref.refs_0_, f32[1024,128]{1,0:T(8,128)} %copy-done, f32[256,128]{1,0:T(8,128)} %copy-done.3, f32[20,4,128]{2,1,0:T(4,128)} %copy-done.9, f32[20,4,128]{2,1,0:T(4,128)} %copy-done.11), custom_call_target="tpu_custom_call" | custom-call | tf_op jit(solution)/shard_map/extend/pallas_call | solution.py:299
  73.2 0.8 collective-permute-start.7
  74.0 0.6 copy-done.8
  75.2 2.3 %extend.2 = (f32[24,72,128]{2,1,0:T(8,128)}, f32[72,128]{1,0:T(8,128)}) custom-call(s32[3]{0:T(128)} %pad_add_fusion.place_ref.refs_0_, f32[1024,128]{1,0:T(8,128)} %get-tuple-element.18.refs_1_, f32[256,128]{1,0:T(8,128)} %copy-done.4, f32[20,4,128]{2,1,0:T(4,128)} %copy-done.8, f32[20,4,128]{2,1,0:T(4,128)} %copy-done.10), custom_call_target="tpu_custom_call" | custom-call | tf_op jit(solution)/shard_map/extend/pallas_call | solution.py:299
  77.5 1.3 %collective-permute-start.8 = (f32[72,128]{1,0:T(8,128)}, f32[72,128]{1,0:T(8,128)S(1)}, u32[]{:S(2)}, u32[]{:S(2)}) collective-permute-start(f32[72,128]{1,0:T(8,128)} %get-tuple-element.27), channel_id=1, source_target_pairs={{0,1},{1,0},{2,3},{3,2},{4,5},{5,4},{6,7},{7,6},{8,9},{9,8},{10,11... | collective-permute-start | bytes 110600 | tf_op jit(solution)/shard_map/ppermute | solution.py:490
  78.8 0.6 copy-done.6
  79.4 5.9 %fixed_sums.1.refs_2_ = f32[32,64,128]{2,1,0:T(8,128)} custom-call(s32[3]{0:T(128)} %pad_add_fusion.place_ref.refs_0_, f32[24,72,128]{2,1,0:T(8,128)} %get-tuple-element.25.fixed_ref.refs_1_, f32[72,128]{1,0:T(8,128)} %copy-done.6), custom_call_target="tpu_custom_call" | custom-call | tf_op jit(solution)/shard_map/fixed_sums/pallas_call | solution.py:393
  85.3 7.5 %warped_sums.1.refs_1_ = f32[48,64,128]{2,1,0:T(8,128)} custom-call(f32[24,72,128]{2,1,0:T(8,128)} %get-tuple-element.22.warped_ref.refs_4_, f32[24,72,128]{2,1,0:T(8,128)} %get-tuple-element.25.fixed_ref.refs_1_), custom_call_target="tpu_custom_call" | custom-call | tf_op jit(solution)/shard_map/warped_sums/pallas_call | solution.py:412
  93.4 5.5 %force.1 = f32[3,16,64,128]{3,2,1,0:T(8,128)} custom-call(s32[3]{0:T(128)} %pad_add_fusion.place_ref.refs_0_, f32[48,64,128]{2,1,0:T(8,128)} %warped_sums.1.refs_1_, f32[32,64,128]{2,1,0:T(8,128)} %fixed_sums.1.refs_2_, bf16[16,64,128]{2,1,0:T(8,128)(2,1)} %refs_3_.1, f32[24,72,128]{2,1,0:T(8,128)} %get-tuple-element.22.warped_ref.refs_4_, ...), custom_call_target="tpu_custom_call" | custom-call | tf_op jit(solution)/shard_map/force/pallas_call | solution.py:466
  (41 shorter events, 3.4 us)
Async XLA Ops:
  6.5 14.0 %collective-permute-start = (bf16[128,8,128]{2,1,0:T(8,128)(2,1)}, bf16[128,8,128]{2,1,0:T(8,128)(2,1)S(1)}, u32[]{:S(2)}, u32[]{:S(2)}) collective-permute-start(bf16[128,8,128]{2,1,0:T(8,128)(2,1)} %get-tuple-element.17.refs_1_), channel_id=1, source_target_pairs={{0,8},{2,10},{4,12},{6,14},{8,0},{10,2},{12,4},{14,6},{1,9},{3,11}... | collective-permute-start | bytes 786440 | tf_op jit(solution)/shard_map/ppermute | solution.py:222
  18.2 10.8 %copy-start.2 = (bf16[16,64,128]{2,1,0:T(8,128)(2,1)S(1)}, bf16[16,64,128]{2,1,0:T(8,128)(2,1)}, u32[]{:S(2)}) copy-start(bf16[16,64,128]{2,1,0:T(8,128)(2,1)} %refs_3_.1) | copy-start | bytes 786436
  20.4 0.7 copy-start.5
  23.8 5.4 %copy-start.13 = (s32[1,1,1,128]{3,2,1,0:T(1,128)S(1)}, s32[1,1,1,128]{3,2,1,0:T(1,128)}, u32[]{:S(2)}) copy-start(s32[1,1,1,128]{3,2,1,0:T(1,128)} %param.11) | copy-start | bytes 1540
  23.8 5.9 %copy-start.7 = (f32[1,1,1,256,8,8]{3,5,4,2,1,0:T(8,128)S(1)}, f32[1,1,1,256,8,8]{3,5,4,2,1,0:T(8,128)}, u32[]{:S(2)}) copy-start(f32[1,1,1,256,8,8]{3,5,4,2,1,0:T(8,128)} %param.13) | copy-start | bytes 196612
  23.8 18.2 %all-to-all-start.1 = ((bf16[8,64,8,128]{3,2,1,0:T(8,128)(2,1)}), bf16[8,64,8,128]{3,2,1,0:T(8,128)(2,1)S(1)}, u32[]{:S(2)}, u32[]{:S(2)}) async-start(bf16[8,64,8,128]{3,2,1,0:T(8,128)(2,1)} %bitcast.19), calls=%async_computation.1 | async-start | bytes 2097152 | tf_op jit(solution)/shard_map/all_to_all | solution.py:225
  29.1 2.3 %copy-start = (f32[1024,128]{1,0:T(8,128)}, f32[1024,128]{1,0:T(8,128)S(1)}, u32[]{:S(2)}) copy-start(f32[1024,128]{1,0:T(8,128)S(1)} %bitcast_convert_fusion.refs_1_) | copy-start | bytes 1572868
  29.1 25.3 %collective-permute-start.4 = (f32[256,128]{1,0:T(8,128)S(1)}, f32[256,128]{1,0:T(8,128)S(1)}, u32[]{:S(2)}, u32[]{:S(2)}) collective-permute-start(f32[256,128]{1,0:T(8,128)S(1)} %constant_dynamic-slice_fusion), channel_id=1, source_target_pairs={{0,16},{16,0},{1,17},{17,1},{2,18},{18,2},{3,19},{19,3},{4,20},{20... | collective-permute-start | bytes 393224 | tf_op jit(solution)/shard_map/ppermute | solution.py:484
  42.0 1.0 %copy-start.1 = (bf16[8,64,8,128]{3,2,1,0:T(8,128)(2,1)}, bf16[8,64,8,128]{3,2,1,0:T(8,128)(2,1)S(1)}, u32[]{:S(2)}) copy-start(bf16[8,64,8,128]{3,2,1,0:T(8,128)(2,1)S(1)} %all-to-all-done.1) | copy-start | bytes 3145732
  54.4 8.6 %collective-permute-start.1 = (f32[256,128]{1,0:T(8,128)}, f32[256,128]{1,0:T(8,128)S(1)}, u32[]{:S(2)}, u32[]{:S(2)}) collective-permute-start(f32[256,128]{1,0:T(8,128)} %get-tuple-element.19), channel_id=1, source_target_pairs={{0,16},{16,0},{1,17},{17,1},{2,18},{18,2},{3,19},{19,3},{4,20},{20... | collective-permute-start | bytes 393224 | tf_op jit(solution)/shard_map/ppermute | solution.py:484
  54.4 0.6 copy-start.3
  56.8 13.0 %collective-permute-start.5 = (f32[20,4,128]{2,1,0:T(4,128)}, f32[20,4,128]{2,1,0:T(4,128)S(1)}, u32[]{:S(2)}, u32[]{:S(2)}) collective-permute-start(f32[20,4,128]{2,1,0:T(4,128)} %get-tuple-element.23), channel_id=1, source_target_pairs={{0,2},{2,0},{4,6},{6,4},{8,10},{10,8},{12,14},{14,12},{1,3},{3,1},... | collective-permute-start | bytes 122888 | tf_op jit(solution)/shard_map/ppermute | solution.py:487
  57.5 12.2 %collective-permute-start.6 = (f32[20,4,128]{2,1,0:T(4,128)}, f32[20,4,128]{2,1,0:T(4,128)S(1)}, u32[]{:S(2)}, u32[]{:S(2)}) collective-permute-start(f32[20,4,128]{2,1,0:T(4,128)} %get-tuple-element.24), channel_id=1, source_target_pairs={{2,4},{4,2},{6,8},{8,6},{10,12},{12,10},{3,5},{5,3},{7,9},{9,7},{1... | collective-permute-start | bytes 122888 | tf_op jit(solution)/shard_map/ppermute | solution.py:487
  63.0 0.7 copy-start.4
  65.4 8.7 %collective-permute-start.2 = (f32[20,4,128]{2,1,0:T(4,128)}, f32[20,4,128]{2,1,0:T(4,128)S(1)}, u32[]{:S(2)}, u32[]{:S(2)}) collective-permute-start(f32[20,4,128]{2,1,0:T(4,128)} %get-tuple-element.20), channel_id=1, source_target_pairs={{0,2},{2,0},{4,6},{6,4},{8,10},{10,8},{12,14},{14,12},{1,3},{3,1},... | collective-permute-start | bytes 122888 | tf_op jit(solution)/shard_map/ppermute | solution.py:487
  65.4 8.7 %collective-permute-start.3 = (f32[20,4,128]{2,1,0:T(4,128)}, f32[20,4,128]{2,1,0:T(4,128)S(1)}, u32[]{:S(2)}, u32[]{:S(2)}) collective-permute-start(f32[20,4,128]{2,1,0:T(4,128)} %get-tuple-element.21), channel_id=1, source_target_pairs={{2,4},{4,2},{6,8},{8,6},{10,12},{12,10},{3,5},{5,3},{7,9},{9,7},{1... | collective-permute-start | bytes 122888 | tf_op jit(solution)/shard_map/ppermute | solution.py:487
  69.8 0.6 copy-start.9
  70.4 0.6 copy-start.11
  73.2 5.5 %collective-permute-start.7 = (f32[72,128]{1,0:T(8,128)}, f32[72,128]{1,0:T(8,128)S(1)}, u32[]{:S(2)}, u32[]{:S(2)}) collective-permute-start(f32[72,128]{1,0:T(8,128)} %get-tuple-element.26), channel_id=1, source_target_pairs={{0,1},{1,0},{2,3},{3,2},{4,5},{5,4},{6,7},{7,6},{8,9},{9,8},{10,11... | collective-permute-start | bytes 110600 | tf_op jit(solution)/shard_map/ppermute | solution.py:490
  74.0 0.6 copy-start.8
  74.6 0.6 copy-start.10
  77.5 15.2 %collective-permute-start.8 = (f32[72,128]{1,0:T(8,128)}, f32[72,128]{1,0:T(8,128)S(1)}, u32[]{:S(2)}, u32[]{:S(2)}) collective-permute-start(f32[72,128]{1,0:T(8,128)} %get-tuple-element.27), channel_id=1, source_target_pairs={{0,1},{1,0},{2,3},{3,2},{4,5},{5,4},{6,7},{7,6},{8,9},{9,8},{10,11... | collective-permute-start | bytes 110600 | tf_op jit(solution)/shard_map/ppermute | solution.py:490
  78.8 0.6 copy-start.6
  92.7 0.6 copy-start.12

commit v3 on v1

--- a/solution.py
+++ b/solution.py
@@ -24,6 +24,7 @@
 ROWS = PER * VZ
 BRICKS = ("gy", "gx")
 F32 = jnp.float32
+LIMIT = 12 * 2**20
 BF16 = jnp.bfloat16
 
 VMEM = pl.BlockSpec(memory_space=pltpu.VMEM)
@@ -88,7 +89,7 @@
             blocks_ref[g * NBX + x] = block.astype(BF16)
         return 0
 
-    lax.fori_loop(0, GROUPS, group, 0)
+    lax.fori_loop(0, GROUPS, group, 0, unroll=4)
 
 
 def prepare(half, moving, owner, ident, groups, capacity):
@@ -103,6 +104,7 @@
         in_specs=[SMEM, VMEM, VMEM, VMEM],
         out_specs=(VMEM, VMEM, VMEM),
         scratch_shapes=[pltpu.VMEM((NZ * NY, NX), F32)],
+        compiler_params=pltpu.CompilerParams(vmem_limit_bytes=LIMIT),
         name="prepare",
     )(half, moving, owner, ident)
 
@@ -113,7 +115,7 @@
     def holder(h, _):
         for k in range(width):
             source = near_ref if k < capacity else far_ref
-            out_ref[h * width + k] = source[request_ref[h * width + k]]
+            out_ref[h * width + k] = source[request_ref[h, 0, k]]
         return 0
 
     lax.fori_loop(0, out_ref.shape[0] // width, holder, 0)
@@ -122,9 +124,10 @@
 def pick(request, near, far, capacity):
     return pl.pallas_call(
         lambda *refs: pick_kernel(capacity, *refs),
-        out_shape=jax.ShapeDtypeStruct((request.shape[0], VZ, BV), BF16),
+        out_shape=jax.ShapeDtypeStruct((request.size, VZ, BV), BF16),
         in_specs=[SMEM, VMEM, VMEM],
         out_specs=VMEM,
+        compiler_params=pltpu.CompilerParams(vmem_limit_bytes=LIMIT),
         name="pick",
     )(request, near, far)
 
@@ -140,7 +143,7 @@
             out_ref[g, k * ROWS : (k + 1) * ROWS, :] = jnp.where(same, tiled, 0.0).astype(BF16)
         return 0
 
-    lax.fori_loop(0, GROUPS, group, 0)
+    lax.fori_loop(0, GROUPS, group, 0, unroll=4)
 
 
 def spread(mix_z):
@@ -149,20 +152,20 @@
         out_shape=jax.ShapeDtypeStruct((GROUPS, 3 * ROWS, ROWS), BF16),
         in_specs=[VMEM],
         out_specs=VMEM,
+        compiler_params=pltpu.CompilerParams(vmem_limit_bytes=LIMIT),
         name="spread",
     )(mix_z)
 
 
-STEP = 2
-
-
-def mix_kernel(flat_ref, received_ref, spread_ref, mix_ref, warped_ref, source):
+STEP = 4
+
+
+def mix_kernel(flat_ref, place_ref, received_ref, spread_ref, mix_ref, warped_ref, side_ref, face_ref):
     step = pl.program_id(0)
     for q in range(STEP):
         g = step * STEP + q
-        for i in range(PER):
-            source[i * VZ : (i + 1) * VZ, :] = received_ref[flat_ref[g * PER + i]].astype(F32)
-        parts = jnp.dot(spread_ref[q], source[...].astype(BF16), preferred_element_type=F32)
+        source = jnp.concatenate([received_ref[flat_ref[g * PER + i]].astype(F32) for i in range(PER)], 0)
+        parts = jnp.dot(spread_ref[q], source.astype(BF16), preferred_element_type=F32)
         mixed = parts[:ROWS] + parts[ROWS : 2 * ROWS] + parts[2 * ROWS :]
         high = mixed.astype(BF16).astype(F32)
         low = mixed - high
@@ -180,27 +183,56 @@
         for y, row in enumerate(swap_chunks(rows)):
             warped_ref[pl.ds(start + y, VZ, stride=NY), :] = row
 
-
-def mix(flat, received, spread_z, mix_yx):
+    @pl.when(step == pl.num_programs(0) - 1)
+    def _():
+        outer(place_ref, warped_ref, side_ref, face_ref)
+
+
+def outer(place_ref, own_ref, side_ref, face_ref):
+    first = jnp.where(place_ref[0] == 0, (NZ - RAD) * NY, 0)
+    side_ref[...] = own_ref[pl.ds(pl.multiple_of(first, NY), RAD * NY), :]
+    low = iota((VY, NX), 0) < RAD
+    for z in range(NZ):
+        face_ref[z] = jnp.where(low, own_ref[z * NY : z * NY + VY, :], own_ref[(z + 1) * NY - VY : (z + 1) * NY, :])
+
+
+OUTER = (
+    jax.ShapeDtypeStruct((NZ * NY, NX), F32),
+    jax.ShapeDtypeStruct((RAD * NY, NX), F32),
+    jax.ShapeDtypeStruct((NZ, VY, NX), F32),
+)
+
+
+def mix(flat, place, received, spread_z, mix_yx):
     return pl.pallas_call(
         mix_kernel,
         grid_spec=pltpu.PrefetchScalarGridSpec(
-            num_scalar_prefetch=1,
+            num_scalar_prefetch=2,
             grid=(GROUPS // STEP,),
             in_specs=[
-                pl.BlockSpec(received.shape, lambda i, f: (0, 0, 0)),
-                pl.BlockSpec((STEP, 3 * ROWS, ROWS), lambda i, f: (i, 0, 0)),
-                pl.BlockSpec((STEP * PER, BV, BV), lambda i, f: (i, 0, 0)),
+                pl.BlockSpec(received.shape, lambda i, f, p: (0, 0, 0)),
+                pl.BlockSpec((STEP, 3 * ROWS, ROWS), lambda i, f, p: (i, 0, 0)),
+                pl.BlockSpec((STEP * PER, BV, BV), lambda i, f, p: (i, 0, 0)),
             ],
-            out_specs=pl.BlockSpec((NZ * NY, NX), lambda i, f: (0, 0)),
-            scratch_shapes=[pltpu.VMEM((ROWS, BV), F32)],
+            out_specs=(
+                pl.BlockSpec((NZ * NY, NX), lambda i, f, p: (0, 0)),
+                pl.BlockSpec((RAD * NY, NX), lambda i, f, p: (0, 0)),
+                pl.BlockSpec((NZ, VY, NX), lambda i, f, p: (0, 0, 0)),
+            ),
         ),
-        out_shape=jax.ShapeDtypeStruct((NZ * NY, NX), F32),
+        out_shape=OUTER,
+        compiler_params=pltpu.CompilerParams(vmem_limit_bytes=LIMIT),
         name="mix",
-    )(flat, received, spread_z, mix_yx)
-
-
-def fetch_and_mix(moving, owners, block_ids, counts, mix_yx, mix_z):
+    )(flat, place, received, spread_z, mix_yx)
+
+
+def image_kernel(place_ref, fixed_ref, own_ref, side_ref, face_ref):
+    for z in range(NZ):
+        own_ref[z * NY : (z + 1) * NY, :] = fixed_ref[z].astype(F32)
+    outer(place_ref, own_ref, side_ref, face_ref)
+
+
+def fetch(moving, owners, block_ids):
     rows_gy = lax.axis_size("gy")
     groups = rows_gy * lax.axis_size("gx")
     holders = groups // 2
@@ -210,69 +242,315 @@
     near, request, flat = prepare(half, moving, owners.reshape(1, SLOTS), block_ids.reshape(1, SLOTS), groups, capacity)
     far = lax.ppermute(near, "gy", [(i, (i + rows_gy // 2) % rows_gy) for i in range(rows_gy)])
     request = lax.all_to_all(request, BRICKS, split_axis=0, concat_axis=0, tiled=True, axis_index_groups=halves)
-    picked = pick(request.reshape(-1), near, far, capacity).reshape(holders, 2 * capacity, VZ, BV)
+    picked = pick(request, near, far, capacity).reshape(holders, 2 * capacity, VZ, BV)
     received = lax.all_to_all(picked, BRICKS, split_axis=0, concat_axis=0, tiled=True, axis_index_groups=halves)
+    return received.reshape(groups * capacity, VZ, BV), flat.reshape(-1)
+
+
+def spread_weights(counts, mix_z):
     slot_pos = jnp.arange(SLOTS, dtype=jnp.int32)
     keep = slot_pos % SOURCES < jnp.repeat(counts.reshape(-1), SOURCES)
-    weights_z = jnp.where(keep[:, None, None], mix_z.reshape(SLOTS, VZ, VZ), 0.0).reshape(SLOTS * VZ, VZ)
-    warped = mix(
-        flat.reshape(-1),
-        received.reshape(groups * capacity, VZ, BV),
-        spread(weights_z),
-        mix_yx.reshape(SLOTS, BV, BV),
+    return spread(jnp.where(keep[:, None, None], mix_z.reshape(SLOTS, VZ, VZ), 0.0).reshape(SLOTS * VZ, VZ))
+
+
+REACH = 2 * RAD
+EZ = NZ + REACH
+EY = NY + REACH
+COUNT = float((REACH + 1) ** 3)
+
+
+def call(kernel, name, outs, *args, scratch=()):
+    return pl.pallas_call(
+        kernel,
+        out_shape=outs,
+        in_specs=[SMEM] + [VMEM] * (len(args) - 1),
+        out_specs=jax.tree.map(lambda _: VMEM, outs),
+        scratch_shapes=scratch,
+        compiler_params=pltpu.CompilerParams(vmem_limit_bytes=LIMIT),
+        name=name,
+    )(*args)
+
+
+def array(*shape):
+    return jax.ShapeDtypeStruct(shape, F32)
+
+
+def rows_kernel(place_ref, face_ref, side_ref, *outs):
+    even = place_ref[1] == 0
+    low = iota((VY, NX), 0) < RAD
+    for p in range(NZ + RAD):
+        if p < NZ:
+            face = face_ref[p]
+        else:
+            at = (p - NZ) * NY
+            face = jnp.where(low, side_ref[at : at + VY, :], side_ref[at + NY - VY : at + NY, :])
+        outs[0][p] = jnp.where(even, face[RAD:], face[:RAD])
+        if len(outs) == 2:
+            outs[1][p] = jnp.where(even, face[:RAD], face[RAD:])
+
+
+def extended_planes(place_ref, own, side):
+    low = place_ref[0] == 0
+    empty = jnp.zeros_like(side[0])
+    before = [jnp.where(low, empty, s) for s in side]
+    after = [jnp.where(low, s, empty) for s in side]
+    return before + own + after
+
+
+def pack(place_ref, planes, k):
+    even = place_ref[2] == 0
+    lift = jnp.where(even, RAD, 0) if k == 0 else jnp.where(even, 0, RAD)
+    slot = iota((VY, NX), 1) // RAD
+    packed = jnp.zeros((VY, NX), F32)
+    for p, rows in enumerate(planes):
+        packed = jnp.where(slot == p, pltpu.roll(rows, lift + p * RAD, 1), packed)
+    return packed
+
+
+def window(parts, length):
+    two = [parts[i] + parts[i + 1] for i in range(len(parts) - 1)]
+    four = [two[i] + two[i + 2] for i in range(len(two) - 2)]
+    eight = [four[i] + four[i + 4] for i in range(len(four) - 4)]
+    return [eight[i] + parts[i + 8] for i in range(length)]
+
+
+def own_kernel(x_count, with_image, place_ref, own_ref, side_ref, *refs):
+    image_ref, sums_ref, *columns = refs
+
+    def rows_of(q, _):
+        at = pl.multiple_of(q * VY, VY)
+        rows = pl.ds(at, VY)
+        own = [own_ref[pl.ds(pl.multiple_of(z * NY + at, VY), VY), :] for z in range(NZ)]
+        side = [side_ref[pl.ds(pl.multiple_of(z * NY + at, VY), VY), :] for z in range(RAD)]
+        planes = extended_planes(place_ref, own, side)
+        for k in range(x_count):
+            columns[k][rows, :] = pack(place_ref, planes, k)
+        fields = [planes, [v * v for v in planes]]
+        if with_image:
+            fields.append([image_ref[p, rows, :] * v for p, v in enumerate(planes)])
+        else:
+            for p, v in enumerate(planes):
+                image_ref[p, rows, :] = v
+        for f, parts in enumerate(fields):
+            for z, total in enumerate(window(parts, NZ)):
+                sums_ref[f * NZ + z, rows, :] = total
+        return 0
+
+    lax.fori_loop(0, NBY, rows_of, 0)
+
+
+def columns_kernel(y_count, x_count, place_ref, *refs):
+    halos, packed, (rows_ref, *columns) = refs[:y_count], refs[y_count : y_count + x_count], refs[y_count + x_count :]
+    even = place_ref[1] == 0
+    planes = []
+    for p in range(NZ + RAD):
+        first = halos[0][p]
+        second = halos[1][p] if y_count == 2 else jnp.zeros_like(first)
+        planes.append(jnp.concatenate([jnp.where(even, first, second), jnp.where(even, second, first)], 0))
+    planes = extended_planes(place_ref, planes[:NZ], planes[NZ:])
+    for p, rows in enumerate(planes):
+        rows_ref[p] = rows
+    for k in range(x_count):
+        columns[k][:NY] = packed[k][...]
+        columns[k][NY:] = pack(place_ref, planes, k)
+
+
+def window_rows(value):
+    two = value + pltpu.roll(value, EY - 1, 0)
+    four = two + pltpu.roll(two, EY - 2, 0)
+    return (value + pltpu.roll(four, RAD, 0) + pltpu.roll(four, EY - 1, 0))[:NY]
+
+
+def split_dot(value, table):
+    total = None
+    for part in pieces(value, 3):
+        term = jnp.dot(part, table, preferred_element_type=F32)
+        total = term if total is None else total + term
+    return total
+
+
+def edge_table(right):
+    row, col = iota((NX, NX), 0), iota((NX, NX), 1)
+    plane, i = row // RAD, row % RAD
+    z, j = col // RAD, col % RAD
+    reach = jnp.where(right, j - i, i - j)
+    inside = (plane >= z) & (plane <= z + REACH) & (z < NZ) & (plane < EZ) & (reach >= 0)
+    return jnp.where(inside, 1.0, 0.0).astype(BF16)
+
+
+def at_edge(right):
+    return iota((NY, NX), 1) // RAD == jnp.where(right, NX // RAD - 1, 0)
+
+
+def edge_part(sums, z, right, mask):
+    base = jnp.where(right, NX - RAD, 0)
+    return jnp.where(mask, pltpu.roll(sums, lax.rem(base + NX - RAD * z, NX), 1), 0.0)
+
+
+def side_is_right(place_ref, k):
+    even = place_ref[2] == 0
+    return even if k == 0 else jnp.logical_not(even)
+
+
+def sums_kernel(kinds, place_ref, own_sums_ref, *refs):
+    halo_refs, out_ref, outer_sums = refs[:-2], refs[-2], refs[-1]
+    first = [halo_refs[0][p] for p in range(EZ)]
+    fields = [first, [v * v for v in first]]
+    if kinds == 3:
+        fields.append([halo_refs[1][p] * v for p, v in enumerate(first)])
+    for f, parts in enumerate(fields):
+        for z, total in enumerate(window(parts, NZ)):
+            outer_sums[f * NZ + z] = total
+    near = jnp.where(jnp.abs(iota((NX, NX), 0) - iota((NX, NX), 1)) <= RAD, 1.0, 0.0).astype(BF16)
+
+    def one(i, _):
+        out_ref[i] = split_dot(window_rows(jnp.concatenate([own_sums_ref[i], outer_sums[i]], 0)), near)
+        return 0
+
+    lax.fori_loop(0, kinds * NZ, one, 0, unroll=4)
+
+
+def sums(kinds, place, own_sums, *halo_rows):
+    return call(
+        lambda *refs: sums_kernel(kinds, *refs),
+        "sums",
+        array(kinds * NZ, NY, NX),
+        place,
+        own_sums,
+        *halo_rows,
+        scratch=(pltpu.VMEM((kinds * NZ, VY, NX), F32),),
     )
-    return warped.reshape(NZ, NY, NX)
-
-
-def padded_2(block, sides, width):
-    for axis, dim in sides:
-        count = lax.axis_size(axis)
-        forward = [(i, i + 1) for i in range(count - 1)]
-        backward = [(target, source) for source, target in forward]
-        low = lax.ppermute(
-            lax.slice_in_dim(block, block.shape[dim] - width, None, axis=dim), axis, forward
-        )
-        high = lax.ppermute(lax.slice_in_dim(block, 0, width, axis=dim), axis, backward)
-        block = jnp.concatenate([low, block, high], axis=dim)
-    return block
-
-
-def box_along(padded, axis):
-    length = padded.shape[axis] - 2 * RAD
-    total = lax.slice_in_dim(padded, 0, length, axis=axis)
-    for shift in range(1, 2 * RAD + 1):
-        total = total + lax.slice_in_dim(padded, shift, shift + length, axis=axis)
-    return total
+
+
+def force_kernel(x_count, place_ref, sums_ref, fixed_sums_ref, fixed_ref, own_ref, side_ref, rows_ref, *refs):
+    warped_halos, fixed_halos = refs[:x_count], refs[x_count : 2 * x_count]
+    force_ref, edges = refs[2 * x_count], refs[2 * x_count + 1]
+    for k in range(x_count):
+        table = edge_table(side_is_right(place_ref, k))
+        w, f = warped_halos[k][...], fixed_halos[k][...]
+        for i, field in enumerate([w, w * w, f * w, f, f * f]):
+            edges[6 * k + i] = split_dot(window_rows(field), table)
+        edges[6 * k + 5] = w[:NY]
+    scale = 1.0 / COUNT
+    lane = iota((NY, NX), 1)
+    low = place_ref[0] == 0
+
+    def plane(z, _):
+        at = pl.multiple_of(z * NY, NY)
+        box = [sums_ref[f * NZ + z] for f in range(3)] + [fixed_sums_ref[f * NZ + z] for f in range(2)]
+        own = own_ref[pl.ds(at, NY), :]
+        after = jnp.where(lane == NX - 1, 0.0, pltpu.roll(own, NX - 1, 1))
+        before = jnp.where(lane == 0, 0.0, pltpu.roll(own, 1, 1))
+        for k in range(x_count):
+            right = side_is_right(place_ref, k)
+            mask = at_edge(right)
+            box = [total + edge_part(edges[6 * k + i], z, right, mask) for i, total in enumerate(box)]
+            turn = jnp.where(right, NX - 1, NX + 1 - RAD) + NX - RAD * (z + RAD)
+            halo = pltpu.roll(edges[6 * k + 5], lax.rem(turn, NX), 1)
+            after = jnp.where(lane == jnp.where(right, NX - 1, -1), halo, after)
+            before = jnp.where(lane == jnp.where(right, -1, 0), halo, before)
+        sum_w, sum_ww, sum_fw, sum_f, sum_ff = box
+        mean_w = sum_w * scale
+        mean_f = sum_f * scale
+        cov = sum_fw * scale - mean_f * mean_w
+        var_f = sum_ff * scale - mean_f * mean_f + 1e-5
+        var_w = sum_ww * scale - mean_w * mean_w + 1e-5
+        image = fixed_ref[z].astype(F32)
+        deriv = 2.0 * cov / (var_f * var_w) * ((image - mean_f) - cov / var_w * (own - mean_w))
+        half = 0.5 * deriv
+        up = own_ref[pl.ds(pl.multiple_of(jnp.minimum(at + NY, (NZ - 1) * NY), NY), NY), :]
+        down = own_ref[pl.ds(pl.multiple_of(jnp.maximum(at - NY, 0), NY), NY), :]
+        up = jnp.where(z == NZ - 1, jnp.where(low, side_ref[:NY, :], 0.0), up)
+        down = jnp.where(z == 0, jnp.where(low, 0.0, side_ref[(RAD - 1) * NY :, :]), down)
+        force_ref[0, z] = half * (up - down)
+        tall = jnp.concatenate([own, rows_ref[z + RAD]], 0)
+        force_ref[1, z] = half * (pltpu.roll(tall, EY - 1, 0) - pltpu.roll(tall, 1, 0))[:NY]
+        force_ref[2, z] = half * (after - before)
+        return 0
+
+    lax.fori_loop(0, NZ, plane, 0, unroll=2)
+
+
+def pairings(size):
+    even = [(i, i ^ 1) for i in range(size) if (i ^ 1) < size]
+    odd = [(i, i + 1 if i % 2 else i - 1) for i in range(1, size)]
+    odd = [(i, j) for i, j in odd if j < size]
+    return [pairs for pairs in (even, odd) if pairs]
+
+
+def exchange_rows(place, face, side):
+    side = lax.ppermute(side, "gz", pairings(lax.axis_size("gz"))[0])
+    along = pairings(lax.axis_size("gy"))
+    sent = call(rows_kernel, "rows", (array(NZ + RAD, RAD, NX),) * len(along), place, face, side)
+    received = [lax.ppermute(s, "gy", pairs) for s, pairs in reversed(list(zip(sent, along)))][::-1]
+    return side, received
+
+
+def pack_columns(place, received, packed):
+    count = len(packed)
+    rows, *columns = call(
+        lambda *refs: columns_kernel(len(received), count, *refs),
+        "columns",
+        (array(EZ, VY, NX),) + (array(EY, NX),) * count,
+        place,
+        *received,
+        *packed,
+    )
+    return rows, columns
 
 
 def per_device(fixed, moving, owners, block_ids, counts, mix_yx, mix_z):
-    warped = fetch_and_mix(moving, owners, block_ids, counts, mix_yx, mix_z)
-    image = fixed.astype(jnp.float32)
-    fields = jnp.stack([image, warped, image * image, warped * warped, image * warped])
-    padded = padded_2(fields, (("gz", 1),), RAD)
-    sums = box_along(padded, 1)
-    padded = padded_2(sums, (("gy", 2),), RAD)
-    sums = box_along(padded, 2)
-    padded = padded_2(sums, (("gx", 3),), RAD)
-    sums = box_along(padded, 3)
-    wpad = padded_2(warped, (("gz", 0), ("gy", 1), ("gx", 2)), 1)
-    count = float((2 * RAD + 1) ** 3)
-    mean_f = sums[0] / count
-    mean_w = sums[1] / count
-    cov = sums[4] / count - mean_f * mean_w
-    var_f = sums[2] / count - mean_f * mean_f
-    var_w = sums[3] / count - mean_w * mean_w
-    deriv = (
-        2.0
-        * cov
-        / ((var_f + 1e-05) * (var_w + 1e-05))
-        * (image - mean_f - cov / (var_w + 1e-05) * (warped - mean_w))
+    place = jnp.stack([lax.axis_index("gz"), lax.axis_index("gy") % 2, lax.axis_index("gx") % 2]).astype(jnp.int32)
+    along = pairings(lax.axis_size("gx"))
+    count = len(along)
+    received, flat = fetch(moving, owners, block_ids)
+    weights = spread_weights(counts, mix_z)
+    image, image_side, image_face = call(image_kernel, "image", OUTER, place, fixed)
+    image_side, image_halos = exchange_rows(place, image_face, image_side)
+    image_sums, image_planes, *image_packed = call(
+        lambda place_ref, own_ref, side_ref, sums_ref, image_ref, *columns: own_kernel(
+            count, False, place_ref, own_ref, side_ref, image_ref, sums_ref, *columns
+        ),
+        "image_own",
+        (array(2 * NZ, NY, NX), array(EZ, NY, NX)) + (array(NY, NX),) * count,
+        place,
+        image,
+        image_side,
     )
-    slope_z = (wpad[2:, 1:-1, 1:-1] - wpad[:-2, 1:-1, 1:-1]) * 0.5
-    slope_y = (wpad[1:-1, 2:, 1:-1] - wpad[1:-1, :-2, 1:-1]) * 0.5
-    slope_x = (wpad[1:-1, 1:-1, 2:] - wpad[1:-1, 1:-1, :-2]) * 0.5
-    force = jnp.stack([deriv * slope_z, deriv * slope_y, deriv * slope_x])
-    return (warped, force)
+    image_rows, image_columns = pack_columns(place, image_halos, image_packed)
+    received, image_columns, weights = lax.optimization_barrier((received, image_columns, weights))
+    image_columns = [lax.ppermute(c, "gx", pairs) for c, pairs in zip(image_columns, along)]
+    warped, side, face = mix(flat, place, received, weights, mix_yx.reshape(SLOTS, BV, BV))
+    side, row_halos = exchange_rows(place, face, side)
+    own_sums, *packed = call(
+        lambda *refs: own_kernel(count, True, *refs),
+        "own",
+        (array(3 * NZ, NY, NX),) + (array(NY, NX),) * count,
+        place,
+        warped,
+        side,
+        image_planes,
+    )
+    box_f = sums(2, place, image_sums, image_rows)
+    rows, columns = pack_columns(place, row_halos, packed)
+    columns = [lax.ppermute(c, "gx", pairs) for c, pairs in zip(columns, along)]
+    box = sums(3, place, own_sums, rows, image_rows)
+    force = call(
+        lambda *refs: force_kernel(count, *refs),
+        "force",
+        array(3, NZ, NY, NX),
+        place,
+        box,
+        box_f,
+        fixed,
+        warped,
+        side,
+        rows,
+        *columns,
+        *image_columns,
+        scratch=(pltpu.VMEM((6 * count, NY, NX), F32),),
+    )
+    return warped.reshape(NZ, NY, NX), force
 
 
 def solution(mesh):

time: 144 us -> 74.3 us (0.52)
  other arithmetic: 27.4 us -> 0.42 us
  local copies, waits for them, and re-layouts: 28.7 us -> 9.47 us
  starting transfers between devices: 38.7 us -> 22.5 us
  waiting for transfers between devices: 15.4 us -> 6.25 us
  Pallas kernels: 24.6 us -> 26.7 us
    add x3 -> x0, other arithmetic: 20.8 us -> none  [box_along(): total = total + lax.slice_in_dim(padded, shift, shift + length, axis=axis)]
    ppermute x13 -> x9, starting transfers between devices: 33.3 us -> 17.2 us  [the longest x4 12.3 us: exchange_rows(): lax.ppermute(s, 'gy', pairs)]
    pallas_call x0 -> x10, Pallas kernels: none -> 15.5 us  [call(): pl.pallas_call(kernel, out_shape=outs, in_specs=[SMEM] + [VMEM] * (len(ar...]
    slice x9 -> x0, local copies, waits for them, and re-layouts: 12.5 us -> none  [the longest x5 6.64 us: padded_2(): lax.slice_in_dim(block, block.shape[dim] - width, None, axis=dim)]
    ppermute x6 -> x0, local copies, waits for them, and re-layouts: 9.02 us -> none  [the longest x3 4.54 us: padded_2(): lax.ppermute(lax.slice_in_dim(block, 0, width, axis=dim), axis, backward)]
    all_to_all x1, waiting for transfers between devices: 5.72 us -> 0.01 us  [fetch(): lax.all_to_all(picked, BRICKS, split_axis=0, concat_axis=0, tiled=True, a...]
    pallas_call x1, Pallas kernels: 11.3 us -> 6.58 us  [mix(): pl.pallas_call(mix_kernel, grid_spec=pltpu.PrefetchScalarGridSpec(num_sca...]
    pallas_call x1, Pallas kernels: 5.84 us -> 1.5 us  [prepare(): pl.pallas_call(prepare_kernel, out_shape=(jax.ShapeDtypeStruct((BLOCKS, V...]
  transfers between devices with their start and end apart: 14 -> 10, of which waited for: 4 -> 4; matrix products, arithmetic and copies ran while one was open for 16% -> 2% of each run, Pallas kernels for 3% -> 17%
where the time goes in v3:
time: 74.3 us; the launch traced here: 73.4 us
  Pallas kernels  26.7 us (36%)
  starting transfers between devices  22.5 us (30%)
  local copies, waits for them, and re-layouts  9.47 us (13%)
  blocking collectives  7.21 us (10%)
  waiting for transfers between devices  6.25 us (8%)
  between operations  0.87 us (1%)
    pallas_call x10, Pallas kernels, call(): pl.pallas_call(kernel, out_shape=outs, in_specs=[SMEM] + [VMEM] * (len(ar...  15.5 us
    ppermute x4, starting transfers between devices, exchange_rows(): lax.ppermute(s, 'gy', pairs)  12.3 us
    unnamed x27, local copies, waits for them, and re-layouts  9.02 us
    all_to_all x1, blocking collectives, fetch(): lax.all_to_all(request, BRICKS, split_axis=0, concat_axis=0, tiled=True,...  7.21 us
    pallas_call x1, Pallas kernels, mix(): pl.pallas_call(mix_kernel, grid_spec=pltpu.PrefetchScalarGridSpec(num_sca...  6.58 us
    all_to_all x1, starting transfers between devices, fetch(): lax.all_to_all(picked, BRICKS, split_axis=0, concat_axis=0, tiled=True, a...  5.23 us
    ppermute x1, waiting for transfers between devices, fetch(): lax.ppermute(near, 'gy', [(i, (i + rows_gy // 2) % rows_gy) for i in rang...  3.85 us
    ppermute x1, starting transfers between devices, fetch(): lax.ppermute(near, 'gy', [(i, (i + rows_gy // 2) % rows_gy) for i in rang...  2.65 us
  transfers between devices with their start and end apart: 10, of which 4 were waited for; matrix products, arithmetic and copies ran while one was open for 2% of the time, Pallas kernels for 17%

profile of v3, /device:TPU:14, one launch (start us, length us, event | category | flops | bytes accessed | tf_op | source)
XLA Modules:
  0.0 73.4 jit_solution(4373506031555591365)
XLA Ops:
  0.6 0.9 %copy-done.8 = bf16[16,64,128]{2,1,0:T(8,128)(2,1)S(1)} copy-done((bf16[16,64,128]{2,1,0:T(8,128)(2,1)S(1)}, bf16[16,64,128]{2,1,0:T(8,128)(2,1)}, u32[]{:S(2)}) %copy-start.8) | copy-done | bytes 262168
  1.6 0.7 copy-done.9
  2.3 0.7 copy-done.10
  2.9 1.5 %prepare.1 = (bf16[128,8,128]{2,1,0:T(8,128)(2,1)S(1)}, s32[8,1,64]{2,1,0:T(1,128)S(1)}, s32[1,256]{1,0:T(1,128)S(1)}) custom-call(s32[1]{0:T(128)} %bitcast.half_ref, bf16[16,64,128]{2,1,0:T(8,128)(2,1)S(1)} %copy-done.8, s32[1,256]{1,0:T(1,128)S(1)} %bitcast.17, s32[1,256]{1,0:T(1,128)S(1)} %bitcast.18), custom_call_target="tpu_custom_call" | custom-call | tf_op jit(solution)/shard_map/prepare/pallas_call | solution.py:97
  4.4 2.7 %collective-permute-start = (bf16[128,8,128]{2,1,0:T(8,128)(2,1)S(1)}, bf16[128,8,128]{2,1,0:T(8,128)(2,1)S(1)}, u32[]{:S(2)}, u32[]{:S(2)}) collective-permute-start(bf16[128,8,128]{2,1,0:T(8,128)(2,1)S(1)} %get-tuple-element.29.refs_1_), channel_id=1, source_target_pairs={{0,8},{2,10},{4,12},{6,14},{8,0},{10,2},{12,4},{14,6},{1,9},{3,11}... | collective-permute-start | bytes 786440 | tf_op jit(solution)/shard_map/ppermute | solution.py:243
  7.1 7.2 %all_to_all.10.refs_0_ = s32[8,1,64]{2,1,0:T(1,128)S(1)} all-to-all(s32[8,1,64]{2,1,0:T(1,128)S(1)} %get-tuple-element.28), channel_id=1, replica_groups={{0,1,2,3,4,5,6,7},{8,9,10,11,12,13,14,15},{16,17,18,19,20,21,22,23},{24..., dimensions={0} | all-to-all | bytes 4096 | tf_op jit(solution)/shard_map/all_to_all | solution.py:244
  14.3 3.9 %collective-permute-done.refs_2_ = bf16[128,8,128]{2,1,0:T(8,128)(2,1)S(1)} collective-permute-done((bf16[128,8,128]{2,1,0:T(8,128)(2,1)S(1)}, bf16[128,8,128]{2,1,0:T(8,128)(2,1)S(1)}, u32[]{:S(2)}, u32[]{:S(2)}) %collective-permute-start) | collective-permute-done | bytes 262176 | tf_op jit(solution)/shard_map/ppermute | solution.py:243
  18.2 2.2 %pick.1 = bf16[512,8,128]{2,1,0:T(8,128)(2,1)} custom-call(s32[8,1,64]{2,1,0:T(1,128)S(1)} %all_to_all.10.refs_0_, bf16[128,8,128]{2,1,0:T(8,128)(2,1)S(1)} %get-tuple-element.29.refs_1_, bf16[128,8,128]{2,1,0:T(8,128)(2,1)S(1)} %collective-permute-done.refs_2_), custom_call_target="tpu_custom_call" | custom-call | tf_op jit(solution)/shard_map/pick/pallas_call | solution.py:125
  20.3 5.2 %all-to-all-start.1 = ((bf16[8,64,8,128]{3,2,1,0:T(8,128)(2,1)}), bf16[8,64,8,128]{3,2,1,0:T(8,128)(2,1)S(1)}, u32[]{:S(2)}, u32[]{:S(2)}) async-start(bf16[8,64,8,128]{3,2,1,0:T(8,128)(2,1)} %bitcast.7), calls=%async_computation.1 | async-start | bytes 2097152 | tf_op jit(solution)/shard_map/all_to_all | solution.py:246
  25.6 0.6 image.1
  28.2 0.6 collective-permute-start.2
  28.8 5.3 %collective-permute-start.3 = (f32[20,4,128]{2,1,0:T(4,128)S(1)}, f32[20,4,128]{2,1,0:T(4,128)S(1)}, u32[]{:S(2)}, u32[]{:S(2)}) collective-permute-start(f32[20,4,128]{2,1,0:T(4,128)S(1)} %get-tuple-element.33), channel_id=1, source_target_pairs={{2,4},{4,2},{6,8},{8,6},{10,12},{12,10},{3,5},{5,3},{7,9},{9,7},{1... | collective-permute-start | bytes 122888 | tf_op jit(solution)/shard_map/ppermute | solution.py:485
  34.5 1.0 %spread.1.spread_ref = bf16[16,384,128]{2,1,0:T(8,128)(2,1)S(1)} custom-call(f32[2048,8]{1,0:T(8,128)S(1)} %bitcast_select_fusion.mix_ref), custom_call_target="tpu_custom_call" | custom-call | tf_op jit(solution)/shard_map/spread/pallas_call | solution.py:150
  35.5 1.4 %image_own.1 = (f32[32,64,128]{2,1,0:T(8,128)S(1)}, f32[24,64,128]{2,1,0:T(8,128)S(1)}, f32[64,128]{1,0:T(8,128)S(1)}) custom-call(s32[3]{0:T(128)S(1)} %pad_add_fusion.place_ref.refs_0_, f32[1024,128]{1,0:T(8,128)S(1)} %get-tuple-element.34.own_ref, f32[256,128]{1,0:T(8,128)S(1)} %collective-permute-done.1.side_ref), custom_call_target="tpu_custom_call" | custom-call | tf_op jit(solution)/shard_map/image_own/pallas_call | solution.py:263
  36.9 1.0 %copy-done.3 = f32[32,64,128]{2,1,0:T(8,128)} copy-done((f32[32,64,128]{2,1,0:T(8,128)}, f32[32,64,128]{2,1,0:T(8,128)S(1)}, u32[]{:S(2)}) %copy-start.3) | copy-done | bytes 1048600
  37.8 0.9 %copy-done.6 = f32[24,64,128]{2,1,0:T(8,128)} copy-done((f32[24,64,128]{2,1,0:T(8,128)}, f32[24,64,128]{2,1,0:T(8,128)S(1)}, u32[]{:S(2)}) %copy-start.6) | copy-done | bytes 786456
  38.7 0.6 collective-permute-done.2.refs_1_
  39.3 0.6 columns.2
  40.0 3.4 %copy-done = bf16[1,1,1,256,128,128]{5,4,3,2,1,0:T(8,128)(2,1)S(1)} copy-done((bf16[1,1,1,256,128,128]{5,4,3,2,1,0:T(8,128)(2,1)S(1)}, bf16[1,1,1,256,128,128]{5,4,3,2,1,0:T(8,128)(2,1)}, u32[]{:S(2)}) %copy-start) | copy-done | bytes 8388632
  43.4 6.6 %mix.1 = (f32[1024,128]{1,0:T(8,128)}, f32[256,128]{1,0:T(8,128)S(1)}, f32[16,8,128]{2,1,0:T(8,128)S(1)}) custom-call(s32[256]{0:T(256)S(1)} %bitcast.19, s32[3]{0:T(128)S(1)} %pad_add_fusion.place_ref.refs_0_, bf16[512,8,128]{2,1,0:T(8,128)(2,1)S(1)} %bitcast.15, bf16[16,384,128]{2,1,0:T(8,128)(2,1)S(1)} %spread.1.spread_ref, ...), custom_call_target="tpu_custom_call" | custom-call | tf_op jit(solution)/shard_map/mix/pallas_call | solution.py:207
  50.0 1.3 %collective-permute-done.4.refs_2_.side_ref.refs_5_ = f32[256,128]{1,0:T(8,128)S(1)} collective-permute-done((f32[256,128]{1,0:T(8,128)S(1)}, f32[256,128]{1,0:T(8,128)S(1)}, u32[]{:S(2)}, u32[]{:S(2)}) %collective-permute-start.4) | collective-permute-done | bytes 131104 | tf_op jit(solution)/shard_map/ppermute | solution.py:482
  51.3 0.6 rows.3
  51.9 1.8 %collective-permute-start.5 = (f32[20,4,128]{2,1,0:T(4,128)S(1)}, f32[20,4,128]{2,1,0:T(4,128)S(1)}, u32[]{:S(2)}, u32[]{:S(2)}) collective-permute-start(f32[20,4,128]{2,1,0:T(4,128)S(1)} %get-tuple-element.44), channel_id=1, source_target_pairs={{0,2},{2,0},{4,6},{6,4},{8,10},{10,8},{12,14},{14,12},{1,3},{3,1},... | collective-permute-start | bytes 122888 | tf_op jit(solution)/shard_map/ppermute | solution.py:485
  53.7 4.6 %collective-permute-start.6 = (f32[20,4,128]{2,1,0:T(4,128)S(1)}, f32[20,4,128]{2,1,0:T(4,128)S(1)}, u32[]{:S(2)}, u32[]{:S(2)}) collective-permute-start(f32[20,4,128]{2,1,0:T(4,128)S(1)} %get-tuple-element.45), channel_id=1, source_target_pairs={{2,4},{4,2},{6,8},{8,6},{10,12},{12,10},{3,5},{5,3},{7,9},{9,7},{1... | collective-permute-start | bytes 122888 | tf_op jit(solution)/shard_map/ppermute | solution.py:485
  58.3 1.0 %collective-permute-start.8 = (f32[72,128]{1,0:T(8,128)S(1)}, f32[72,128]{1,0:T(8,128)S(1)}, u32[]{:S(2)}, u32[]{:S(2)}) collective-permute-start(f32[72,128]{1,0:T(8,128)S(1)} %get-tuple-element.51), channel_id=1, source_target_pairs={{0,1},{1,0},{2,3},{3,2},{4,5},{5,4},{6,7},{7,6},{8,9},{9,8},{10,11... | collective-permute-start | bytes 110600 | tf_op jit(solution)/shard_map/ppermute | solution.py:522
  59.4 1.0 %copy-done.1 = f32[1024,128]{1,0:T(8,128)S(1)} copy-done((f32[1024,128]{1,0:T(8,128)S(1)}, f32[1024,128]{1,0:T(8,128)}, u32[]{:S(2)}) %copy-start.1) | copy-done | bytes 524312
  60.4 1.3 %own.1 = (f32[48,64,128]{2,1,0:T(8,128)S(1)}, f32[64,128]{1,0:T(8,128)S(1)}) custom-call(s32[3]{0:T(128)S(1)} %pad_add_fusion.place_ref.refs_0_, f32[1024,128]{1,0:T(8,128)S(1)} %copy-done.1, f32[256,128]{1,0:T(8,128)S(1)} %collective-permute-done.4.refs_2_.side_ref.refs_5_, f32[24,64,128]{2,1,0:T(8,128)S(1)} %copy-done.7), custom_call_target="tpu_custom_call" | custom-call | tf_op jit(solution)/shard_map/own/pallas_call | solution.py:263
  61.8 0.6 columns.3
  62.4 1.1 %collective-permute-start.7 = (f32[72,128]{1,0:T(8,128)S(1)}, f32[72,128]{1,0:T(8,128)S(1)}, u32[]{:S(2)}, u32[]{:S(2)}) collective-permute-start(f32[72,128]{1,0:T(8,128)S(1)} %get-tuple-element.50), channel_id=1, source_target_pairs={{0,1},{1,0},{2,3},{3,2},{4,5},{5,4},{6,7},{7,6},{8,9},{9,8},{10,11... | collective-permute-start | bytes 110600 | tf_op jit(solution)/shard_map/ppermute | solution.py:536
  63.6 2.5 %sums.3.refs_2_ = f32[32,64,128]{2,1,0:T(8,128)S(1)} custom-call(s32[3]{0:T(128)S(1)} %pad_add_fusion.place_ref.refs_0_, f32[32,64,128]{2,1,0:T(8,128)S(1)} %copy-done.4, f32[24,8,128]{2,1,0:T(8,128)S(1)} %get-tuple-element.48.refs_3_.refs_2_), custom_call_target="tpu_custom_call" | custom-call | tf_op jit(solution)/shard_map/sums/pallas_call | solution.py:263
  66.1 3.5 %sums.2.refs_1_ = f32[48,64,128]{2,1,0:T(8,128)S(1)} custom-call(s32[3]{0:T(128)S(1)} %pad_add_fusion.place_ref.refs_0_, f32[48,64,128]{2,1,0:T(8,128)S(1)} %get-tuple-element.42.refs_1_, f32[24,8,128]{2,1,0:T(8,128)S(1)} %get-tuple-element.47.refs_2_.refs_6_, f32[24,8,128]{2,1,0:T(8,128)S(1)} %get-tuple-element.48.refs_3_.refs_2_), custom_call_target="tpu_custom_call" | custom-call | tf_op jit(solution)/shard_map/sums/pallas_call | solution.py:263
  69.7 3.8 %force.1 = f32[3,16,64,128]{3,2,1,0:T(8,128)} custom-call(s32[3]{0:T(128)S(1)} %pad_add_fusion.place_ref.refs_0_, f32[48,64,128]{2,1,0:T(8,128)S(1)} %sums.2.refs_1_, f32[32,64,128]{2,1,0:T(8,128)S(1)} %sums.3.refs_2_, bf16[16,64,128]{2,1,0:T(8,128)(2,1)S(1)} %copy-done.5, f32[1024,128]{1,0:T(8,128)S(1)} %copy-done.2, ...), custom_call_target="tpu_custom_call" | custom-call | tf_op jit(solution)/shard_map/force/pallas_call | solution.py:263
  (37 shorter events, 2.4 us)
Async XLA Ops:
  0.6 1.0 %copy-start.8 = (bf16[16,64,128]{2,1,0:T(8,128)(2,1)S(1)}, bf16[16,64,128]{2,1,0:T(8,128)(2,1)}, u32[]{:S(2)}) copy-start(bf16[16,64,128]{2,1,0:T(8,128)(2,1)} %moving_ref.1) | copy-start | bytes 786436
  1.6 0.7 copy-start.9
  2.3 0.7 copy-start.10
  4.4 13.7 %collective-permute-start = (bf16[128,8,128]{2,1,0:T(8,128)(2,1)S(1)}, bf16[128,8,128]{2,1,0:T(8,128)(2,1)S(1)}, u32[]{:S(2)}, u32[]{:S(2)}) collective-permute-start(bf16[128,8,128]{2,1,0:T(8,128)(2,1)S(1)} %get-tuple-element.29.refs_1_), channel_id=1, source_target_pairs={{0,8},{2,10},{4,12},{6,14},{8,0},{10,2},{12,4},{14,6},{1,9},{3,11}... | collective-permute-start | bytes 786440 | tf_op jit(solution)/shard_map/ppermute | solution.py:243
  14.3 11.3 %copy-start.5 = (bf16[16,64,128]{2,1,0:T(8,128)(2,1)S(1)}, bf16[16,64,128]{2,1,0:T(8,128)(2,1)}, u32[]{:S(2)}) copy-start(bf16[16,64,128]{2,1,0:T(8,128)(2,1)} %refs_3_.1) | copy-start | bytes 786436
  20.3 6.0 %copy-start.12 = (s32[1,1,1,128]{3,2,1,0:T(1,128)S(1)}, s32[1,1,1,128]{3,2,1,0:T(1,128)}, u32[]{:S(2)}) copy-start(s32[1,1,1,128]{3,2,1,0:T(1,128)} %param.11) | copy-start | bytes 1540
  20.3 6.5 %copy-start.11 = (f32[1,1,1,256,8,8]{3,5,4,2,1,0:T(8,128)S(1)}, f32[1,1,1,256,8,8]{3,5,4,2,1,0:T(8,128)}, u32[]{:S(2)}) copy-start(f32[1,1,1,256,8,8]{3,5,4,2,1,0:T(8,128)} %param.13) | copy-start | bytes 196612
  20.3 19.7 %all-to-all-start.1 = ((bf16[8,64,8,128]{3,2,1,0:T(8,128)(2,1)}), bf16[8,64,8,128]{3,2,1,0:T(8,128)(2,1)S(1)}, u32[]{:S(2)}, u32[]{:S(2)}) async-start(bf16[8,64,8,128]{3,2,1,0:T(8,128)(2,1)} %bitcast.7), calls=%async_computation.1 | async-start | bytes 2097152 | tf_op jit(solution)/shard_map/all_to_all | solution.py:246
  26.2 1.4 %collective-permute-start.1 = (f32[256,128]{1,0:T(8,128)S(1)}, f32[256,128]{1,0:T(8,128)S(1)}, u32[]{:S(2)}, u32[]{:S(2)}) collective-permute-start(f32[256,128]{1,0:T(8,128)S(1)} %get-tuple-element.31), channel_id=1, source_target_pairs={{0,16},{16,0},{1,17},{17,1},{2,18},{18,2},{3,19},{19,3},{4,20},{20... | collective-permute-start | bytes 393224 | tf_op jit(solution)/shard_map/ppermute | solution.py:482
  28.2 11.1 %collective-permute-start.2 = (f32[20,4,128]{2,1,0:T(4,128)S(1)}, f32[20,4,128]{2,1,0:T(4,128)S(1)}, u32[]{:S(2)}, u32[]{:S(2)}) collective-permute-start(f32[20,4,128]{2,1,0:T(4,128)S(1)} %get-tuple-element.32), channel_id=1, source_target_pairs={{0,2},{2,0},{4,6},{6,4},{8,10},{10,8},{12,14},{14,12},{1,3},{3,1},... | collective-permute-start | bytes 122888 | tf_op jit(solution)/shard_map/ppermute | solution.py:485
  28.8 10.5 %collective-permute-start.3 = (f32[20,4,128]{2,1,0:T(4,128)S(1)}, f32[20,4,128]{2,1,0:T(4,128)S(1)}, u32[]{:S(2)}, u32[]{:S(2)}) collective-permute-start(f32[20,4,128]{2,1,0:T(4,128)S(1)} %get-tuple-element.33), channel_id=1, source_target_pairs={{2,4},{4,2},{6,8},{8,6},{10,12},{12,10},{3,5},{5,3},{7,9},{9,7},{1... | collective-permute-start | bytes 122888 | tf_op jit(solution)/shard_map/ppermute | solution.py:485
  36.8 1.0 %copy-start.3 = (f32[32,64,128]{2,1,0:T(8,128)}, f32[32,64,128]{2,1,0:T(8,128)S(1)}, u32[]{:S(2)}) copy-start(f32[32,64,128]{2,1,0:T(8,128)S(1)} %get-tuple-element.49.refs_1_) | copy-start | bytes 3145732
  37.8 0.9 %copy-start.6 = (f32[24,64,128]{2,1,0:T(8,128)}, f32[24,64,128]{2,1,0:T(8,128)S(1)}, u32[]{:S(2)}) copy-start(f32[24,64,128]{2,1,0:T(8,128)S(1)} %get-tuple-element.41.refs_3_) | copy-start | bytes 2359300
  40.0 3.4 %copy-start = (bf16[1,1,1,256,128,128]{5,4,3,2,1,0:T(8,128)(2,1)S(1)}, bf16[1,1,1,256,128,128]{5,4,3,2,1,0:T(8,128)(2,1)}, u32[]{:S(2)}) copy-start(bf16[1,1,1,256,128,128]{5,4,3,2,1,0:T(8,128)(2,1)} %param.12) | copy-start | bytes 25165828
  43.4 16.0 %copy-start.7 = (f32[24,64,128]{2,1,0:T(8,128)S(1)}, f32[24,64,128]{2,1,0:T(8,128)}, u32[]{:S(2)}) copy-start(f32[24,64,128]{2,1,0:T(8,128)} %copy-done.6) | copy-start | bytes 2359300
  43.4 20.2 %copy-start.4 = (f32[32,64,128]{2,1,0:T(8,128)S(1)}, f32[32,64,128]{2,1,0:T(8,128)}, u32[]{:S(2)}) copy-start(f32[32,64,128]{2,1,0:T(8,128)} %copy-done.3) | copy-start | bytes 3145732
  50.0 1.3 %collective-permute-start.4 = (f32[256,128]{1,0:T(8,128)S(1)}, f32[256,128]{1,0:T(8,128)S(1)}, u32[]{:S(2)}, u32[]{:S(2)}) collective-permute-start(f32[256,128]{1,0:T(8,128)S(1)} %get-tuple-element.40), channel_id=1, source_target_pairs={{0,16},{16,0},{1,17},{17,1},{2,18},{18,2},{3,19},{19,3},{4,20},{20... | collective-permute-start | bytes 393224 | tf_op jit(solution)/shard_map/ppermute | solution.py:482
  51.9 9.9 %collective-permute-start.5 = (f32[20,4,128]{2,1,0:T(4,128)S(1)}, f32[20,4,128]{2,1,0:T(4,128)S(1)}, u32[]{:S(2)}, u32[]{:S(2)}) collective-permute-start(f32[20,4,128]{2,1,0:T(4,128)S(1)} %get-tuple-element.44), channel_id=1, source_target_pairs={{0,2},{2,0},{4,6},{6,4},{8,10},{10,8},{12,14},{14,12},{1,3},{3,1},... | collective-permute-start | bytes 122888 | tf_op jit(solution)/shard_map/ppermute | solution.py:485
  53.7 8.1 %collective-permute-start.6 = (f32[20,4,128]{2,1,0:T(4,128)S(1)}, f32[20,4,128]{2,1,0:T(4,128)S(1)}, u32[]{:S(2)}, u32[]{:S(2)}) collective-permute-start(f32[20,4,128]{2,1,0:T(4,128)S(1)} %get-tuple-element.45), channel_id=1, source_target_pairs={{2,4},{4,2},{6,8},{8,6},{10,12},{12,10},{3,5},{5,3},{7,9},{9,7},{1... | collective-permute-start | bytes 122888 | tf_op jit(solution)/shard_map/ppermute | solution.py:485
  58.3 11.3 %collective-permute-start.8 = (f32[72,128]{1,0:T(8,128)S(1)}, f32[72,128]{1,0:T(8,128)S(1)}, u32[]{:S(2)}, u32[]{:S(2)}) collective-permute-start(f32[72,128]{1,0:T(8,128)S(1)} %get-tuple-element.51), channel_id=1, source_target_pairs={{0,1},{1,0},{2,3},{3,2},{4,5},{5,4},{6,7},{7,6},{8,9},{9,8},{10,11... | collective-permute-start | bytes 110600 | tf_op jit(solution)/shard_map/ppermute | solution.py:522
  59.4 1.0 %copy-start.1 = (f32[1024,128]{1,0:T(8,128)S(1)}, f32[1024,128]{1,0:T(8,128)}, u32[]{:S(2)}) copy-start(f32[1024,128]{1,0:T(8,128)} %get-tuple-element.39.refs_1_.refs_4_) | copy-start | bytes 1572868
  62.4 7.2 %collective-permute-start.7 = (f32[72,128]{1,0:T(8,128)S(1)}, f32[72,128]{1,0:T(8,128)S(1)}, u32[]{:S(2)}, u32[]{:S(2)}) collective-permute-start(f32[72,128]{1,0:T(8,128)S(1)} %get-tuple-element.50), channel_id=1, source_target_pairs={{0,1},{1,0},{2,3},{3,2},{4,5},{5,4},{6,7},{7,6},{8,9},{9,8},{10,11... | collective-permute-start | bytes 110600 | tf_op jit(solution)/shard_map/ppermute | solution.py:536
  66.1 3.6 %copy-start.2 = (f32[1024,128]{1,0:T(8,128)S(1)}, f32[1024,128]{1,0:T(8,128)}, u32[]{:S(2)}) copy-start(f32[1024,128]{1,0:T(8,128)} %get-tuple-element.39.refs_1_.refs_4_) | copy-start | bytes 1572868

commit v4 on v3

v4 whole, which is shorter than its diff:
```python
import jax
import jax.numpy as jnp
from jax import lax
from jax.experimental import pallas as pl
from jax.experimental.pallas import tpu as pltpu
from jax.sharding import PartitionSpec as P


VZ = 8
VY = 8
VX = 16
NBZ = 2
NBY = 8
NBX = 8
SOURCES = 2
RAD = 4
BV = VY * VX
BLOCKS = NBZ * NBY * NBX
SLOTS = BLOCKS * SOURCES
NZ = NBZ * VZ
NY = NBY * VY
NX = NBX * VX
GROUPS = NBZ * NBY
PER = NBX * SOURCES
ROWS = PER * VZ
BRICKS = ("gy", "gx")
F32 = jnp.float32
LIMIT = 12 * 2**20
WIDE = 20 * 2**20
BF16 = jnp.bfloat16

VMEM = pl.BlockSpec(memory_space=pltpu.VMEM)
SMEM = pl.BlockSpec(memory_space=pltpu.SMEM)


OUTER = (
    jax.ShapeDtypeStruct((NZ * NY, NX), F32),
    jax.ShapeDtypeStruct((RAD * NY, NX), F32),
    jax.ShapeDtypeStruct((NZ, VY, NX), F32),
)


def iota(shape, dim):
    return lax.broadcasted_iota(jnp.int32, shape, dim)


def pieces(value, count):
    parts = []
    for _ in range(count - 1):
        part = value.astype(BF16)
        parts.append(part)
        value = value - part.astype(F32)
    parts.append(value.astype(BF16))
    return parts


def swap_chunks(rows):
    chunk = iota((VZ, BV), 1) // VX
    for k in (1, 2, 4):
        low = (chunk & k) == 0
        out = list(rows)
        for b in range(8):
            if b & k == 0:
                first, second = rows[b], rows[b + k]
                out[b] = jnp.where(low, first, pltpu.roll(second, k * VX, 1))
                out[b + k] = jnp.where(low, pltpu.roll(first, BV - k * VX, 1), second)
        rows = out
    return rows


def prepare_kernel(
    half_ref, place_ref, moving_hbm, fixed_hbm, owner_hbm, ident_hbm,
    blocks_ref, request_ref, flat_ref, image_ref, side_ref, face_ref,
    moving_ref, fixed_ref, owner_ref, ident_ref, wide, sems,
):
    pairs = [(owner_hbm, owner_ref), (ident_hbm, ident_ref), (moving_hbm, moving_ref), (fixed_hbm, fixed_ref)]
    copies = [pltpu.make_async_copy(source, target, sems.at[i]) for i, (source, target) in enumerate(pairs)]
    for copy in copies:
        copy.start()
    holders, _, width = request_ref.shape
    capacity = width // 2
    half = half_ref[0]
    copies[0].wait()
    copies[1].wait()
    owner = owner_ref[...]
    ident = ident_ref[...].astype(F32)
    groups = 2 * holders
    named = jnp.where(owner == iota((groups, SLOTS), 0), 1.0, 0.0)
    earlier = jnp.where(iota((SLOTS, SLOTS), 0) < iota((SLOTS, SLOTS), 1), 1.0, 0.0).astype(BF16)
    before = jnp.dot(named.astype(BF16), earlier, preferred_element_type=F32)
    rank = jnp.sum(named * before, axis=0, keepdims=True).astype(jnp.int32)
    upper = jnp.where(owner >= holders, 1, 0)
    holder = owner - upper * holders
    place = jnp.where(upper == half, 0, capacity) + rank
    flat_ref[...] = holder * width + place
    wanted = jnp.where(holder == iota((holders, SLOTS), 0), ident, 0.0).astype(BF16)
    at = jnp.where(place == iota((width, SLOTS), 0), 1.0, 0.0).astype(BF16)
    request = lax.dot_general(wanted, at, (((1,), (1,)), ((), ())), preferred_element_type=F32).astype(jnp.int32)
    for h in range(holders):
        request_ref[h] = request[h : h + 1, :]
    copies[2].wait()
    for z in range(NZ):
        wide[z * NY : (z + 1) * NY, :] = moving_ref[z].astype(F32)

    def group(g, _):
        start = (g // NBY) * (VZ * NY) + (g % NBY) * VY
        rows = [wide[pl.ds(start + y, VZ, stride=NY), :] for y in range(VY)]
        for x, block in enumerate(swap_chunks(rows)):
            blocks_ref[g * NBX + x] = block.astype(BF16)
        return 0

    lax.fori_loop(0, GROUPS, group, 0, unroll=4)
    copies[3].wait()
    for z in range(NZ):
        image_ref[z * NY : (z + 1) * NY, :] = fixed_ref[z].astype(F32)
    outer(place_ref, image_ref, side_ref, face_ref)


def prepare(half, place, moving, fixed, owner, ident, groups, capacity):
    holders = groups // 2
    hbm = pl.BlockSpec(memory_space=pltpu.HBM)
    return pl.pallas_call(
        prepare_kernel,
        out_shape=(
            jax.ShapeDtypeStruct((BLOCKS, VZ, BV), BF16),
            jax.ShapeDtypeStruct((holders, 1, 2 * capacity), jnp.int32),
            jax.ShapeDtypeStruct((1, SLOTS), jnp.int32),
        )
        + OUTER,
        in_specs=[SMEM, SMEM, hbm, hbm, hbm, hbm],
        out_specs=(VMEM,) * 6,
        scratch_shapes=[
            pltpu.VMEM((NZ, NY, NX), BF16),
            pltpu.VMEM((NZ, NY, NX), BF16),
            pltpu.VMEM((1, SLOTS), jnp.int32),
            pltpu.VMEM((1, SLOTS), jnp.int32),
            pltpu.VMEM((NZ * NY, NX), F32),
            pltpu.SemaphoreType.DMA((4,)),
        ],
        compiler_params=pltpu.CompilerParams(vmem_limit_bytes=LIMIT),
        name="prepare",
    )(half, place, *[pltpu.with_memory_space_constraint(a, pltpu.HBM) for a in (moving, fixed, owner, ident)])


def pick_kernel(capacity, request_ref, near_ref, far_ref, out_ref):
    width = 2 * capacity

    def holder(h, _):
        for k in range(width):
            source = near_ref if k < capacity else far_ref
            out_ref[h * width + k] = source[request_ref[h, 0, k]]
        return 0

    lax.fori_loop(0, out_ref.shape[0] // width, holder, 0)


def pick(request, near, far, capacity):
    return pl.pallas_call(
        lambda *refs: pick_kernel(capacity, *refs),
        out_shape=jax.ShapeDtypeStruct((request.size, VZ, BV), BF16),
        in_specs=[SMEM, VMEM, VMEM],
        out_specs=VMEM,
        compiler_params=pltpu.CompilerParams(vmem_limit_bytes=LIMIT),
        name="pick",
    )(request, near, far)


def spread_kernel(mix_ref, out_ref):
    pick_lane = jnp.where(iota((VZ, ROWS), 1) % VZ == iota((VZ, ROWS), 0), 1.0, 0.0).astype(BF16)
    same = iota((ROWS, ROWS), 0) // VZ == iota((ROWS, ROWS), 1) // VZ

    def group(g, _):
        weights = mix_ref[pl.ds(pl.multiple_of(g * ROWS, ROWS), ROWS), :]
        for k, part in enumerate(pieces(weights, 3)):
            tiled = jnp.dot(part, pick_lane, preferred_element_type=F32)
            out_ref[g, k * ROWS : (k + 1) * ROWS, :] = jnp.where(same, tiled, 0.0).astype(BF16)
        return 0

    lax.fori_loop(0, GROUPS, group, 0, unroll=4)


def spread(mix_z):
    return pl.pallas_call(
        spread_kernel,
        out_shape=jax.ShapeDtypeStruct((GROUPS, 3 * ROWS, ROWS), BF16),
        in_specs=[VMEM],
        out_specs=VMEM,
        compiler_params=pltpu.CompilerParams(vmem_limit_bytes=LIMIT),
        name="spread",
    )(mix_z)


STEP = 4


def mix_kernel(
    place_ref, flat_ref, received_ref, spread_ref, mix_hbm, warped_ref, side_ref, face_ref, weights_ref, sems
):
    share = STEP * PER

    def weights(step):
        rows = pl.ds(step * share, share)
        return pltpu.make_async_copy(mix_hbm.at[rows], weights_ref.at[rows], sems.at[step])

    for step in range(GROUPS // STEP):
        weights(step).start()

    def across_planes(g):
        source = jnp.concatenate([received_ref[flat_ref[g * PER + i]].astype(F32) for i in range(PER)], 0)
        parts = jnp.dot(spread_ref[g], source.astype(BF16), preferred_element_type=F32)
        mixed = parts[:ROWS] + parts[ROWS : 2 * ROWS] + parts[2 * ROWS :]
        high = mixed.astype(BF16).astype(F32)
        return high, mixed - high

    def in_plane(g, high, low):
        rows = []
        for j in range(NBX):
            a = slice(2 * j * VZ, (2 * j + 1) * VZ)
            b = slice((2 * j + 1) * VZ, (2 * j + 2) * VZ)
            left = jnp.concatenate(
                [jnp.concatenate([high[a], high[b]], 1), jnp.concatenate([low[a], low[b]], 1)], 0
            ).astype(BF16)
            right = weights_ref[pl.ds(g * PER + 2 * j, 2)].reshape(2 * BV, BV)
            both = jnp.dot(left, right, preferred_element_type=F32)
            rows.append(both[:VZ] + both[VZ:])
        return rows

    def place_rows(g, rows):
        start = (g // NBY) * (VZ * NY) + (g % NBY) * VY
        for y, row in enumerate(swap_chunks(rows)):
            warped_ref[pl.ds(start + y, VZ, stride=NY), :] = row

    def some(step, _):
        weights(step).wait()
        first = step * STEP
        mixed, done = {}, {}
        for t in range(STEP + 2):
            if t < STEP:
                mixed[t] = across_planes(first + t)
            if 0 <= t - 1 < STEP:
                done[t - 1] = in_plane(first + t - 1, *mixed.pop(t - 1))
            if 0 <= t - 2:
                place_rows(first + t - 2, done.pop(t - 2))
        return 0

    lax.fori_loop(0, GROUPS // STEP, some, 0)
    outer(place_ref, warped_ref, side_ref, face_ref)


def outer(place_ref, own_ref, side_ref, face_ref):
    first = jnp.where(place_ref[0] == 0, (NZ - RAD) * NY, 0)
    side_ref[...] = own_ref[pl.ds(pl.multiple_of(first, NY), RAD * NY), :]
    low = iota((VY, NX), 0) < RAD
    for z in range(NZ):
        face_ref[z] = jnp.where(low, own_ref[z * NY : z * NY + VY, :], own_ref[(z + 1) * NY - VY : (z + 1) * NY, :])


def mix(flat, place, received, spread_z, mix_yx):
    return pl.pallas_call(
        mix_kernel,
        out_shape=OUTER,
        in_specs=[SMEM, SMEM, VMEM, VMEM, pl.BlockSpec(memory_space=pltpu.HBM)],
        out_specs=(VMEM,) * 3,
        scratch_shapes=[
            pltpu.VMEM((SLOTS, BV, BV), BF16),
            pltpu.SemaphoreType.DMA((GROUPS // STEP,)),
        ],
        compiler_params=pltpu.CompilerParams(vmem_limit_bytes=WIDE),
        name="mix",
    )(place, flat, received, spread_z, pltpu.with_memory_space_constraint(mix_yx, pltpu.HBM))


def halves_of_gy():
    groups = lax.axis_size("gy") * lax.axis_size("gx")
    holders = groups // 2
    return groups, max(2, 2 * SLOTS // groups), [list(range(holders)), list(range(holders, groups))]


def exchange_in_half(array):
    _, _, halves = halves_of_gy()
    return lax.all_to_all(array, BRICKS, split_axis=0, concat_axis=0, tiled=True, axis_index_groups=halves)


def ask(place, moving, fixed, owners, block_ids):
    rows_gy = lax.axis_size("gy")
    groups, capacity, _ = halves_of_gy()
    half = (lax.axis_index("gy") >= rows_gy // 2).astype(jnp.int32).reshape(1)
    near, request, flat, *image = prepare(
        half, place, moving, fixed, owners.reshape(1, SLOTS), block_ids.reshape(1, SLOTS), groups, capacity
    )
    far = lax.ppermute(near, "gy", [(i, (i + rows_gy // 2) % rows_gy) for i in range(rows_gy)])
    request = exchange_in_half(request)
    return request, near, far, flat.reshape(-1), image


def answer(request, near, far):
    groups, capacity, _ = halves_of_gy()
    picked = pick(request, near, far, capacity).reshape(groups // 2, 2 * capacity, VZ, BV)
    return exchange_in_half(picked).reshape(groups * capacity, VZ, BV)


def spread_weights(counts, mix_z):
    slot_pos = jnp.arange(SLOTS, dtype=jnp.int32)
    keep = slot_pos % SOURCES < jnp.repeat(counts.reshape(-1), SOURCES)
    return spread(jnp.where(keep[:, None, None], mix_z.reshape(SLOTS, VZ, VZ), 0.0).reshape(SLOTS * VZ, VZ))


REACH = 2 * RAD
EZ = NZ + REACH
EY = NY + REACH
COUNT = float((REACH + 1) ** 3)


def call(kernel, outs, *args, scratch=()):
    return pl.pallas_call(
        kernel,
        out_shape=outs,
        in_specs=[SMEM] + [VMEM] * (len(args) - 1),
        out_specs=jax.tree.map(lambda _: VMEM, outs),
        scratch_shapes=scratch,
        compiler_params=pltpu.CompilerParams(vmem_limit_bytes=LIMIT),
    )(*args)


def array(*shape):
    return jax.ShapeDtypeStruct(shape, F32)


def rows_kernel(packed_count, place_ref, face_ref, side_ref, *refs):
    packed, outs = refs[:packed_count], refs[packed_count:]
    even = place_ref[1] == 0
    low = iota((VY, NX), 0) < RAD
    faces = [face_ref[p] for p in range(NZ)]
    for ref, at in [(side_ref, p * NY) for p in range(RAD)] + [(ref, 0) for ref in packed]:
        faces.append(jnp.where(low, ref[at : at + VY, :], ref[at + NY - VY : at + NY, :]))
    for p, face in enumerate(faces):
        outs[0][p] = jnp.where(even, face[RAD:], face[:RAD])
        if len(outs) == 2:
            outs[1][p] = jnp.where(even, face[:RAD], face[RAD:])


def extended_planes(place_ref, own, side):
    low = place_ref[0] == 0
    empty = jnp.zeros_like(side[0])
    before = [jnp.where(low, empty, s) for s in side]
    after = [jnp.where(low, s, empty) for s in side]
    return before + own + after


def pack(place_ref, planes, k):
    even = place_ref[2] == 0
    lift = jnp.where(even, RAD, 0) if k == 0 else jnp.where(even, 0, RAD)
    slot = iota((VY, NX), 1) // RAD
    packed = jnp.zeros((VY, NX), F32)
    for p, rows in enumerate(planes):
        packed = jnp.where(slot == p, pltpu.roll(rows, lift + p * RAD, 1), packed)
    return packed


def window(parts, length):
    two = [parts[i] + parts[i + 1] for i in range(len(parts) - 1)]
    four = [two[i] + two[i + 2] for i in range(len(two) - 2)]
    eight = [four[i] + four[i + 4] for i in range(len(four) - 4)]
    return [eight[i] + parts[i + 8] for i in range(length)]


def pack_kernel(place_ref, own_ref, side_ref, *columns):
    def rows_of(q, _):
        at = pl.multiple_of(q * VY, VY)
        planes = own_planes(place_ref, own_ref, side_ref, at)
        for k, column in enumerate(columns):
            column[pl.ds(at, VY), :] = pack(place_ref, planes, k)
        return 0

    lax.fori_loop(0, NBY, rows_of, 0, unroll=2)


def own_planes(place_ref, own_ref, side_ref, at):
    own = [own_ref[pl.ds(pl.multiple_of(z * NY + at, VY), VY), :] for z in range(NZ)]
    side = [side_ref[pl.ds(pl.multiple_of(z * NY + at, VY), VY), :] for z in range(RAD)]
    return extended_planes(place_ref, own, side)


def own_kernel(with_image, place_ref, own_ref, side_ref, *refs):
    image_ref, sums_ref, *columns = refs
    if with_image:
        out_ref = columns.pop(0)
        for z in range(NZ):
            out_ref[z] = own_ref[z * NY : (z + 1) * NY, :]

    def rows_of(q, _):
        at = pl.multiple_of(q * VY, VY)
        rows = pl.ds(at, VY)
        planes = own_planes(place_ref, own_ref, side_ref, at)
        for k, column in enumerate(columns):
            column[rows, :] = pack(place_ref, planes, k)
        fields = [planes, [v * v for v in planes]]
        if with_image:
            fields.append([image_ref[p, rows, :] * v for p, v in enumerate(planes)])
        else:
            for p, v in enumerate(planes):
                image_ref[p, rows, :] = v
        for f, parts in enumerate(fields):
            for z, total in enumerate(window(parts, NZ)):
                sums_ref[f * NZ + z, rows, :] = total
        return 0

    lax.fori_loop(0, NBY, rows_of, 0)


def columns_kernel(y_count, x_count, place_ref, *refs):
    halos, packed, (rows_ref, *columns) = refs[:y_count], refs[y_count : y_count + x_count], refs[y_count + x_count :]
    even = place_ref[1] == 0
    planes = []
    for p in range(halos[0].shape[0]):
        first = halos[0][p]
        second = halos[1][p] if y_count == 2 else jnp.zeros_like(first)
        planes.append(jnp.concatenate([jnp.where(even, first, second), jnp.where(even, second, first)], 0))
    come = planes[NZ + RAD :]
    planes = extended_planes(place_ref, planes[:NZ], planes[NZ : NZ + RAD])
    for p, rows in enumerate(planes):
        rows_ref[p] = rows
    for k in range(x_count):
        columns[k][:NY] = packed[k][...]
        columns[k][NY:] = come[k] if come else pack(place_ref, planes, k)


def window_rows(value):
    two = value + pltpu.roll(value, EY - 1, 0)
    four = two + pltpu.roll(two, EY - 2, 0)
    return (value + pltpu.roll(four, RAD, 0) + pltpu.roll(four, EY - 1, 0))[:NY]


def split_dot(value, table):
    total = None
    for part in pieces(value, 3):
        term = jnp.dot(part, table, preferred_element_type=F32)
        total = term if total is None else total + term
    return total


def edge_table(right):
    row, col = iota((NX, NX), 0), iota((NX, NX), 1)
    plane, i = row // RAD, row % RAD
    z, j = col // RAD, col % RAD
    reach = jnp.where(right, j - i, i - j)
    inside = (plane >= z) & (plane <= z + REACH) & (z < NZ) & (plane < EZ) & (reach >= 0)
    return jnp.where(inside, 1.0, 0.0).astype(BF16)


def at_edge(right, rows):
    return iota((rows, NX), 1) // RAD == jnp.where(right, NX // RAD - 1, 0)


def edge_part(sums, z, right, mask):
    base = jnp.where(right, NX - RAD, 0)
    return jnp.where(mask, pltpu.roll(sums, lax.rem(base + NX - RAD * z, NX), 1), 0.0)


def side_is_right(place_ref, k):
    even = place_ref[2] == 0
    return even if k == 0 else jnp.logical_not(even)


def near_columns():
    return jnp.where(jnp.abs(iota((NX, NX), 0) - iota((NX, NX), 1)) <= RAD, 1.0, 0.0).astype(BF16)


def brick_sums(count, load, out_ref, line, pair, four):
    near = near_columns()
    lanes = line.shape[0]

    def some(step, _):
        for k in range(lanes):
            i = step * lanes + k
            own, halo = load(i)
            line[k, :RAD] = halo[RAD:]
            line[k, RAD : RAD + NY] = own
            line[k, RAD + NY : EY] = halo[:RAD]
            pair[k, :EY] = line[k, :EY] + line[k, 1 : EY + 1]
            four[k, :EY] = pair[k, :EY] + pair[k, 2 : EY + 2]
            total = four[k, :NY] + four[k, RAD : RAD + NY] + line[k, REACH : REACH + NY]
            out_ref[i] = split_dot(total, near)
        return 0

    lax.fori_loop(0, count // lanes, some, 0)


LINES = (pltpu.VMEM((4, EY + VY, NX), F32),) * 3


def image_sums_kernel(place_ref, own_sums_ref, out_ref, *lines):
    brick_sums(2 * NZ, lambda i: (own_sums_ref[i], jnp.zeros((VY, NX), F32)), out_ref, *lines)


def halo_sums(fields, outer_sums):
    for f, parts in enumerate(fields):
        for z, total in enumerate(window(parts, NZ)):
            outer_sums[f * NZ + z] = total


def warped_sums_kernel(place_ref, own_sums_ref, rows_ref, image_rows_ref, out_ref, outer_sums, *lines):
    w = [rows_ref[p] for p in range(EZ)]
    halo_sums([w, [v * v for v in w], [image_rows_ref[p] * v for p, v in enumerate(w)]], outer_sums)
    brick_sums(3 * NZ, lambda i: (own_sums_ref[i], outer_sums[i]), out_ref, *lines)


def halo_part(total):
    row = iota(total.shape, 0) % VY
    size = total.shape[0]
    turned = jnp.where(row < RAD, pltpu.roll(total, size - RAD, 0), pltpu.roll(total, RAD, 0))
    for k in (1, 2):
        up, down = pltpu.roll(turned, size - k, 0), pltpu.roll(turned, k, 0)
        turned = turned + jnp.where(row < RAD - k, up, jnp.where(row >= RAD + k, down, 0.0))
    return turned


def add_edges(x_count, place_ref, z, box, edges, stride, start):
    rows = box[0].shape[0]
    for k in range(x_count):
        right = side_is_right(place_ref, k)
        mask = at_edge(right, rows)
        box = [
            total + edge_part(edges[stride * k + i, start : start + rows, :], z, right, mask)
            for i, total in enumerate(box)
        ]
    return box


def image_box_kernel(x_count, place_ref, sums_ref, image_ref, rows_ref, *refs):
    halos, (out_ref, edges, outer_sums) = refs[:x_count], refs[x_count:]
    for k in range(x_count):
        table = edge_table(side_is_right(place_ref, k))
        f = halos[k][...]
        for i, field in enumerate([f, f * f]):
            edges[2 * k + i] = split_dot(window_rows(field), table)
    f = [rows_ref[p] for p in range(EZ)]
    halo_sums([f, [v * v for v in f]], outer_sums)
    outer = split_dot(halo_part(outer_sums[...].reshape(2 * NZ * VY, NX)), near_columns())
    outer_sums[...] = outer.reshape(2 * NZ, VY, NX)
    first = iota((VY, NX), 0) < RAD
    scale = 1.0 / COUNT

    def plane(z, _):
        box = []
        for f in range(2):
            total, rows = sums_ref[f * NZ + z], outer_sums[f * NZ + z]
            box.append(
                jnp.concatenate(
                    [
                        total[:VY] + jnp.where(first, rows, 0.0),
                        total[VY : NY - VY],
                        total[NY - VY :] + jnp.where(first, 0.0, rows),
                    ],
                    0,
                )
            )
        box = add_edges(x_count, place_ref, z, box, edges, 2, 0)
        mean = box[0] * scale
        out_ref[z] = mean
        out_ref[NZ + z] = image_ref[pl.ds(pl.multiple_of(z * NY, NY), NY), :] - mean
        out_ref[2 * NZ + z] = 1.0 / (box[1] * scale - mean * mean + 1e-5)
        return 0

    lax.fori_loop(0, NZ, plane, 0, unroll=2)


HALF = NY // 2


def force_kernel(x_count, place_ref, sums_ref, image_ref, own_ref, side_ref, rows_ref, *refs):
    warped_halos, fixed_halos = refs[:x_count], refs[x_count : 2 * x_count]
    force_ref, edges = refs[2 * x_count], refs[2 * x_count + 1]
    for k in range(x_count):
        table = edge_table(side_is_right(place_ref, k))
        w, f = warped_halos[k][...], fixed_halos[k][...]
        for i, field in enumerate([w, w * w, f * w]):
            edges[4 * k + i] = split_dot(window_rows(field), table)
        edges[4 * k + 3] = w[:NY]
    scale = 1.0 / COUNT
    lane = iota((HALF, NX), 1)
    low = place_ref[0] == 0

    def plane(z, _):
        at = pl.multiple_of(z * NY, NY)
        tall = jnp.concatenate([own_ref[pl.ds(at, NY), :], rows_ref[z + RAD]], 0)
        force_ref[1, z] = (pltpu.roll(tall, EY - 1, 0) - pltpu.roll(tall, 1, 0))[:NY]
        above = pl.multiple_of(jnp.minimum(at + NY, (NZ - 1) * NY), NY)
        below = pl.multiple_of(jnp.maximum(at - NY, 0), NY)
        for h in range(0, NY, HALF):
            part = slice(h, h + HALF)
            own = own_ref[pl.ds(at + h, HALF), :]
            box = [sums_ref[f * NZ + z, part, :] for f in range(3)]
            box = add_edges(x_count, place_ref, z, box, edges, 4, h)
            mean_w = box[0] * scale
            cov = box[2] * scale - image_ref[z, part, :] * mean_w
            ratio = cov / (box[1] * scale - mean_w * mean_w + 1e-5)
            half = (ratio * image_ref[2 * NZ + z, part, :]) * (image_ref[NZ + z, part, :] - ratio * (own - mean_w))
            up, down = own_ref[pl.ds(above + h, HALF), :], own_ref[pl.ds(below + h, HALF), :]
            up = jnp.where(z == NZ - 1, jnp.where(low, side_ref[part, :], 0.0), up)
            down = jnp.where(z == 0, jnp.where(low, 0.0, side_ref[(RAD - 1) * NY + h : (RAD - 1) * NY + h + HALF, :]), down)
            force_ref[0, z, part, :] = half * (up - down)
            force_ref[1, z, part, :] = half * force_ref[1, z, part, :]
            after = jnp.where(lane == NX - 1, 0.0, pltpu.roll(own, NX - 1, 1))
            before = jnp.where(lane == 0, 0.0, pltpu.roll(own, 1, 1))
            for k in range(x_count):
                right = side_is_right(place_ref, k)
                turn = jnp.where(right, NX - 1, NX + 1 - RAD) + NX - RAD * (z + RAD)
                halo = pltpu.roll(edges[4 * k + 3, part, :], lax.rem(turn, NX), 1)
                after = jnp.where(lane == jnp.where(right, NX - 1, -1), halo, after)
                before = jnp.where(lane == jnp.where(right, -1, 0), halo, before)
            force_ref[2, z, part, :] = half * (after - before)
        return 0

    lax.fori_loop(0, NZ, plane, 0)


def pairings(size):
    even = [(i, i ^ 1) for i in range(size) if (i ^ 1) < size]
    odd = [(i, i + 1 if i % 2 else i - 1) for i in range(1, size)]
    odd = [(i, j) for i, j in odd if j < size]
    return [pairs for pairs in (even, odd) if pairs]


def exchange_planes(side):
    return lax.ppermute(side, "gz", pairings(lax.axis_size("gz"))[0])


def rows_to_send(place, face, side, *packed):
    count = len(pairings(lax.axis_size("gy")))
    return call(
        lambda *refs: rows_kernel(len(packed), *refs),
        (array(NZ + RAD + len(packed), RAD, NX),) * count,
        place,
        face,
        side,
        *packed,
    )


def exchange_rows(sent):
    along = pairings(lax.axis_size("gy"))
    return [lax.ppermute(s, "gy", pairs) for s, pairs in reversed(list(zip(sent, along)))][::-1]


def exchange_columns(columns):
    along = pairings(lax.axis_size("gx"))
    return [lax.ppermute(c, "gx", pairs) for c, pairs in zip(columns, along)]


def pack_columns(place, received, packed):
    count = len(packed)
    rows, *columns = call(
        lambda *refs: columns_kernel(len(received), count, *refs),
        (array(EZ, VY, NX),) + (array(EY, NX),) * count,
        place,
        *received,
        *packed,
    )
    return rows, columns


def per_device(fixed, moving, owners, block_ids, counts, mix_yx, mix_z):
    place = jnp.stack([lax.axis_index("gz"), lax.axis_index("gy") % 2, lax.axis_index("gx") % 2]).astype(jnp.int32)
    count = len(pairings(lax.axis_size("gx")))
    request, near, far, flat, (image, image_side, image_face) = ask(place, moving, fixed, owners, block_ids)
    image_side = exchange_planes(image_side)
    image_packed = call(pack_kernel, (array(NY, NX),) * count, place, image, image_side)
    image_packed = exchange_columns(image_packed)
    request, image_packed = lax.optimization_barrier((request, image_packed))
    received = answer(request, near, far)
    image_sent = rows_to_send(place, image_face, image_side, *image_packed)
    image_halos = exchange_rows(image_sent)
    weights = spread_weights(counts, mix_z)
    image_sums, image_planes = call(
        lambda place_ref, own_ref, side_ref, sums_ref, image_ref: own_kernel(
            False, place_ref, own_ref, side_ref, image_ref, sums_ref
        ),
        (array(2 * NZ, NY, NX), array(EZ, NY, NX)),
        place,
        image,
        image_side,
    )
    image_sums = call(image_sums_kernel, array(2 * NZ, NY, NX), place, image_sums, scratch=LINES)
    received, weights, image_sums = lax.optimization_barrier((received, weights, image_sums))
    warped, side, face = mix(flat, place, received, weights, mix_yx.reshape(SLOTS, BV, BV))
    side = exchange_planes(side)
    row_halos = exchange_rows(rows_to_send(place, face, side))
    own_sums, out, *packed = call(
        lambda *refs: own_kernel(True, *refs),
        (array(3 * NZ, NY, NX), array(NZ, NY, NX)) + (array(NY, NX),) * count,
        place,
        warped,
        side,
        image_planes,
    )
    image_rows, image_columns = pack_columns(place, image_halos, image_packed)
    image_box = call(
        lambda *refs: image_box_kernel(count, *refs),
        array(3 * NZ, NY, NX),
        place,
        image_sums,
        image,
        image_rows,
        *image_columns,
        scratch=(pltpu.VMEM((2 * count, NY, NX), F32), pltpu.VMEM((2 * NZ, VY, NX), F32)),
    )
    rows, columns = pack_columns(place, row_halos, packed)
    columns = exchange_columns(columns)
    box = call(
        warped_sums_kernel,
        array(3 * NZ, NY, NX),
        place,
        own_sums,
        rows,
        image_rows,
        scratch=(pltpu.VMEM((3 * NZ, VY, NX), F32),) + LINES,
    )
    force = call(
        lambda *refs: force_kernel(count, *refs),
        array(3, NZ, NY, NX),
        place,
        box,
        image_box,
        warped,
        side,
        rows,
        *columns,
        *image_columns,
        scratch=(pltpu.VMEM((4 * count, NY, NX), F32),),
    )
    return out, force


def solution(mesh):
    return jax.shard_map(
        per_device,
        mesh=mesh,
        in_specs=(
            P("gz", "gy", "gx"),
            P("gz", "gy", "gx"),
            P("gz", "gy", "gx", None, None),
            P("gz", "gy", "gx", None),
            P("gz", "gy", "gx", None),
            P("gz", "gy", "gx", None, None, None),
            P("gz", "gy", "gx", None, None, None),
        ),
        out_specs=(P("gz", "gy", "gx"), P(None, "gz", "gy", "gx")),
        check_vma=False,
    )
```

time: 74.3 us -> 71.8 us (0.966)
  the two profiles are of different devices: /device:TPU:14 before, /device:TPU:4 now
where the time goes in v4:
time: 71.8 us; the launch traced here: 71.6 us
  Pallas kernels  30.2 us (42%)
  starting transfers between devices  21.4 us (30%)
  blocking collectives  8.31 us (12%)
  waiting for transfers between devices  7.66 us (11%)
  local copies, waits for them, and re-layouts  2.75 us (4%)
  between operations  0.86 us (1%)
    pallas_call x11, Pallas kernels, call(): pl.pallas_call(kernel, out_shape=outs, in_specs=[SMEM] + [VMEM] * (len(ar...  18.5 us
    ppermute x4, starting transfers between devices, exchange_rows(): lax.ppermute(s, 'gy', pairs)  10.6 us
    all_to_all x1, blocking collectives, exchange_in_half(): lax.all_to_all(array, BRICKS, split_axis=0, concat_axis=0, tiled=True, ax...  8.31 us
    pallas_call x1, Pallas kernels, mix(): pl.pallas_call(mix_kernel, out_shape=OUTER, in_specs=[SMEM, SMEM, VMEM, V...  5.68 us
    all_to_all x1, waiting for transfers between devices, exchange_in_half(): lax.all_to_all(array, BRICKS, split_axis=0, concat_axis=0, tiled=True, ax...  4.96 us
    all_to_all x1, starting transfers between devices, exchange_in_half(): lax.all_to_all(array, BRICKS, split_axis=0, concat_axis=0, tiled=True, ax...  4.93 us
    ppermute x2, starting transfers between devices, exchange_columns(): return [lax.ppermute(c, 'gx', pairs) for c, pairs in zip(columns, along)]  3.11 us
    pallas_call x1, Pallas kernels, prepare(): pl.pallas_call(prepare_kernel, out_shape=(jax.ShapeDtypeStruct((BLOCKS, V...  2.87 us
  transfers between devices with their start and end apart: 10, of which 3 were waited for; matrix products, arithmetic and copies ran while one was open for 2% of the time, Pallas kernels for 21%

profile of v4, /device:TPU:4, one launch (start us, length us, event | category | flops | bytes accessed | tf_op | source)
XLA Modules:
  0.0 71.6 jit_solution(2300398179410078095)
XLA Ops:
  0.7 2.9 %prepare.1 = (bf16[128,8,128]{2,1,0:T(8,128)(2,1)S(1)}, s32[8,1,64]{2,1,0:T(1,128)S(1)}, s32[1,256]{1,0:T(1,128)S(1)}, f32[1024,128]{1,0:T(8,128)S(1)}, f32[256,...) custom-call(s32[1]{0:T(128)} %bitcast.3.half_ref, s32[3]{0:T(128)S(1)} %pad_add_fusion.place_ref.refs_0_, ...), custom_call_target="tpu_custom_call" | custom-call | tf_op jit(solution)/shard_map/prepare/pallas_call | solution.py:122
  3.6 2.7 %collective-permute-start.2 = (bf16[128,8,128]{2,1,0:T(8,128)(2,1)S(1)}, bf16[128,8,128]{2,1,0:T(8,128)(2,1)S(1)}, u32[]{:S(2)}, u32[]{:S(2)}) collective-permute-start(bf16[128,8,128]{2,1,0:T(8,128)(2,1)S(1)} %get-tuple-element.34.refs_1_), channel_id=1, source_target_pairs={{0,8},{2,10},{4,12},{6,14},{8,0},{10,2},{12,4},{14,6},{1,9},{3,11}... | collective-permute-start | bytes 786440 | tf_op jit(solution)/shard_map/ppermute | solution.py:291
  6.3 1.3 %collective-permute-done.side_ref.refs_2_ = f32[256,128]{1,0:T(8,128)S(1)} collective-permute-done((f32[256,128]{1,0:T(8,128)S(1)}, f32[256,128]{1,0:T(8,128)S(1)}, u32[]{:S(2)}, u32[]{:S(2)}) %collective-permute-start) | collective-permute-done | bytes 131104 | tf_op jit(solution)/shard_map/ppermute | solution.py:626
  7.6 1.0 %shard_map.86 = f32[64,128]{1,0:T(8,128)S(1)} custom-call(s32[3]{0:T(128)S(1)} %pad_add_fusion.place_ref.refs_0_, f32[1024,128]{1,0:T(8,128)S(1)} %get-tuple-element.31.own_ref.refs_2_, f32[256,128]{1,0:T(8,128)S(1)} %collective-permute-done.side_ref.refs_2_), custom_call_target="tpu_custom_call" | custom-call | tf_op jit(solution)/shard_map/pallas_call | solution.py:315
  8.6 1.6 %collective-permute-start.1 = (f32[64,128]{1,0:T(8,128)S(1)}, f32[64,128]{1,0:T(8,128)S(1)}, u32[]{:S(2)}, u32[]{:S(2)}) collective-permute-start(f32[64,128]{1,0:T(8,128)S(1)} %shard_map.86), channel_id=1, source_target_pairs={{0,1},{1,0},{2,3},{3,2},{4,5},{5,4},{6,7},{7,6},{8,9},{9,8},{10,11... | collective-permute-start | bytes 98312 | tf_op jit(solution)/shard_map/ppermute | solution.py:648
  10.2 8.3 %all_to_all.10.refs_0_ = s32[8,1,64]{2,1,0:T(1,128)S(1)} all-to-all(s32[8,1,64]{2,1,0:T(1,128)S(1)} %get-tuple-element.30), channel_id=1, replica_groups={{0,1,2,3,4,5,6,7},{8,9,10,11,12,13,14,15},{16,17,18,19,20,21,22,23},{24..., dimensions={0} | all-to-all | bytes 4096 | tf_op jit(solution)/shard_map/all_to_all | solution.py:281
  18.5 2.2 %pick.1 = bf16[512,8,128]{2,1,0:T(8,128)(2,1)} custom-call(s32[8,1,64]{2,1,0:T(1,128)S(1)} %all_to_all.10.refs_0_, bf16[128,8,128]{2,1,0:T(8,128)(2,1)S(1)} %get-tuple-element.34.refs_1_, bf16[128,8,128]{2,1,0:T(8,128)(2,1)S(1)} %collective-permute-done.2.refs_2_), custom_call_target="tpu_custom_call" | custom-call | tf_op jit(solution)/shard_map/pick/pallas_call | solution.py:158
  20.7 4.9 %all-to-all-start.1 = ((bf16[8,64,8,128]{3,2,1,0:T(8,128)(2,1)}), bf16[8,64,8,128]{3,2,1,0:T(8,128)(2,1)S(1)}, u32[]{:S(2)}, u32[]{:S(2)}) async-start(bf16[8,64,8,128]{3,2,1,0:T(8,128)(2,1)} %bitcast.7), calls=%async_computation.1 | async-start | bytes 2097152 | tf_op jit(solution)/shard_map/all_to_all | solution.py:281
  25.7 0.1 reshape.61
  26.0 0.1 broadcast_in_dim.22
  26.1 0.4 copy.10
  26.5 0.3 bitcast_select_fusion.mix_ref
  26.8 1.0 %spread.1.spread_ref = bf16[16,384,128]{2,1,0:T(8,128)(2,1)S(1)} custom-call(f32[2048,8]{1,0:T(8,128)S(1)} %bitcast_select_fusion.mix_ref), custom_call_target="tpu_custom_call" | custom-call | tf_op jit(solution)/shard_map/spread/pallas_call | solution.py:183
  27.8 0.8 %shard_map.87 = (f32[32,64,128]{2,1,0:T(8,128)S(1)}, f32[24,64,128]{2,1,0:T(8,128)S(1)}) custom-call(s32[3]{0:T(128)S(1)} %pad_add_fusion.place_ref.refs_0_, f32[1024,128]{1,0:T(8,128)S(1)} %get-tuple-element.31.own_ref.refs_2_, f32[256,128]{1,0:T(8,128)S(1)} %collective-permute-done.side_ref.refs_2_), custom_call_target="tpu_custom_call" | custom-call | tf_op jit(solution)/shard_map/pallas_call | solution.py:315
  28.7 0.9 %copy-done.2 = f32[24,64,128]{2,1,0:T(8,128)} copy-done((f32[24,64,128]{2,1,0:T(8,128)}, f32[24,64,128]{2,1,0:T(8,128)S(1)}, u32[]{:S(2)}) %copy-start.2) | copy-done | bytes 786456
  29.6 2.7 %shard_map.88.refs_1_ = f32[32,64,128]{2,1,0:T(8,128)S(1)} custom-call(s32[3]{0:T(128)S(1)} %pad_add_fusion.place_ref.refs_0_, f32[32,64,128]{2,1,0:T(8,128)S(1)} %get-tuple-element.35.own_sums_ref), custom_call_target="tpu_custom_call" | custom-call | tf_op jit(solution)/shard_map/pallas_call | solution.py:315
  32.3 1.0 %copy-done = f32[32,64,128]{2,1,0:T(8,128)} copy-done((f32[32,64,128]{2,1,0:T(8,128)}, f32[32,64,128]{2,1,0:T(8,128)S(1)}, u32[]{:S(2)}) %copy-start) | copy-done | bytes 1048600
  33.3 5.0 %all-to-all-done.1 = bf16[8,64,8,128]{3,2,1,0:T(8,128)(2,1)S(1)} async-done(((bf16[8,64,8,128]{3,2,1,0:T(8,128)(2,1)}), bf16[8,64,8,128]{3,2,1,0:T(8,128)(2,1)S(1)}, u32[]{:S(2)}, u32[]{:S(2)}) %all-to-all-start.1) | async-done | bytes 1048608 | tf_op jit(solution)/shard_map/all_to_all | solution.py:281
  38.2 5.7 %mix.1 = (f32[1024,128]{1,0:T(8,128)S(1)}, f32[256,128]{1,0:T(8,128)S(1)}, f32[16,8,128]{2,1,0:T(8,128)S(1)}) custom-call(s32[3]{0:T(128)S(1)} %pad_add_fusion.place_ref.refs_0_, s32[256]{0:T(256)S(1)} %bitcast.14, bf16[512,8,128]{2,1,0:T(8,128)(2,1)S(1)} %bitcast.13, bf16[16,384,128]{2,1,0:T(8,128)(2,1)S(1)} %spread.1.spread_ref, ...), custom_call_target="tpu_custom_call" | custom-call | tf_op jit(solution)/shard_map/mix/pallas_call | solution.py:259
  44.0 1.3 %collective-permute-done.3.refs_2_.refs_4_ = f32[256,128]{1,0:T(8,128)S(1)} collective-permute-done((f32[256,128]{1,0:T(8,128)S(1)}, f32[256,128]{1,0:T(8,128)S(1)}, u32[]{:S(2)}, u32[]{:S(2)}) %collective-permute-start.3) | collective-permute-done | bytes 131104 | tf_op jit(solution)/shard_map/ppermute | solution.py:626
  45.3 0.6 shard_map.90
  45.9 1.5 %collective-permute-start.4 = (f32[20,4,128]{2,1,0:T(4,128)S(1)}, f32[20,4,128]{2,1,0:T(4,128)S(1)}, u32[]{:S(2)}, u32[]{:S(2)}) collective-permute-start(f32[20,4,128]{2,1,0:T(4,128)S(1)} %get-tuple-element.44), channel_id=1, source_target_pairs={{0,2},{2,0},{4,6},{6,4},{8,10},{10,8},{12,14},{14,12},{1,3},{3,1},... | collective-permute-start | bytes 122888 | tf_op jit(solution)/shard_map/ppermute | solution.py:643
  47.4 3.1 %collective-permute-start.5 = (f32[20,4,128]{2,1,0:T(4,128)S(1)}, f32[20,4,128]{2,1,0:T(4,128)S(1)}, u32[]{:S(2)}, u32[]{:S(2)}) collective-permute-start(f32[20,4,128]{2,1,0:T(4,128)S(1)} %get-tuple-element.45), channel_id=1, source_target_pairs={{2,4},{4,2},{6,8},{8,6},{10,12},{12,10},{3,5},{5,3},{7,9},{9,7},{1... | collective-permute-start | bytes 122888 | tf_op jit(solution)/shard_map/ppermute | solution.py:643
  50.5 0.6 shard_map.92
  51.2 6.0 %collective-permute-start.7 = (f32[21,4,128]{2,1,0:T(4,128)S(1)}, f32[21,4,128]{2,1,0:T(4,128)S(1)}, u32[]{:S(2)}, u32[]{:S(2)}) collective-permute-start(f32[21,4,128]{2,1,0:T(4,128)S(1)} %get-tuple-element.51), channel_id=1, source_target_pairs={{2,4},{4,2},{6,8},{8,6},{10,12},{12,10},{3,5},{5,3},{7,9},{9,7},{1... | collective-permute-start | bytes 129032 | tf_op jit(solution)/shard_map/ppermute | solution.py:643
  57.1 2.1 %shard_map.89 = (f32[48,64,128]{2,1,0:T(8,128)S(1)}, f32[16,64,128]{2,1,0:T(8,128)}, f32[64,128]{1,0:T(8,128)S(1)}) custom-call(s32[3]{0:T(128)S(1)} %pad_add_fusion.place_ref.refs_0_, f32[1024,128]{1,0:T(8,128)S(1)} %get-tuple-element.38.refs_1_.refs_3_, f32[256,128]{1,0:T(8,128)S(1)} %collective-permute-done.3.refs_2_.refs_4_, f32[24,64,128]{2,1,0:T(8,128)S(1)} %copy-done.3), custom_call_target="tpu_custom_call" | custom-call | tf_op jit(solution)/shard_map/pallas_call | solution.py:315
  59.3 0.6 shard_map.91
  59.9 1.6 %collective-permute-start.8 = (f32[72,128]{1,0:T(8,128)S(1)}, f32[72,128]{1,0:T(8,128)S(1)}, u32[]{:S(2)}, u32[]{:S(2)}) collective-permute-start(f32[72,128]{1,0:T(8,128)S(1)} %get-tuple-element.55), channel_id=1, source_target_pairs={{0,1},{1,0},{2,3},{3,2},{4,5},{5,4},{6,7},{7,6},{8,9},{9,8},{10,11... | collective-permute-start | bytes 110600 | tf_op jit(solution)/shard_map/ppermute | solution.py:648
  61.5 0.6 shard_map.93
  62.0 1.9 %shard_map.95.refs_2_ = f32[48,64,128]{2,1,0:T(8,128)S(1)} custom-call(s32[3]{0:T(128)S(1)} %pad_add_fusion.place_ref.refs_0_, f32[32,64,128]{2,1,0:T(8,128)S(1)} %copy-done.1, f32[1024,128]{1,0:T(8,128)S(1)} %get-tuple-element.31.own_ref.refs_2_, f32[24,8,128]{2,1,0:T(8,128)S(1)} %get-tuple-element.52.image_rows_ref.refs_3_, ...), custom_call_target="tpu_custom_call" | custom-call | tf_op jit(solution)/shard_map/pallas_call | solution.py:315
  63.9 3.7 %shard_map.94.refs_1_ = f32[48,64,128]{2,1,0:T(8,128)S(1)} custom-call(s32[3]{0:T(128)S(1)} %pad_add_fusion.place_ref.refs_0_, f32[48,64,128]{2,1,0:T(8,128)S(1)} %get-tuple-element.42.own_sums_ref, f32[24,8,128]{2,1,0:T(8,128)S(1)} %get-tuple-element.47.rows_ref.refs_5_, f32[24,8,128]{2,1,0:T(8,128)S(1)} %get-tuple-element.52.image_rows_ref.refs_3_), custom_call_target="tpu_custom_call" | custom-call | tf_op jit(solution)/shard_map/pallas_call | solution.py:315
  67.6 3.9 %shard_map.96 = f32[3,16,64,128]{3,2,1,0:T(8,128)} custom-call(s32[3]{0:T(128)S(1)} %pad_add_fusion.place_ref.refs_0_, f32[48,64,128]{2,1,0:T(8,128)S(1)} %shard_map.94.refs_1_, f32[48,64,128]{2,1,0:T(8,128)S(1)} %shard_map.95.refs_2_, f32[1024,128]{1,0:T(8,128)S(1)} %get-tuple-element.38.refs_1_.refs_3_, ...), custom_call_target="tpu_custom_call" | custom-call | tf_op jit(solution)/shard_map/pallas_call | solution.py:315
  (24 shorter events, 0.4 us)
Async XLA Ops:
  3.6 14.9 %collective-permute-start.2 = (bf16[128,8,128]{2,1,0:T(8,128)(2,1)S(1)}, bf16[128,8,128]{2,1,0:T(8,128)(2,1)S(1)}, u32[]{:S(2)}, u32[]{:S(2)}) collective-permute-start(bf16[128,8,128]{2,1,0:T(8,128)(2,1)S(1)} %get-tuple-element.34.refs_1_), channel_id=1, source_target_pairs={{0,8},{2,10},{4,12},{6,14},{8,0},{10,2},{12,4},{14,6},{1,9},{3,11}... | collective-permute-start | bytes 786440 | tf_op jit(solution)/shard_map/ppermute | solution.py:291
  6.3 1.3 %collective-permute-start = (f32[256,128]{1,0:T(8,128)S(1)}, f32[256,128]{1,0:T(8,128)S(1)}, u32[]{:S(2)}, u32[]{:S(2)}) collective-permute-start(f32[256,128]{1,0:T(8,128)S(1)} %get-tuple-element.32), channel_id=1, source_target_pairs={{0,16},{16,0},{1,17},{17,1},{2,18},{18,2},{3,19},{19,3},{4,20},{20... | collective-permute-start | bytes 393224 | tf_op jit(solution)/shard_map/ppermute | solution.py:626
  8.6 9.9 %collective-permute-start.1 = (f32[64,128]{1,0:T(8,128)S(1)}, f32[64,128]{1,0:T(8,128)S(1)}, u32[]{:S(2)}, u32[]{:S(2)}) collective-permute-start(f32[64,128]{1,0:T(8,128)S(1)} %shard_map.86), channel_id=1, source_target_pairs={{0,1},{1,0},{2,3},{3,2},{4,5},{5,4},{6,7},{7,6},{8,9},{9,8},{10,11... | collective-permute-start | bytes 98312 | tf_op jit(solution)/shard_map/ppermute | solution.py:648
  18.5 7.1 %copy-start.5 = (s32[1,1,1,128]{3,2,1,0:T(1,128)S(1)}, s32[1,1,1,128]{3,2,1,0:T(1,128)}, u32[]{:S(2)}) copy-start(s32[1,1,1,128]{3,2,1,0:T(1,128)} %param.11) | copy-start | bytes 1540
  18.5 7.6 %copy-start.4 = (f32[1,1,1,256,8,8]{3,5,4,2,1,0:T(8,128)S(1)}, f32[1,1,1,256,8,8]{3,5,4,2,1,0:T(8,128)}, u32[]{:S(2)}) copy-start(f32[1,1,1,256,8,8]{3,5,4,2,1,0:T(8,128)} %param.13) | copy-start | bytes 196612
  20.7 17.5 %all-to-all-start.1 = ((bf16[8,64,8,128]{3,2,1,0:T(8,128)(2,1)}), bf16[8,64,8,128]{3,2,1,0:T(8,128)(2,1)S(1)}, u32[]{:S(2)}, u32[]{:S(2)}) async-start(bf16[8,64,8,128]{3,2,1,0:T(8,128)(2,1)} %bitcast.7), calls=%async_computation.1 | async-start | bytes 2097152 | tf_op jit(solution)/shard_map/all_to_all | solution.py:281
  28.7 0.9 %copy-start.2 = (f32[24,64,128]{2,1,0:T(8,128)}, f32[24,64,128]{2,1,0:T(8,128)S(1)}, u32[]{:S(2)}) copy-start(f32[24,64,128]{2,1,0:T(8,128)S(1)} %get-tuple-element.40.refs_3_) | copy-start | bytes 2359300
  32.3 1.0 %copy-start = (f32[32,64,128]{2,1,0:T(8,128)}, f32[32,64,128]{2,1,0:T(8,128)S(1)}, u32[]{:S(2)}) copy-start(f32[32,64,128]{2,1,0:T(8,128)S(1)} %shard_map.88.refs_1_) | copy-start | bytes 3145732
  38.2 18.9 %copy-start.3 = (f32[24,64,128]{2,1,0:T(8,128)S(1)}, f32[24,64,128]{2,1,0:T(8,128)}, u32[]{:S(2)}) copy-start(f32[24,64,128]{2,1,0:T(8,128)} %copy-done.2) | copy-start | bytes 2359300
  43.9 18.1 %copy-start.1 = (f32[32,64,128]{2,1,0:T(8,128)S(1)}, f32[32,64,128]{2,1,0:T(8,128)}, u32[]{:S(2)}) copy-start(f32[32,64,128]{2,1,0:T(8,128)} %copy-done) | copy-start | bytes 3145732
  43.9 1.4 %collective-permute-start.3 = (f32[256,128]{1,0:T(8,128)S(1)}, f32[256,128]{1,0:T(8,128)S(1)}, u32[]{:S(2)}, u32[]{:S(2)}) collective-permute-start(f32[256,128]{1,0:T(8,128)S(1)} %get-tuple-element.39), channel_id=1, source_target_pairs={{0,16},{16,0},{1,17},{17,1},{2,18},{18,2},{3,19},{19,3},{4,20},{20... | collective-permute-start | bytes 393224 | tf_op jit(solution)/shard_map/ppermute | solution.py:626
  45.9 13.3 %collective-permute-start.4 = (f32[20,4,128]{2,1,0:T(4,128)S(1)}, f32[20,4,128]{2,1,0:T(4,128)S(1)}, u32[]{:S(2)}, u32[]{:S(2)}) collective-permute-start(f32[20,4,128]{2,1,0:T(4,128)S(1)} %get-tuple-element.44), channel_id=1, source_target_pairs={{0,2},{2,0},{4,6},{6,4},{8,10},{10,8},{12,14},{14,12},{1,3},{3,1},... | collective-permute-start | bytes 122888 | tf_op jit(solution)/shard_map/ppermute | solution.py:643
  47.4 11.8 %collective-permute-start.5 = (f32[20,4,128]{2,1,0:T(4,128)S(1)}, f32[20,4,128]{2,1,0:T(4,128)S(1)}, u32[]{:S(2)}, u32[]{:S(2)}) collective-permute-start(f32[20,4,128]{2,1,0:T(4,128)S(1)} %get-tuple-element.45), channel_id=1, source_target_pairs={{2,4},{4,2},{6,8},{8,6},{10,12},{12,10},{3,5},{5,3},{7,9},{9,7},{1... | collective-permute-start | bytes 122888 | tf_op jit(solution)/shard_map/ppermute | solution.py:643
  51.1 10.4 %collective-permute-start.6 = (f32[21,4,128]{2,1,0:T(4,128)S(1)}, f32[21,4,128]{2,1,0:T(4,128)S(1)}, u32[]{:S(2)}, u32[]{:S(2)}) collective-permute-start(f32[21,4,128]{2,1,0:T(4,128)S(1)} %get-tuple-element.50), channel_id=1, source_target_pairs={{0,2},{2,0},{4,6},{6,4},{8,10},{10,8},{12,14},{14,12},{1,3},{3,1},... | collective-permute-start | bytes 129032 | tf_op jit(solution)/shard_map/ppermute | solution.py:643
  51.2 10.3 %collective-permute-start.7 = (f32[21,4,128]{2,1,0:T(4,128)S(1)}, f32[21,4,128]{2,1,0:T(4,128)S(1)}, u32[]{:S(2)}, u32[]{:S(2)}) collective-permute-start(f32[21,4,128]{2,1,0:T(4,128)S(1)} %get-tuple-element.51), channel_id=1, source_target_pairs={{2,4},{4,2},{6,8},{8,6},{10,12},{12,10},{3,5},{5,3},{7,9},{9,7},{1... | collective-permute-start | bytes 129032 | tf_op jit(solution)/shard_map/ppermute | solution.py:643
  59.9 7.7 %collective-permute-start.8 = (f32[72,128]{1,0:T(8,128)S(1)}, f32[72,128]{1,0:T(8,128)S(1)}, u32[]{:S(2)}, u32[]{:S(2)}) collective-permute-start(f32[72,128]{1,0:T(8,128)S(1)} %get-tuple-element.55), channel_id=1, source_target_pairs={{0,1},{1,0},{2,3},{3,2},{4,5},{5,4},{6,7},{7,6},{8,9},{9,8},{10,11... | collective-permute-start | bytes 110600 | tf_op jit(solution)/shard_map/ppermute | solution.py:648

commit v5 on v4

--- a/solution.py
+++ b/solution.py
@@ -145,13 +145,10 @@
 def pick_kernel(capacity, request_ref, near_ref, far_ref, out_ref):
     width = 2 * capacity
 
-    def holder(h, _):
+    for h in range(out_ref.shape[0] // width):
         for k in range(width):
             source = near_ref if k < capacity else far_ref
             out_ref[h * width + k] = source[request_ref[h, 0, k]]
-        return 0
-
-    lax.fori_loop(0, out_ref.shape[0] // width, holder, 0)
 
 
 def pick(request, near, far, capacity):
@@ -194,15 +191,17 @@
 
 
 def mix_kernel(
-    place_ref, flat_ref, received_ref, spread_ref, mix_hbm, warped_ref, side_ref, face_ref, weights_ref, sems
+    place_ref, flat_ref, received_ref, spread_ref, mix_hbm, warped_ref, side_ref, face_ref,
+    weights_ref, left_ref, blocks_ref, sems,
 ):
     share = STEP * PER
+    steps = GROUPS // STEP
 
     def weights(step):
         rows = pl.ds(step * share, share)
         return pltpu.make_async_copy(mix_hbm.at[rows], weights_ref.at[rows], sems.at[step])
 
-    for step in range(GROUPS // STEP):
+    for step in range(steps):
         weights(step).start()
 
     def across_planes(g):
@@ -210,40 +209,35 @@
         parts = jnp.dot(spread_ref[g], source.astype(BF16), preferred_element_type=F32)
         mixed = parts[:ROWS] + parts[ROWS : 2 * ROWS] + parts[2 * ROWS :]
         high = mixed.astype(BF16).astype(F32)
-        return high, mixed - high
-
-    def in_plane(g, high, low):
-        rows = []
+        low = mixed - high
         for j in range(NBX):
             a = slice(2 * j * VZ, (2 * j + 1) * VZ)
             b = slice((2 * j + 1) * VZ, (2 * j + 2) * VZ)
-            left = jnp.concatenate(
+            left_ref[g * NBX + j] = jnp.concatenate(
                 [jnp.concatenate([high[a], high[b]], 1), jnp.concatenate([low[a], low[b]], 1)], 0
             ).astype(BF16)
-            right = weights_ref[pl.ds(g * PER + 2 * j, 2)].reshape(2 * BV, BV)
-            both = jnp.dot(left, right, preferred_element_type=F32)
-            rows.append(both[:VZ] + both[VZ:])
-        return rows
-
-    def place_rows(g, rows):
+
+    def in_plane(g):
+        for j in range(NBX):
+            right = weights_ref[g * PER + 2 * j : g * PER + 2 * j + 2].reshape(2 * BV, BV)
+            both = jnp.dot(left_ref[g * NBX + j], right, preferred_element_type=F32)
+            blocks_ref[g * NBX + j] = both[:VZ] + both[VZ:]
+
+    def into_rows(g):
         start = (g // NBY) * (VZ * NY) + (g % NBY) * VY
-        for y, row in enumerate(swap_chunks(rows)):
+        for y, row in enumerate(swap_chunks([blocks_ref[g * NBX + j] for j in range(NBX)])):
             warped_ref[pl.ds(start + y, VZ, stride=NY), :] = row
 
-    def some(step, _):
-        weights(step).wait()
-        first = step * STEP
-        mixed, done = {}, {}
-        for t in range(STEP + 2):
-            if t < STEP:
-                mixed[t] = across_planes(first + t)
-            if 0 <= t - 1 < STEP:
-                done[t - 1] = in_plane(first + t - 1, *mixed.pop(t - 1))
-            if 0 <= t - 2:
-                place_rows(first + t - 2, done.pop(t - 2))
-        return 0
-
-    lax.fori_loop(0, GROUPS // STEP, some, 0)
+    for step in range(-1, steps + 1):
+        if 0 <= step < steps:
+            weights(step).wait()
+        for q in range(STEP):
+            if step + 1 < steps:
+                across_planes((step + 1) * STEP + q)
+            if 0 <= step < steps:
+                in_plane(step * STEP + q)
+            if step >= 1:
+                into_rows((step - 1) * STEP + q)
     outer(place_ref, warped_ref, side_ref, face_ref)
 
 
@@ -263,6 +257,8 @@
         out_specs=(VMEM,) * 3,
         scratch_shapes=[
             pltpu.VMEM((SLOTS, BV, BV), BF16),
+            pltpu.VMEM((BLOCKS, 2 * VZ, 2 * BV), BF16),
+            pltpu.VMEM((BLOCKS, VZ, BV), F32),
             pltpu.SemaphoreType.DMA((GROUPS // STEP,)),
         ],
         compiler_params=pltpu.CompilerParams(vmem_limit_bytes=WIDE),
@@ -311,12 +307,15 @@
 COUNT = float((REACH + 1) ** 3)
 
 
-def call(kernel, outs, *args, scratch=()):
+def call(kernel, outs, *args, scratch=(), out_hbm=None):
+    specs = jax.tree.map(lambda _: VMEM, outs)
+    if out_hbm is not None:
+        specs = tuple(pl.BlockSpec(memory_space=pltpu.HBM) if i == out_hbm else VMEM for i in range(len(outs)))
     return pl.pallas_call(
         kernel,
         out_shape=outs,
         in_specs=[SMEM] + [VMEM] * (len(args) - 1),
-        out_specs=jax.tree.map(lambda _: VMEM, outs),
+        out_specs=specs,
         scratch_shapes=scratch,
         compiler_params=pltpu.CompilerParams(vmem_limit_bytes=LIMIT),
     )(*args)
@@ -384,9 +383,9 @@
 def own_kernel(with_image, place_ref, own_ref, side_ref, *refs):
     image_ref, sums_ref, *columns = refs
     if with_image:
-        out_ref = columns.pop(0)
-        for z in range(NZ):
-            out_ref[z] = own_ref[z * NY : (z + 1) * NY, :]
+        out_hbm, sem = columns.pop(0), columns.pop()
+        copy = pltpu.make_async_copy(own_ref, out_hbm, sem)
+        copy.start()
 
     def rows_of(q, _):
         at = pl.multiple_of(q * VY, VY)
@@ -406,6 +405,8 @@
         return 0
 
     lax.fori_loop(0, NBY, rows_of, 0)
+    if with_image:
+        copy.wait()
 
 
 def columns_kernel(y_count, x_count, place_ref, *refs):
@@ -471,16 +472,20 @@
     lanes = line.shape[0]
 
     def some(step, _):
+        totals = []
         for k in range(lanes):
-            i = step * lanes + k
-            own, halo = load(i)
+            own, halo = load(step * lanes + k)
             line[k, :RAD] = halo[RAD:]
             line[k, RAD : RAD + NY] = own
             line[k, RAD + NY : EY] = halo[:RAD]
             pair[k, :EY] = line[k, :EY] + line[k, 1 : EY + 1]
             four[k, :EY] = pair[k, :EY] + pair[k, 2 : EY + 2]
-            total = four[k, :NY] + four[k, RAD : RAD + NY] + line[k, REACH : REACH + NY]
-            out_ref[i] = split_dot(total, near)
+            totals.append(four[k, :NY] + four[k, RAD : RAD + NY] + line[k, REACH : REACH + NY])
+        parts = [pieces(total, 3) for total in totals]
+        sums = jnp.dot(jnp.concatenate([p for part in parts for p in part], 0), near, preferred_element_type=F32)
+        for k in range(lanes):
+            at = 3 * k * NY
+            out_ref[step * lanes + k] = sums[at : at + NY] + sums[at + NY : at + 2 * NY] + sums[at + 2 * NY : at + 3 * NY]
         return 0
 
     lax.fori_loop(0, count // lanes, some, 0)
@@ -499,7 +504,7 @@
             outer_sums[f * NZ + z] = total
 
 
-def warped_sums_kernel(place_ref, own_sums_ref, rows_ref, image_rows_ref, out_ref, outer_sums, *lines):
+def warped_sums_kernel(own_sums_ref, rows_ref, image_rows_ref, out_ref, outer_sums, *lines):
     w = [rows_ref[p] for p in range(EZ)]
     halo_sums([w, [v * v for v in w], [image_rows_ref[p] * v for p, v in enumerate(w)]], outer_sums)
     brick_sums(3 * NZ, lambda i: (own_sums_ref[i], outer_sums[i]), out_ref, *lines)
@@ -565,12 +570,21 @@
     lax.fori_loop(0, NZ, plane, 0, unroll=2)
 
 
+def finish_kernel(y_count, x_count, place_ref, *refs):
+    halos, refs = refs[: y_count + x_count], refs[y_count + x_count :]
+    sums_ref, image_ref, own_sums_ref, rows_ref, box_ref, out_ref = refs[:6]
+    columns, (image_rows, edges, image_outer, outer_sums, *lines) = refs[6 : 6 + x_count], refs[6 + x_count :]
+    columns_kernel(y_count, x_count, place_ref, *halos, image_rows, *columns)
+    image_box_kernel(x_count, place_ref, sums_ref, image_ref, image_rows, *columns, box_ref, edges, image_outer)
+    warped_sums_kernel(own_sums_ref, rows_ref, image_rows, out_ref, outer_sums, *lines)
+
+
 HALF = NY // 2
 
 
 def force_kernel(x_count, place_ref, sums_ref, image_ref, own_ref, side_ref, rows_ref, *refs):
     warped_halos, fixed_halos = refs[:x_count], refs[x_count : 2 * x_count]
-    force_ref, edges = refs[2 * x_count], refs[2 * x_count + 1]
+    force_hbm, edges, force_ref, sems = refs[2 * x_count :]
     for k in range(x_count):
         table = edge_table(side_is_right(place_ref, k))
         w, f = warped_halos[k][...], fixed_halos[k][...]
@@ -612,7 +626,17 @@
             force_ref[2, z, part, :] = half * (after - before)
         return 0
 
-    lax.fori_loop(0, NZ, plane, 0)
+    def out(group):
+        rows = pl.ds(group * RAD, RAD)
+        return [pltpu.make_async_copy(force_ref.at[d, rows], force_hbm.at[d, rows], sems.at[d, group]) for d in range(3)]
+
+    for group in range(NZ // RAD):
+        lax.fori_loop(group * RAD, (group + 1) * RAD, plane, 0)
+        for copy in out(group):
+            copy.start()
+    for group in range(NZ // RAD):
+        for copy in out(group):
+            copy.wait()
 
 
 def pairings(size):
@@ -688,37 +712,37 @@
     row_halos = exchange_rows(rows_to_send(place, face, side))
     own_sums, out, *packed = call(
         lambda *refs: own_kernel(True, *refs),
-        (array(3 * NZ, NY, NX), array(NZ, NY, NX)) + (array(NY, NX),) * count,
+        (array(3 * NZ, NY, NX), array(NZ * NY, NX)) + (array(NY, NX),) * count,
         place,
         warped,
         side,
         image_planes,
-    )
-    image_rows, image_columns = pack_columns(place, image_halos, image_packed)
-    image_box = call(
-        lambda *refs: image_box_kernel(count, *refs),
-        array(3 * NZ, NY, NX),
-        place,
-        image_sums,
-        image,
-        image_rows,
-        *image_columns,
-        scratch=(pltpu.VMEM((2 * count, NY, NX), F32), pltpu.VMEM((2 * NZ, VY, NX), F32)),
+        scratch=(pltpu.SemaphoreType.DMA,),
+        out_hbm=1,
     )
     rows, columns = pack_columns(place, row_halos, packed)
     columns = exchange_columns(columns)
-    box = call(
-        warped_sums_kernel,
-        array(3 * NZ, NY, NX),
+    image_box, box, *image_columns = call(
+        lambda *refs: finish_kernel(len(image_halos), count, *refs),
+        (array(3 * NZ, NY, NX), array(3 * NZ, NY, NX)) + (array(EY, NX),) * count,
         place,
+        *image_halos,
+        *image_packed,
+        image_sums,
+        image,
         own_sums,
         rows,
-        image_rows,
-        scratch=(pltpu.VMEM((3 * NZ, VY, NX), F32),) + LINES,
+        scratch=(
+            pltpu.VMEM((EZ, VY, NX), F32),
+            pltpu.VMEM((2 * count, NY, NX), F32),
+            pltpu.VMEM((2 * NZ, VY, NX), F32),
+            pltpu.VMEM((3 * NZ, VY, NX), F32),
+        )
+        + LINES,
     )
-    force = call(
+    (force,) = call(
         lambda *refs: force_kernel(count, *refs),
-        array(3, NZ, NY, NX),
+        (array(3, NZ, NY, NX),),
         place,
         box,
         image_box,
@@ -727,9 +751,14 @@
         rows,
         *columns,
         *image_columns,
-        scratch=(pltpu.VMEM((4 * count, NY, NX), F32),),
+        scratch=(
+            pltpu.VMEM((4 * count, NY, NX), F32),
+            pltpu.VMEM((3, NZ, NY, NX), F32),
+            pltpu.SemaphoreType.DMA((3, NZ // RAD)),
+        ),
+        out_hbm=0,
     )
-    return out, force
+    return out.reshape(NZ, NY, NX), force
 
 
 def solution(mesh):

time: 71.8 us -> 68.3 us (0.951)
  Pallas kernels: 30.2 us -> 26.3 us
    pallas_call x11 -> x9, Pallas kernels: 18.5 us -> 15.6 us  [call(): pl.pallas_call(kernel, out_shape=outs, in_specs=[SMEM] + [VMEM] * (len(ar...]
    pallas_call x1, Pallas kernels: 5.68 us -> 4.81 us  [mix(): pl.pallas_call(mix_kernel, out_shape=OUTER, in_specs=[SMEM, SMEM, VMEM, V...]
  transfers between devices with their start and end apart: 10 -> 10, of which waited for: 3 -> 3; matrix products, arithmetic and copies ran while one was open for 2% -> 2% of each run, Pallas kernels for 21% -> 18%
where the time goes in v5:
time: 68.3 us; the launch traced here: 68 us
  Pallas kernels  26.3 us (39%)
  starting transfers between devices  21.4 us (31%)
  blocking collectives  8.31 us (12%)
  waiting for transfers between devices  7.99 us (12%)
  local copies, waits for them, and re-layouts  2.76 us (4%)
  between operations  0.85 us (1%)
    pallas_call x9, Pallas kernels, call(): pl.pallas_call(kernel, out_shape=outs, in_specs=[SMEM] + [VMEM] * (len(ar...  15.6 us
    ppermute x4, starting transfers between devices, exchange_rows(): lax.ppermute(s, 'gy', pairs)  10.6 us
    all_to_all x1, blocking collectives, exchange_in_half(): lax.all_to_all(array, BRICKS, split_axis=0, concat_axis=0, tiled=True, ax...  8.31 us
    all_to_all x1, waiting for transfers between devices, exchange_in_half(): lax.all_to_all(array, BRICKS, split_axis=0, concat_axis=0, tiled=True, ax...  5.28 us
    all_to_all x1, starting transfers between devices, exchange_in_half(): lax.all_to_all(array, BRICKS, split_axis=0, concat_axis=0, tiled=True, ax...  4.93 us
    pallas_call x1, Pallas kernels, mix(): pl.pallas_call(mix_kernel, out_shape=OUTER, in_specs=[SMEM, SMEM, VMEM, V...  4.81 us
    ppermute x2, starting transfers between devices, exchange_columns(): return [lax.ppermute(c, 'gx', pairs) for c, pairs in zip(columns, along)]  3.11 us
    pallas_call x1, Pallas kernels, prepare(): pl.pallas_call(prepare_kernel, out_shape=(jax.ShapeDtypeStruct((BLOCKS, V...  2.87 us
  transfers between devices with their start and end apart: 10, of which 3 were waited for; matrix products, arithmetic and copies ran while one was open for 2% of the time, Pallas kernels for 18%

profile of v5, /device:TPU:4, one launch (start us, length us, event | category | flops | bytes accessed | tf_op | source)
XLA Modules:
  0.0 68.0 jit_solution(7980195761301799478)
XLA Ops:
  0.6 0.1 pad_add_fusion.place_ref.refs_0_
  0.7 2.9 %prepare.1 = (bf16[128,8,128]{2,1,0:T(8,128)(2,1)S(1)}, s32[8,1,64]{2,1,0:T(1,128)S(1)}, s32[1,256]{1,0:T(1,128)S(1)}, f32[1024,128]{1,0:T(8,128)S(1)}, f32[256,...) custom-call(s32[1]{0:T(128)} %bitcast.3.half_ref, s32[3]{0:T(128)S(1)} %pad_add_fusion.place_ref.refs_0_, ...), custom_call_target="tpu_custom_call" | custom-call | tf_op jit(solution)/shard_map/prepare/pallas_call | solution.py:122
  3.6 2.7 %collective-permute-start.2 = (bf16[128,8,128]{2,1,0:T(8,128)(2,1)S(1)}, bf16[128,8,128]{2,1,0:T(8,128)(2,1)S(1)}, u32[]{:S(2)}, u32[]{:S(2)}) collective-permute-start(bf16[128,8,128]{2,1,0:T(8,128)(2,1)S(1)} %get-tuple-element.35.refs_1_), channel_id=1, source_target_pairs={{0,8},{2,10},{4,12},{6,14},{8,0},{10,2},{12,4},{14,6},{1,9},{3,11}... | collective-permute-start | bytes 786440 | tf_op jit(solution)/shard_map/ppermute | solution.py:287
  6.3 1.3 %collective-permute-done.side_ref.refs_2_ = f32[256,128]{1,0:T(8,128)S(1)} collective-permute-done((f32[256,128]{1,0:T(8,128)S(1)}, f32[256,128]{1,0:T(8,128)S(1)}, u32[]{:S(2)}, u32[]{:S(2)}) %collective-permute-start) | collective-permute-done | bytes 131104 | tf_op jit(solution)/shard_map/ppermute | solution.py:650
  7.6 1.0 %shard_map.86 = f32[64,128]{1,0:T(8,128)S(1)} custom-call(s32[3]{0:T(128)S(1)} %pad_add_fusion.place_ref.refs_0_, f32[1024,128]{1,0:T(8,128)S(1)} %get-tuple-element.32.own_ref.refs_5_, f32[256,128]{1,0:T(8,128)S(1)} %collective-permute-done.side_ref.refs_2_), custom_call_target="tpu_custom_call" | custom-call | tf_op jit(solution)/shard_map/pallas_call | solution.py:314
  8.6 1.6 %collective-permute-start.1 = (f32[64,128]{1,0:T(8,128)S(1)}, f32[64,128]{1,0:T(8,128)S(1)}, u32[]{:S(2)}, u32[]{:S(2)}) collective-permute-start(f32[64,128]{1,0:T(8,128)S(1)} %shard_map.86), channel_id=1, source_target_pairs={{0,1},{1,0},{2,3},{3,2},{4,5},{5,4},{6,7},{7,6},{8,9},{9,8},{10,11... | collective-permute-start | bytes 98312 | tf_op jit(solution)/shard_map/ppermute | solution.py:672
  10.2 8.3 %all_to_all.10.refs_0_ = s32[8,1,64]{2,1,0:T(1,128)S(1)} all-to-all(s32[8,1,64]{2,1,0:T(1,128)S(1)} %get-tuple-element.31), channel_id=1, replica_groups={{0,1,2,3,4,5,6,7},{8,9,10,11,12,13,14,15},{16,17,18,19,20,21,22,23},{24..., dimensions={0} | all-to-all | bytes 4096 | tf_op jit(solution)/shard_map/all_to_all | solution.py:277
  18.5 2.0 %pick.1 = bf16[512,8,128]{2,1,0:T(8,128)(2,1)} custom-call(s32[8,1,64]{2,1,0:T(1,128)S(1)} %all_to_all.10.refs_0_, bf16[128,8,128]{2,1,0:T(8,128)(2,1)S(1)} %get-tuple-element.35.refs_1_, bf16[128,8,128]{2,1,0:T(8,128)(2,1)S(1)} %collective-permute-done.2.refs_2_), custom_call_target="tpu_custom_call" | custom-call | tf_op jit(solution)/shard_map/pick/pallas_call | solution.py:155
  20.5 4.9 %all-to-all-start.1 = ((bf16[8,64,8,128]{3,2,1,0:T(8,128)(2,1)}), bf16[8,64,8,128]{3,2,1,0:T(8,128)(2,1)S(1)}, u32[]{:S(2)}, u32[]{:S(2)}) async-start(bf16[8,64,8,128]{3,2,1,0:T(8,128)(2,1)} %bitcast.7), calls=%async_computation.1 | async-start | bytes 2097152 | tf_op jit(solution)/shard_map/all_to_all | solution.py:277
  25.5 0.1 reshape.64
  25.7 0.1 broadcast_in_dim.21
  25.8 0.1 broadcast_in_dim.22
  25.9 0.4 copy.10
  26.3 0.3 bitcast_select_fusion.mix_ref
  26.7 1.0 %spread.1.spread_ref = bf16[16,384,128]{2,1,0:T(8,128)(2,1)S(1)} custom-call(f32[2048,8]{1,0:T(8,128)S(1)} %bitcast_select_fusion.mix_ref), custom_call_target="tpu_custom_call" | custom-call | tf_op jit(solution)/shard_map/spread/pallas_call | solution.py:180
  27.7 0.8 %shard_map.87 = (f32[32,64,128]{2,1,0:T(8,128)S(1)}, f32[24,64,128]{2,1,0:T(8,128)S(1)}) custom-call(s32[3]{0:T(128)S(1)} %pad_add_fusion.place_ref.refs_0_, f32[1024,128]{1,0:T(8,128)S(1)} %get-tuple-element.32.own_ref.refs_5_, f32[256,128]{1,0:T(8,128)S(1)} %collective-permute-done.side_ref.refs_2_), custom_call_target="tpu_custom_call" | custom-call | tf_op jit(solution)/shard_map/pallas_call | solution.py:314
  28.5 0.9 %copy-done.2 = f32[24,64,128]{2,1,0:T(8,128)} copy-done((f32[24,64,128]{2,1,0:T(8,128)}, f32[24,64,128]{2,1,0:T(8,128)S(1)}, u32[]{:S(2)}) %copy-start.2) | copy-done | bytes 786456
  29.4 2.3 %shard_map.88.refs_4_ = f32[32,64,128]{2,1,0:T(8,128)S(1)} custom-call(s32[3]{0:T(128)S(1)} %pad_add_fusion.place_ref.refs_0_, f32[32,64,128]{2,1,0:T(8,128)S(1)} %get-tuple-element.36.own_sums_ref), custom_call_target="tpu_custom_call" | custom-call | tf_op jit(solution)/shard_map/pallas_call | solution.py:314
  31.8 1.0 %copy-done = f32[32,64,128]{2,1,0:T(8,128)} copy-done((f32[32,64,128]{2,1,0:T(8,128)}, f32[32,64,128]{2,1,0:T(8,128)S(1)}, u32[]{:S(2)}) %copy-start) | copy-done | bytes 1048600
  32.8 5.3 %all-to-all-done.1 = bf16[8,64,8,128]{3,2,1,0:T(8,128)(2,1)S(1)} async-done(((bf16[8,64,8,128]{3,2,1,0:T(8,128)(2,1)}), bf16[8,64,8,128]{3,2,1,0:T(8,128)(2,1)S(1)}, u32[]{:S(2)}, u32[]{:S(2)}) %all-to-all-start.1) | async-done | bytes 1048608 | tf_op jit(solution)/shard_map/all_to_all | solution.py:277
  38.0 4.8 %mix.1 = (f32[1024,128]{1,0:T(8,128)S(1)}, f32[256,128]{1,0:T(8,128)S(1)}, f32[16,8,128]{2,1,0:T(8,128)S(1)}) custom-call(s32[3]{0:T(128)S(1)} %pad_add_fusion.place_ref.refs_0_, s32[256]{0:T(256)S(1)} %bitcast.15, bf16[512,8,128]{2,1,0:T(8,128)(2,1)S(1)} %bitcast.14, bf16[16,384,128]{2,1,0:T(8,128)(2,1)S(1)} %spread.1.spread_ref, ...), custom_call_target="tpu_custom_call" | custom-call | tf_op jit(solution)/shard_map/mix/pallas_call | solution.py:253
  42.9 1.3 %collective-permute-done.3.refs_2_.refs_4_ = f32[256,128]{1,0:T(8,128)S(1)} collective-permute-done((f32[256,128]{1,0:T(8,128)S(1)}, f32[256,128]{1,0:T(8,128)S(1)}, u32[]{:S(2)}, u32[]{:S(2)}) %collective-permute-start.3) | collective-permute-done | bytes 131104 | tf_op jit(solution)/shard_map/ppermute | solution.py:650
  44.3 0.6 shard_map.91
  44.8 1.5 %collective-permute-start.6 = (f32[20,4,128]{2,1,0:T(4,128)S(1)}, f32[20,4,128]{2,1,0:T(4,128)S(1)}, u32[]{:S(2)}, u32[]{:S(2)}) collective-permute-start(f32[20,4,128]{2,1,0:T(4,128)S(1)} %get-tuple-element.50), channel_id=1, source_target_pairs={{0,2},{2,0},{4,6},{6,4},{8,10},{10,8},{12,14},{14,12},{1,3},{3,1},... | collective-permute-start | bytes 122888 | tf_op jit(solution)/shard_map/ppermute | solution.py:667
  46.4 3.1 %collective-permute-start.7 = (f32[20,4,128]{2,1,0:T(4,128)S(1)}, f32[20,4,128]{2,1,0:T(4,128)S(1)}, u32[]{:S(2)}, u32[]{:S(2)}) collective-permute-start(f32[20,4,128]{2,1,0:T(4,128)S(1)} %get-tuple-element.51), channel_id=1, source_target_pairs={{2,4},{4,2},{6,8},{8,6},{10,12},{12,10},{3,5},{5,3},{7,9},{9,7},{1... | collective-permute-start | bytes 122888 | tf_op jit(solution)/shard_map/ppermute | solution.py:667
  49.4 0.6 shard_map.90
  50.1 6.0 %collective-permute-start.5 = (f32[21,4,128]{2,1,0:T(4,128)S(1)}, f32[21,4,128]{2,1,0:T(4,128)S(1)}, u32[]{:S(2)}, u32[]{:S(2)}) collective-permute-start(f32[21,4,128]{2,1,0:T(4,128)S(1)} %get-tuple-element.46), channel_id=1, source_target_pairs={{2,4},{4,2},{6,8},{8,6},{10,12},{12,10},{3,5},{5,3},{7,9},{9,7},{1... | collective-permute-start | bytes 129032 | tf_op jit(solution)/shard_map/ppermute | solution.py:667
  56.1 1.4 %shard_map.89 = (f32[48,64,128]{2,1,0:T(8,128)S(1)}, f32[1024,128]{1,0:T(8,128)}, f32[64,128]{1,0:T(8,128)S(1)}) custom-call(s32[3]{0:T(128)S(1)} %pad_add_fusion.place_ref.refs_0_, f32[1024,128]{1,0:T(8,128)S(1)} %get-tuple-element.39.refs_1_.refs_3_, f32[256,128]{1,0:T(8,128)S(1)} %collective-permute-done.3.refs_2_.refs_4_, f32[24,64,128]{2,1,0:T(8,128)S(1)} %copy-done.3), custom_call_target="tpu_custom_call" | custom-call | tf_op jit(solution)/shard_map/pallas_call | solution.py:314
  57.5 0.6 shard_map.92
  58.2 1.6 %collective-permute-start.8 = (f32[72,128]{1,0:T(8,128)S(1)}, f32[72,128]{1,0:T(8,128)S(1)}, u32[]{:S(2)}, u32[]{:S(2)}) collective-permute-start(f32[72,128]{1,0:T(8,128)S(1)} %get-tuple-element.56), channel_id=1, source_target_pairs={{0,1},{1,0},{2,3},{3,2},{4,5},{5,4},{6,7},{7,6},{8,9},{9,8},{10,11... | collective-permute-start | bytes 110600 | tf_op jit(solution)/shard_map/ppermute | solution.py:672
  59.7 4.6 %shard_map.93 = (f32[48,64,128]{2,1,0:T(8,128)S(1)}, f32[48,64,128]{2,1,0:T(8,128)S(1)}, f32[72,128]{1,0:T(8,128)S(1)}) custom-call(s32[3]{0:T(128)S(1)} %pad_add_fusion.place_ref.refs_0_, f32[21,4,128]{2,1,0:T(4,128)S(1)} %collective-permute-done.4.refs_1_, f32[21,4,128]{2,1,0:T(4,128)S(1)} %collective-permute-done.5.refs_2_, ...), custom_call_target="tpu_custom_call" | custom-call | tf_op jit(solution)/shard_map/pallas_call | solution.py:314
  64.3 3.7 %shard_map.94 = f32[3,16,64,128]{3,2,1,0:T(8,128)} custom-call(s32[3]{0:T(128)S(1)} %pad_add_fusion.place_ref.refs_0_, f32[48,64,128]{2,1,0:T(8,128)S(1)} %get-tuple-element.54.refs_1_, f32[48,64,128]{2,1,0:T(8,128)S(1)} %get-tuple-element.55.refs_2_, f32[1024,128]{1,0:T(8,128)S(1)} %get-tuple-element.39.refs_1_.refs_3_, ...), custom_call_target="tpu_custom_call" | custom-call | tf_op jit(solution)/shard_map/pallas_call | solution.py:314
  (22 shorter events, 0.3 us)
Async XLA Ops:
  3.6 14.9 %collective-permute-start.2 = (bf16[128,8,128]{2,1,0:T(8,128)(2,1)S(1)}, bf16[128,8,128]{2,1,0:T(8,128)(2,1)S(1)}, u32[]{:S(2)}, u32[]{:S(2)}) collective-permute-start(bf16[128,8,128]{2,1,0:T(8,128)(2,1)S(1)} %get-tuple-element.35.refs_1_), channel_id=1, source_target_pairs={{0,8},{2,10},{4,12},{6,14},{8,0},{10,2},{12,4},{14,6},{1,9},{3,11}... | collective-permute-start | bytes 786440 | tf_op jit(solution)/shard_map/ppermute | solution.py:287
  6.3 1.3 %collective-permute-start = (f32[256,128]{1,0:T(8,128)S(1)}, f32[256,128]{1,0:T(8,128)S(1)}, u32[]{:S(2)}, u32[]{:S(2)}) collective-permute-start(f32[256,128]{1,0:T(8,128)S(1)} %get-tuple-element.33), channel_id=1, source_target_pairs={{0,16},{16,0},{1,17},{17,1},{2,18},{18,2},{3,19},{19,3},{4,20},{20... | collective-permute-start | bytes 393224 | tf_op jit(solution)/shard_map/ppermute | solution.py:650
  8.6 9.9 %collective-permute-start.1 = (f32[64,128]{1,0:T(8,128)S(1)}, f32[64,128]{1,0:T(8,128)S(1)}, u32[]{:S(2)}, u32[]{:S(2)}) collective-permute-start(f32[64,128]{1,0:T(8,128)S(1)} %shard_map.86), channel_id=1, source_target_pairs={{0,1},{1,0},{2,3},{3,2},{4,5},{5,4},{6,7},{7,6},{8,9},{9,8},{10,11... | collective-permute-start | bytes 98312 | tf_op jit(solution)/shard_map/ppermute | solution.py:672
  18.5 6.9 %copy-start.5 = (s32[1,1,1,128]{3,2,1,0:T(1,128)S(1)}, s32[1,1,1,128]{3,2,1,0:T(1,128)}, u32[]{:S(2)}) copy-start(s32[1,1,1,128]{3,2,1,0:T(1,128)} %param.11) | copy-start | bytes 1540
  18.5 7.4 %copy-start.4 = (f32[1,1,1,256,8,8]{3,5,4,2,1,0:T(8,128)S(1)}, f32[1,1,1,256,8,8]{3,5,4,2,1,0:T(8,128)}, u32[]{:S(2)}) copy-start(f32[1,1,1,256,8,8]{3,5,4,2,1,0:T(8,128)} %param.13) | copy-start | bytes 196612
  20.5 17.5 %all-to-all-start.1 = ((bf16[8,64,8,128]{3,2,1,0:T(8,128)(2,1)}), bf16[8,64,8,128]{3,2,1,0:T(8,128)(2,1)S(1)}, u32[]{:S(2)}, u32[]{:S(2)}) async-start(bf16[8,64,8,128]{3,2,1,0:T(8,128)(2,1)} %bitcast.7), calls=%async_computation.1 | async-start | bytes 2097152 | tf_op jit(solution)/shard_map/all_to_all | solution.py:277
  28.5 0.9 %copy-start.2 = (f32[24,64,128]{2,1,0:T(8,128)}, f32[24,64,128]{2,1,0:T(8,128)S(1)}, u32[]{:S(2)}) copy-start(f32[24,64,128]{2,1,0:T(8,128)S(1)} %get-tuple-element.41.refs_3_) | copy-start | bytes 2359300
  31.7 1.0 %copy-start = (f32[32,64,128]{2,1,0:T(8,128)}, f32[32,64,128]{2,1,0:T(8,128)S(1)}, u32[]{:S(2)}) copy-start(f32[32,64,128]{2,1,0:T(8,128)S(1)} %shard_map.88.refs_4_) | copy-start | bytes 3145732
  38.0 18.0 %copy-start.3 = (f32[24,64,128]{2,1,0:T(8,128)S(1)}, f32[24,64,128]{2,1,0:T(8,128)}, u32[]{:S(2)}) copy-start(f32[24,64,128]{2,1,0:T(8,128)} %copy-done.2) | copy-start | bytes 2359300
  42.9 16.9 %copy-start.1 = (f32[32,64,128]{2,1,0:T(8,128)S(1)}, f32[32,64,128]{2,1,0:T(8,128)}, u32[]{:S(2)}) copy-start(f32[32,64,128]{2,1,0:T(8,128)} %copy-done) | copy-start | bytes 3145732
  42.9 1.4 %collective-permute-start.3 = (f32[256,128]{1,0:T(8,128)S(1)}, f32[256,128]{1,0:T(8,128)S(1)}, u32[]{:S(2)}, u32[]{:S(2)}) collective-permute-start(f32[256,128]{1,0:T(8,128)S(1)} %get-tuple-element.40), channel_id=1, source_target_pairs={{0,16},{16,0},{1,17},{17,1},{2,18},{18,2},{3,19},{19,3},{4,20},{20... | collective-permute-start | bytes 393224 | tf_op jit(solution)/shard_map/ppermute | solution.py:650
  44.8 12.6 %collective-permute-start.6 = (f32[20,4,128]{2,1,0:T(4,128)S(1)}, f32[20,4,128]{2,1,0:T(4,128)S(1)}, u32[]{:S(2)}, u32[]{:S(2)}) collective-permute-start(f32[20,4,128]{2,1,0:T(4,128)S(1)} %get-tuple-element.50), channel_id=1, source_target_pairs={{0,2},{2,0},{4,6},{6,4},{8,10},{10,8},{12,14},{14,12},{1,3},{3,1},... | collective-permute-start | bytes 122888 | tf_op jit(solution)/shard_map/ppermute | solution.py:667
  46.4 11.1 %collective-permute-start.7 = (f32[20,4,128]{2,1,0:T(4,128)S(1)}, f32[20,4,128]{2,1,0:T(4,128)S(1)}, u32[]{:S(2)}, u32[]{:S(2)}) collective-permute-start(f32[20,4,128]{2,1,0:T(4,128)S(1)} %get-tuple-element.51), channel_id=1, source_target_pairs={{2,4},{4,2},{6,8},{8,6},{10,12},{12,10},{3,5},{5,3},{7,9},{9,7},{1... | collective-permute-start | bytes 122888 | tf_op jit(solution)/shard_map/ppermute | solution.py:667
  50.0 9.7 %collective-permute-start.4 = (f32[21,4,128]{2,1,0:T(4,128)S(1)}, f32[21,4,128]{2,1,0:T(4,128)S(1)}, u32[]{:S(2)}, u32[]{:S(2)}) collective-permute-start(f32[21,4,128]{2,1,0:T(4,128)S(1)} %get-tuple-element.45), channel_id=1, source_target_pairs={{0,2},{2,0},{4,6},{6,4},{8,10},{10,8},{12,14},{14,12},{1,3},{3,1},... | collective-permute-start | bytes 129032 | tf_op jit(solution)/shard_map/ppermute | solution.py:667
  50.1 9.6 %collective-permute-start.5 = (f32[21,4,128]{2,1,0:T(4,128)S(1)}, f32[21,4,128]{2,1,0:T(4,128)S(1)}, u32[]{:S(2)}, u32[]{:S(2)}) collective-permute-start(f32[21,4,128]{2,1,0:T(4,128)S(1)} %get-tuple-element.46), channel_id=1, source_target_pairs={{2,4},{4,2},{6,8},{8,6},{10,12},{12,10},{3,5},{5,3},{7,9},{9,7},{1... | collective-permute-start | bytes 129032 | tf_op jit(solution)/shard_map/ppermute | solution.py:667
  58.2 6.2 %collective-permute-start.8 = (f32[72,128]{1,0:T(8,128)S(1)}, f32[72,128]{1,0:T(8,128)S(1)}, u32[]{:S(2)}, u32[]{:S(2)}) collective-permute-start(f32[72,128]{1,0:T(8,128)S(1)} %get-tuple-element.56), channel_id=1, source_target_pairs={{0,1},{1,0},{2,3},{3,2},{4,5},{5,4},{6,7},{7,6},{8,9},{9,8},{10,11... | collective-permute-start | bytes 110600 | tf_op jit(solution)/shard_map/ppermute | solution.py:672

commit v6 on v5

--- a/solution.py
+++ b/solution.py
@@ -69,11 +69,11 @@
 
 
 def prepare_kernel(
-    half_ref, place_ref, moving_hbm, fixed_hbm, owner_hbm, ident_hbm,
-    blocks_ref, request_ref, flat_ref, image_ref, side_ref, face_ref,
-    moving_ref, fixed_ref, owner_ref, ident_ref, wide, sems,
+    half_ref, moving_hbm, owner_hbm, ident_hbm,
+    blocks_ref, request_ref, flat_ref,
+    moving_ref, owner_ref, ident_ref, wide, sems,
 ):
-    pairs = [(owner_hbm, owner_ref), (ident_hbm, ident_ref), (moving_hbm, moving_ref), (fixed_hbm, fixed_ref)]
+    pairs = [(owner_hbm, owner_ref), (ident_hbm, ident_ref), (moving_hbm, moving_ref)]
     copies = [pltpu.make_async_copy(source, target, sems.at[i]) for i, (source, target) in enumerate(pairs)]
     for copy in copies:
         copy.start()
@@ -110,13 +110,30 @@
         return 0
 
     lax.fori_loop(0, GROUPS, group, 0, unroll=4)
-    copies[3].wait()
+
+
+def image_kernel(place_ref, fixed_hbm, image_ref, side_ref, face_ref, fixed_ref, sem):
+    copy = pltpu.make_async_copy(fixed_hbm, fixed_ref, sem)
+    copy.start()
+    copy.wait()
     for z in range(NZ):
         image_ref[z * NY : (z + 1) * NY, :] = fixed_ref[z].astype(F32)
     outer(place_ref, image_ref, side_ref, face_ref)
 
 
-def prepare(half, place, moving, fixed, owner, ident, groups, capacity):
+def widen(place, fixed):
+    return pl.pallas_call(
+        image_kernel,
+        out_shape=OUTER,
+        in_specs=[SMEM, pl.BlockSpec(memory_space=pltpu.HBM)],
+        out_specs=(VMEM,) * 3,
+        scratch_shapes=[pltpu.VMEM((NZ, NY, NX), BF16), pltpu.SemaphoreType.DMA],
+        compiler_params=pltpu.CompilerParams(vmem_limit_bytes=LIMIT),
+        name="image",
+    )(place, pltpu.with_memory_space_constraint(fixed, pltpu.HBM))
+
+
+def prepare(half, moving, owner, ident, groups, capacity):
     holders = groups // 2
     hbm = pl.BlockSpec(memory_space=pltpu.HBM)
     return pl.pallas_call(
@@ -125,21 +142,19 @@
             jax.ShapeDtypeStruct((BLOCKS, VZ, BV), BF16),
             jax.ShapeDtypeStruct((holders, 1, 2 * capacity), jnp.int32),
             jax.ShapeDtypeStruct((1, SLOTS), jnp.int32),
-        )
-        + OUTER,
-        in_specs=[SMEM, SMEM, hbm, hbm, hbm, hbm],
-        out_specs=(VMEM,) * 6,
+        ),
+        in_specs=[SMEM, hbm, hbm, hbm],
+        out_specs=(VMEM,) * 3,
         scratch_shapes=[
-            pltpu.VMEM((NZ, NY, NX), BF16),
             pltpu.VMEM((NZ, NY, NX), BF16),
             pltpu.VMEM((1, SLOTS), jnp.int32),
             pltpu.VMEM((1, SLOTS), jnp.int32),
             pltpu.VMEM((NZ * NY, NX), F32),
-            pltpu.SemaphoreType.DMA((4,)),
+            pltpu.SemaphoreType.DMA((3,)),
         ],
         compiler_params=pltpu.CompilerParams(vmem_limit_bytes=LIMIT),
         name="prepare",
-    )(half, place, *[pltpu.with_memory_space_constraint(a, pltpu.HBM) for a in (moving, fixed, owner, ident)])
+    )(half, *[pltpu.with_memory_space_constraint(a, pltpu.HBM) for a in (moving, owner, ident)])
 
 
 def pick_kernel(capacity, request_ref, near_ref, far_ref, out_ref):
@@ -277,22 +292,21 @@
     return lax.all_to_all(array, BRICKS, split_axis=0, concat_axis=0, tiled=True, axis_index_groups=halves)
 
 
-def ask(place, moving, fixed, owners, block_ids):
+def ask(moving, owners, block_ids):
     rows_gy = lax.axis_size("gy")
     groups, capacity, _ = halves_of_gy()
     half = (lax.axis_index("gy") >= rows_gy // 2).astype(jnp.int32).reshape(1)
-    near, request, flat, *image = prepare(
-        half, place, moving, fixed, owners.reshape(1, SLOTS), block_ids.reshape(1, SLOTS), groups, capacity
-    )
+    near, request, flat = prepare(half, moving, owners.reshape(1, SLOTS), block_ids.reshape(1, SLOTS), groups, capacity)
     far = lax.ppermute(near, "gy", [(i, (i + rows_gy // 2) % rows_gy) for i in range(rows_gy)])
     request = exchange_in_half(request)
-    return request, near, far, flat.reshape(-1), image
+    return request, near, far, flat.reshape(-1)
 
 
 def answer(request, near, far):
     groups, capacity, _ = halves_of_gy()
     picked = pick(request, near, far, capacity).reshape(groups // 2, 2 * capacity, VZ, BV)
-    return exchange_in_half(picked).reshape(groups * capacity, VZ, BV)
+    received = exchange_in_half(picked)
+    return received.reshape(groups * capacity, VZ, BV)
 
 
 def spread_weights(counts, mix_z):
@@ -631,7 +645,7 @@
         return [pltpu.make_async_copy(force_ref.at[d, rows], force_hbm.at[d, rows], sems.at[d, group]) for d in range(3)]
 
     for group in range(NZ // RAD):
-        lax.fori_loop(group * RAD, (group + 1) * RAD, plane, 0)
+        lax.fori_loop(group * RAD, (group + 1) * RAD, plane, 0, unroll=2)
         for copy in out(group):
             copy.start()
     for group in range(NZ // RAD):
@@ -687,11 +701,11 @@
 def per_device(fixed, moving, owners, block_ids, counts, mix_yx, mix_z):
     place = jnp.stack([lax.axis_index("gz"), lax.axis_index("gy") % 2, lax.axis_index("gx") % 2]).astype(jnp.int32)
     count = len(pairings(lax.axis_size("gx")))
-    request, near, far, flat, (image, image_side, image_face) = ask(place, moving, fixed, owners, block_ids)
+    request, near, far, flat = ask(moving, owners, block_ids)
+    image, image_side, image_face = widen(place, fixed)
     image_side = exchange_planes(image_side)
     image_packed = call(pack_kernel, (array(NY, NX),) * count, place, image, image_side)
     image_packed = exchange_columns(image_packed)
-    request, image_packed = lax.optimization_barrier((request, image_packed))
     received = answer(request, near, far)
     image_sent = rows_to_send(place, image_face, image_side, *image_packed)
     image_halos = exchange_rows(image_sent)

time: 68.3 us -> 72.2 us (1.057)
  waiting for transfers between devices: 7.99 us -> 11 us
  blocking collectives: 8.31 us -> 9.31 us
    ppermute x1, waiting for transfers between devices: 0.01 us -> 2.69 us  [ask(): lax.ppermute(near, 'gy', [(i, (i + rows_gy // 2) % rows_gy) for i in rang...]
    ppermute x2, waiting for transfers between devices: 0.01 us -> 2.66 us  [exchange_columns(): return [lax.ppermute(c, 'gx', pairs) for c, pairs in zip(columns, along)]]
    pallas_call x0 -> x1, Pallas kernels: none -> 1.55 us  [widen(): pl.pallas_call(image_kernel, out_shape=OUTER, in_specs=[SMEM, pl.BlockSpe...]
    ppermute x2, waiting for transfers between devices: 2.68 us -> 1.34 us  [exchange_planes(): return lax.ppermute(side, 'gz', pairings(lax.axis_size('gz'))[0])]
    all_to_all x1, waiting for transfers between devices: 5.28 us -> 4.27 us  [exchange_in_half(): lax.all_to_all(array, BRICKS, split_axis=0, concat_axis=0, tiled=True, ax...]
    all_to_all x1, blocking collectives: 8.31 us -> 9.31 us  [exchange_in_half(): lax.all_to_all(array, BRICKS, split_axis=0, concat_axis=0, tiled=True, ax...]
  transfers between devices with their start and end apart: 10 -> 10, of which waited for: 3 -> 4; matrix products, arithmetic and copies ran while one was open for 2% -> 2% of each run, Pallas kernels for 18% -> 19%
where the time goes in v6:
time: 72.2 us; the launch traced here: 71.9 us
  Pallas kernels  26.6 us (37%)
  starting transfers between devices  21 us (29%)
  waiting for transfers between devices  11 us (15%)
  blocking collectives  9.31 us (13%)
  local copies, waits for them, and re-layouts  2.77 us (4%)
  between operations  0.87 us (1%)
    pallas_call x9, Pallas kernels, call(): pl.pallas_call(kernel, out_shape=outs, in_specs=[SMEM] + [VMEM] * (len(ar...  15 us
    ppermute x4, starting transfers between devices, exchange_rows(): lax.ppermute(s, 'gy', pairs)  10.8 us
    all_to_all x1, blocking collectives, exchange_in_half(): lax.all_to_all(array, BRICKS, split_axis=0, concat_axis=0, tiled=True, ax...  9.31 us
    pallas_call x1, Pallas kernels, mix(): pl.pallas_call(mix_kernel, out_shape=OUTER, in_specs=[SMEM, SMEM, VMEM, V...  4.81 us
    all_to_all x1, starting transfers between devices, exchange_in_half(): lax.all_to_all(array, BRICKS, split_axis=0, concat_axis=0, tiled=True, ax...  4.44 us
    all_to_all x1, waiting for transfers between devices, exchange_in_half(): lax.all_to_all(array, BRICKS, split_axis=0, concat_axis=0, tiled=True, ax...  4.27 us
    ppermute x2, starting transfers between devices, exchange_columns(): return [lax.ppermute(c, 'gx', pairs) for c, pairs in zip(columns, along)]  2.98 us
    ppermute x1, waiting for transfers between devices, ask(): lax.ppermute(near, 'gy', [(i, (i + rows_gy // 2) % rows_gy) for i in rang...  2.69 us
  transfers between devices with their start and end apart: 10, of which 4 were waited for; matrix products, arithmetic and copies ran while one was open for 2% of the time, Pallas kernels for 19%

profile of v6, /device:TPU:4, one launch (start us, length us, event | category | flops | bytes accessed | tf_op | source)
XLA Modules:
  0.0 71.9 jit_solution(438467951154945472)
XLA Ops:
  0.6 2.3 %prepare.1 = (bf16[128,8,128]{2,1,0:T(8,128)(2,1)S(1)}, s32[8,1,64]{2,1,0:T(1,128)S(1)}, s32[1,256]{1,0:T(1,128)S(1)}) custom-call(s32[1]{0:T(128)} %bitcast.3.half_ref, bf16[16,64,128]{2,1,0:T(8,128)(2,1)} %moving_hbm.1, s32[1,256]{1,0:T(1,128)} %bitcast.17, s32[1,256]{1,0:T(1,128)} %bitcast.18), custom_call_target="tpu_custom_call" | custom-call | tf_op jit(solution)/shard_map/prepare/pallas_call | solution.py:139
  2.9 2.7 %collective-permute-start = (bf16[128,8,128]{2,1,0:T(8,128)(2,1)S(1)}, bf16[128,8,128]{2,1,0:T(8,128)(2,1)S(1)}, u32[]{:S(2)}, u32[]{:S(2)}) collective-permute-start(bf16[128,8,128]{2,1,0:T(8,128)(2,1)S(1)} %get-tuple-element.30.refs_1_), channel_id=1, source_target_pairs={{0,8},{2,10},{4,12},{6,14},{8,0},{10,2},{12,4},{14,6},{1,9},{3,11}... | collective-permute-start | bytes 786440 | tf_op jit(solution)/shard_map/ppermute | solution.py:300
  5.6 9.3 %all_to_all.10.refs_0_ = s32[8,1,64]{2,1,0:T(1,128)S(1)} all-to-all(s32[8,1,64]{2,1,0:T(1,128)S(1)} %get-tuple-element.29), channel_id=1, replica_groups={{0,1,2,3,4,5,6,7},{8,9,10,11,12,13,14,15},{16,17,18,19,20,21,22,23},{24..., dimensions={0} | all-to-all | bytes 4096 | tf_op jit(solution)/shard_map/all_to_all | solution.py:292
  14.9 2.7 %collective-permute-done.refs_2_ = bf16[128,8,128]{2,1,0:T(8,128)(2,1)S(1)} collective-permute-done((bf16[128,8,128]{2,1,0:T(8,128)(2,1)S(1)}, bf16[128,8,128]{2,1,0:T(8,128)(2,1)S(1)}, u32[]{:S(2)}, u32[]{:S(2)}) %collective-permute-start) | collective-permute-done | bytes 262176 | tf_op jit(solution)/shard_map/ppermute | solution.py:300
  17.6 2.0 %pick.1 = bf16[512,8,128]{2,1,0:T(8,128)(2,1)} custom-call(s32[8,1,64]{2,1,0:T(1,128)S(1)} %all_to_all.10.refs_0_, bf16[128,8,128]{2,1,0:T(8,128)(2,1)S(1)} %get-tuple-element.30.refs_1_, bf16[128,8,128]{2,1,0:T(8,128)(2,1)S(1)} %collective-permute-done.refs_2_), custom_call_target="tpu_custom_call" | custom-call | tf_op jit(solution)/shard_map/pick/pallas_call | solution.py:170
  19.5 4.4 %all-to-all-start.1 = ((bf16[8,64,8,128]{3,2,1,0:T(8,128)(2,1)}), bf16[8,64,8,128]{3,2,1,0:T(8,128)(2,1)S(1)}, u32[]{:S(2)}, u32[]{:S(2)}) async-start(bf16[8,64,8,128]{3,2,1,0:T(8,128)(2,1)} %bitcast.7), calls=%async_computation.1 | async-start | bytes 2097152 | tf_op jit(solution)/shard_map/all_to_all | solution.py:292
  24.1 1.5 %image.1 = (f32[1024,128]{1,0:T(8,128)S(1)}, f32[256,128]{1,0:T(8,128)S(1)}, f32[16,8,128]{2,1,0:T(8,128)S(1)}) custom-call(s32[3]{0:T(128)S(1)} %pad_add_fusion.place_ref.refs_0_, bf16[16,64,128]{2,1,0:T(8,128)(2,1)} %fixed_hbm.1), custom_call_target="tpu_custom_call" | custom-call | tf_op jit(solution)/shard_map/image/pallas_call | solution.py:125
  25.8 0.1 reshape.64
  26.1 0.1 broadcast_in_dim.22
  26.2 0.4 copy.10
  26.6 0.3 bitcast_select_fusion.mix_ref
  26.9 1.0 %spread.1.spread_ref = bf16[16,384,128]{2,1,0:T(8,128)(2,1)S(1)} custom-call(f32[2048,8]{1,0:T(8,128)S(1)} %bitcast_select_fusion.mix_ref), custom_call_target="tpu_custom_call" | custom-call | tf_op jit(solution)/shard_map/spread/pallas_call | solution.py:195
  28.0 0.8 %shard_map.86 = (f32[32,64,128]{2,1,0:T(8,128)S(1)}, f32[24,64,128]{2,1,0:T(8,128)S(1)}) custom-call(s32[3]{0:T(128)S(1)} %pad_add_fusion.place_ref.refs_0_, f32[1024,128]{1,0:T(8,128)S(1)} %get-tuple-element.31.own_ref.refs_5_, f32[256,128]{1,0:T(8,128)S(1)} %collective-permute-done.1.side_ref.refs_2_), custom_call_target="tpu_custom_call" | custom-call | tf_op jit(solution)/shard_map/pallas_call | solution.py:328
  28.8 0.9 %copy-done.2 = f32[24,64,128]{2,1,0:T(8,128)} copy-done((f32[24,64,128]{2,1,0:T(8,128)}, f32[24,64,128]{2,1,0:T(8,128)S(1)}, u32[]{:S(2)}) %copy-start.2) | copy-done | bytes 786456
  29.7 2.3 %shard_map.87.refs_4_ = f32[32,64,128]{2,1,0:T(8,128)S(1)} custom-call(s32[3]{0:T(128)S(1)} %pad_add_fusion.place_ref.refs_0_, f32[32,64,128]{2,1,0:T(8,128)S(1)} %get-tuple-element.33.own_sums_ref), custom_call_target="tpu_custom_call" | custom-call | tf_op jit(solution)/shard_map/pallas_call | solution.py:328
  32.0 1.0 %copy-done = f32[32,64,128]{2,1,0:T(8,128)} copy-done((f32[32,64,128]{2,1,0:T(8,128)}, f32[32,64,128]{2,1,0:T(8,128)S(1)}, u32[]{:S(2)}) %copy-start) | copy-done | bytes 1048600
  33.1 4.3 %all-to-all-done.1 = bf16[8,64,8,128]{3,2,1,0:T(8,128)(2,1)S(1)} async-done(((bf16[8,64,8,128]{3,2,1,0:T(8,128)(2,1)}), bf16[8,64,8,128]{3,2,1,0:T(8,128)(2,1)S(1)}, u32[]{:S(2)}, u32[]{:S(2)}) %all-to-all-start.1) | async-done | bytes 1048608 | tf_op jit(solution)/shard_map/all_to_all | solution.py:292
  37.3 4.8 %mix.1 = (f32[1024,128]{1,0:T(8,128)S(1)}, f32[256,128]{1,0:T(8,128)S(1)}, f32[16,8,128]{2,1,0:T(8,128)S(1)}) custom-call(s32[3]{0:T(128)S(1)} %pad_add_fusion.place_ref.refs_0_, s32[256]{0:T(256)S(1)} %bitcast.15, bf16[512,8,128]{2,1,0:T(8,128)(2,1)S(1)} %bitcast.14, bf16[16,384,128]{2,1,0:T(8,128)(2,1)S(1)} %spread.1.spread_ref, ...), custom_call_target="tpu_custom_call" | custom-call | tf_op jit(solution)/shard_map/mix/pallas_call | solution.py:268
  42.2 1.3 %collective-permute-done.2.refs_2_.refs_4_ = f32[256,128]{1,0:T(8,128)S(1)} collective-permute-done((f32[256,128]{1,0:T(8,128)S(1)}, f32[256,128]{1,0:T(8,128)S(1)}, u32[]{:S(2)}, u32[]{:S(2)}) %collective-permute-start.2) | collective-permute-done | bytes 131104 | tf_op jit(solution)/shard_map/ppermute | solution.py:664
  43.6 0.6 shard_map.91
  44.1 1.5 %collective-permute-start.6 = (f32[20,4,128]{2,1,0:T(4,128)S(1)}, f32[20,4,128]{2,1,0:T(4,128)S(1)}, u32[]{:S(2)}, u32[]{:S(2)}) collective-permute-start(f32[20,4,128]{2,1,0:T(4,128)S(1)} %get-tuple-element.46), channel_id=1, source_target_pairs={{0,2},{2,0},{4,6},{6,4},{8,10},{10,8},{12,14},{14,12},{1,3},{3,1},... | collective-permute-start | bytes 122888 | tf_op jit(solution)/shard_map/ppermute | solution.py:681
  45.7 3.2 %collective-permute-start.7 = (f32[20,4,128]{2,1,0:T(4,128)S(1)}, f32[20,4,128]{2,1,0:T(4,128)S(1)}, u32[]{:S(2)}, u32[]{:S(2)}) collective-permute-start(f32[20,4,128]{2,1,0:T(4,128)S(1)} %get-tuple-element.47), channel_id=1, source_target_pairs={{2,4},{4,2},{6,8},{8,6},{10,12},{12,10},{3,5},{5,3},{7,9},{9,7},{1... | collective-permute-start | bytes 122888 | tf_op jit(solution)/shard_map/ppermute | solution.py:681
  48.9 1.0 %shard_map.89 = f32[64,128]{1,0:T(8,128)S(1)} custom-call(s32[3]{0:T(128)S(1)} %pad_add_fusion.place_ref.refs_0_, f32[1024,128]{1,0:T(8,128)S(1)} %get-tuple-element.31.own_ref.refs_5_, f32[256,128]{1,0:T(8,128)S(1)} %collective-permute-done.1.side_ref.refs_2_), custom_call_target="tpu_custom_call" | custom-call | tf_op jit(solution)/shard_map/pallas_call | solution.py:328
  49.9 1.3 %collective-permute-start.3 = (f32[64,128]{1,0:T(8,128)S(1)}, f32[64,128]{1,0:T(8,128)S(1)}, u32[]{:S(2)}, u32[]{:S(2)}) collective-permute-start(f32[64,128]{1,0:T(8,128)S(1)} %shard_map.89), channel_id=1, source_target_pairs={{0,1},{1,0},{2,3},{3,2},{4,5},{5,4},{6,7},{7,6},{8,9},{9,8},{10,11... | collective-permute-start | bytes 98312 | tf_op jit(solution)/shard_map/ppermute | solution.py:686
  51.3 2.6 %collective-permute-done.3.refs_3_ = f32[64,128]{1,0:T(8,128)S(1)} collective-permute-done((f32[64,128]{1,0:T(8,128)S(1)}, f32[64,128]{1,0:T(8,128)S(1)}, u32[]{:S(2)}, u32[]{:S(2)}) %collective-permute-start.3) | collective-permute-done | bytes 32800 | tf_op jit(solution)/shard_map/ppermute | solution.py:686
  53.9 0.6 shard_map.90
  54.6 6.0 %collective-permute-start.5 = (f32[21,4,128]{2,1,0:T(4,128)S(1)}, f32[21,4,128]{2,1,0:T(4,128)S(1)}, u32[]{:S(2)}, u32[]{:S(2)}) collective-permute-start(f32[21,4,128]{2,1,0:T(4,128)S(1)} %get-tuple-element.42), channel_id=1, source_target_pairs={{2,4},{4,2},{6,8},{8,6},{10,12},{12,10},{3,5},{5,3},{7,9},{9,7},{1... | collective-permute-start | bytes 129032 | tf_op jit(solution)/shard_map/ppermute | solution.py:681
  60.5 1.4 %shard_map.88 = (f32[48,64,128]{2,1,0:T(8,128)S(1)}, f32[1024,128]{1,0:T(8,128)}, f32[64,128]{1,0:T(8,128)S(1)}) custom-call(s32[3]{0:T(128)S(1)} %pad_add_fusion.place_ref.refs_0_, f32[1024,128]{1,0:T(8,128)S(1)} %get-tuple-element.36.refs_1_.refs_3_, f32[256,128]{1,0:T(8,128)S(1)} %collective-permute-done.2.refs_2_.refs_4_, f32[24,64,128]{2,1,0:T(8,128)S(1)} %copy-done.3), custom_call_target="tpu_custom_call" | custom-call | tf_op jit(solution)/shard_map/pallas_call | solution.py:328
  62.0 0.6 shard_map.92
  62.6 1.6 %collective-permute-start.8 = (f32[72,128]{1,0:T(8,128)S(1)}, f32[72,128]{1,0:T(8,128)S(1)}, u32[]{:S(2)}, u32[]{:S(2)}) collective-permute-start(f32[72,128]{1,0:T(8,128)S(1)} %get-tuple-element.52), channel_id=1, source_target_pairs={{0,1},{1,0},{2,3},{3,2},{4,5},{5,4},{6,7},{7,6},{8,9},{9,8},{10,11... | collective-permute-start | bytes 110600 | tf_op jit(solution)/shard_map/ppermute | solution.py:686
  64.3 4.6 %shard_map.93 = (f32[48,64,128]{2,1,0:T(8,128)S(1)}, f32[48,64,128]{2,1,0:T(8,128)S(1)}, f32[72,128]{1,0:T(8,128)S(1)}) custom-call(s32[3]{0:T(128)S(1)} %pad_add_fusion.place_ref.refs_0_, f32[21,4,128]{2,1,0:T(4,128)S(1)} %collective-permute-done.4.refs_1_, f32[21,4,128]{2,1,0:T(4,128)S(1)} %collective-permute-done.5.refs_2_, ...), custom_call_target="tpu_custom_call" | custom-call | tf_op jit(solution)/shard_map/pallas_call | solution.py:328
  68.9 3.1 %shard_map.94 = f32[3,16,64,128]{3,2,1,0:T(8,128)} custom-call(s32[3]{0:T(128)S(1)} %pad_add_fusion.place_ref.refs_0_, f32[48,64,128]{2,1,0:T(8,128)S(1)} %get-tuple-element.50.refs_1_, f32[48,64,128]{2,1,0:T(8,128)S(1)} %get-tuple-element.51.refs_2_, f32[1024,128]{1,0:T(8,128)S(1)} %get-tuple-element.36.refs_1_.refs_3_, ...), custom_call_target="tpu_custom_call" | custom-call | tf_op jit(solution)/shard_map/pallas_call | solution.py:328
  (23 shorter events, 0.5 us)
Async XLA Ops:
  2.9 14.6 %collective-permute-start = (bf16[128,8,128]{2,1,0:T(8,128)(2,1)S(1)}, bf16[128,8,128]{2,1,0:T(8,128)(2,1)S(1)}, u32[]{:S(2)}, u32[]{:S(2)}) collective-permute-start(bf16[128,8,128]{2,1,0:T(8,128)(2,1)S(1)} %get-tuple-element.30.refs_1_), channel_id=1, source_target_pairs={{0,8},{2,10},{4,12},{6,14},{8,0},{10,2},{12,4},{14,6},{1,9},{3,11}... | collective-permute-start | bytes 786440 | tf_op jit(solution)/shard_map/ppermute | solution.py:300
  19.5 6.2 %copy-start.5 = (s32[1,1,1,128]{3,2,1,0:T(1,128)S(1)}, s32[1,1,1,128]{3,2,1,0:T(1,128)}, u32[]{:S(2)}) copy-start(s32[1,1,1,128]{3,2,1,0:T(1,128)} %param.11) | copy-start | bytes 1540
  19.5 6.6 %copy-start.4 = (f32[1,1,1,256,8,8]{3,5,4,2,1,0:T(8,128)S(1)}, f32[1,1,1,256,8,8]{3,5,4,2,1,0:T(8,128)}, u32[]{:S(2)}) copy-start(f32[1,1,1,256,8,8]{3,5,4,2,1,0:T(8,128)} %param.13) | copy-start | bytes 196612
  19.5 17.8 %all-to-all-start.1 = ((bf16[8,64,8,128]{3,2,1,0:T(8,128)(2,1)}), bf16[8,64,8,128]{3,2,1,0:T(8,128)(2,1)S(1)}, u32[]{:S(2)}, u32[]{:S(2)}) async-start(bf16[8,64,8,128]{3,2,1,0:T(8,128)(2,1)} %bitcast.7), calls=%async_computation.1 | async-start | bytes 2097152 | tf_op jit(solution)/shard_map/all_to_all | solution.py:292
  25.6 2.3 %collective-permute-start.1 = (f32[256,128]{1,0:T(8,128)S(1)}, f32[256,128]{1,0:T(8,128)S(1)}, u32[]{:S(2)}, u32[]{:S(2)}) collective-permute-start(f32[256,128]{1,0:T(8,128)S(1)} %get-tuple-element.32), channel_id=1, source_target_pairs={{0,16},{16,0},{1,17},{17,1},{2,18},{18,2},{3,19},{19,3},{4,20},{20... | collective-permute-start | bytes 393224 | tf_op jit(solution)/shard_map/ppermute | solution.py:664
  28.8 0.9 %copy-start.2 = (f32[24,64,128]{2,1,0:T(8,128)}, f32[24,64,128]{2,1,0:T(8,128)S(1)}, u32[]{:S(2)}) copy-start(f32[24,64,128]{2,1,0:T(8,128)S(1)} %get-tuple-element.38.refs_3_) | copy-start | bytes 2359300
  32.0 1.0 %copy-start = (f32[32,64,128]{2,1,0:T(8,128)}, f32[32,64,128]{2,1,0:T(8,128)S(1)}, u32[]{:S(2)}) copy-start(f32[32,64,128]{2,1,0:T(8,128)S(1)} %shard_map.87.refs_4_) | copy-start | bytes 3145732
  37.3 23.2 %copy-start.3 = (f32[24,64,128]{2,1,0:T(8,128)S(1)}, f32[24,64,128]{2,1,0:T(8,128)}, u32[]{:S(2)}) copy-start(f32[24,64,128]{2,1,0:T(8,128)} %copy-done.2) | copy-start | bytes 2359300
  42.1 22.1 %copy-start.1 = (f32[32,64,128]{2,1,0:T(8,128)S(1)}, f32[32,64,128]{2,1,0:T(8,128)}, u32[]{:S(2)}) copy-start(f32[32,64,128]{2,1,0:T(8,128)} %copy-done) | copy-start | bytes 3145732
  42.2 1.4 %collective-permute-start.2 = (f32[256,128]{1,0:T(8,128)S(1)}, f32[256,128]{1,0:T(8,128)S(1)}, u32[]{:S(2)}, u32[]{:S(2)}) collective-permute-start(f32[256,128]{1,0:T(8,128)S(1)} %get-tuple-element.37), channel_id=1, source_target_pairs={{0,16},{16,0},{1,17},{17,1},{2,18},{18,2},{3,19},{19,3},{4,20},{20... | collective-permute-start | bytes 393224 | tf_op jit(solution)/shard_map/ppermute | solution.py:664
  44.1 17.8 %collective-permute-start.6 = (f32[20,4,128]{2,1,0:T(4,128)S(1)}, f32[20,4,128]{2,1,0:T(4,128)S(1)}, u32[]{:S(2)}, u32[]{:S(2)}) collective-permute-start(f32[20,4,128]{2,1,0:T(4,128)S(1)} %get-tuple-element.46), channel_id=1, source_target_pairs={{0,2},{2,0},{4,6},{6,4},{8,10},{10,8},{12,14},{14,12},{1,3},{3,1},... | collective-permute-start | bytes 122888 | tf_op jit(solution)/shard_map/ppermute | solution.py:681
  45.7 16.3 %collective-permute-start.7 = (f32[20,4,128]{2,1,0:T(4,128)S(1)}, f32[20,4,128]{2,1,0:T(4,128)S(1)}, u32[]{:S(2)}, u32[]{:S(2)}) collective-permute-start(f32[20,4,128]{2,1,0:T(4,128)S(1)} %get-tuple-element.47), channel_id=1, source_target_pairs={{2,4},{4,2},{6,8},{8,6},{10,12},{12,10},{3,5},{5,3},{7,9},{9,7},{1... | collective-permute-start | bytes 122888 | tf_op jit(solution)/shard_map/ppermute | solution.py:681
  49.9 4.0 %collective-permute-start.3 = (f32[64,128]{1,0:T(8,128)S(1)}, f32[64,128]{1,0:T(8,128)S(1)}, u32[]{:S(2)}, u32[]{:S(2)}) collective-permute-start(f32[64,128]{1,0:T(8,128)S(1)} %shard_map.89), channel_id=1, source_target_pairs={{0,1},{1,0},{2,3},{3,2},{4,5},{5,4},{6,7},{7,6},{8,9},{9,8},{10,11... | collective-permute-start | bytes 98312 | tf_op jit(solution)/shard_map/ppermute | solution.py:686
  54.5 9.8 %collective-permute-start.4 = (f32[21,4,128]{2,1,0:T(4,128)S(1)}, f32[21,4,128]{2,1,0:T(4,128)S(1)}, u32[]{:S(2)}, u32[]{:S(2)}) collective-permute-start(f32[21,4,128]{2,1,0:T(4,128)S(1)} %get-tuple-element.41), channel_id=1, source_target_pairs={{0,2},{2,0},{4,6},{6,4},{8,10},{10,8},{12,14},{14,12},{1,3},{3,1},... | collective-permute-start | bytes 129032 | tf_op jit(solution)/shard_map/ppermute | solution.py:681
  54.6 9.7 %collective-permute-start.5 = (f32[21,4,128]{2,1,0:T(4,128)S(1)}, f32[21,4,128]{2,1,0:T(4,128)S(1)}, u32[]{:S(2)}, u32[]{:S(2)}) collective-permute-start(f32[21,4,128]{2,1,0:T(4,128)S(1)} %get-tuple-element.42), channel_id=1, source_target_pairs={{2,4},{4,2},{6,8},{8,6},{10,12},{12,10},{3,5},{5,3},{7,9},{9,7},{1... | collective-permute-start | bytes 129032 | tf_op jit(solution)/shard_map/ppermute | solution.py:681
  62.6 6.3 %collective-permute-start.8 = (f32[72,128]{1,0:T(8,128)S(1)}, f32[72,128]{1,0:T(8,128)S(1)}, u32[]{:S(2)}, u32[]{:S(2)}) collective-permute-start(f32[72,128]{1,0:T(8,128)S(1)} %get-tuple-element.52), channel_id=1, source_target_pairs={{0,1},{1,0},{2,3},{3,2},{4,5},{5,4},{6,7},{7,6},{8,9},{9,8},{10,11... | collective-permute-start | bytes 110600 | tf_op jit(solution)/shard_map/ppermute | solution.py:686

commit v7 on v6

--- a/solution.py
+++ b/solution.py
@@ -394,33 +394,33 @@
     return extended_planes(place_ref, own, side)
 
 
-def own_kernel(with_image, place_ref, own_ref, side_ref, *refs):
-    image_ref, sums_ref, *columns = refs
-    if with_image:
-        out_hbm, sem = columns.pop(0), columns.pop()
-        copy = pltpu.make_async_copy(own_ref, out_hbm, sem)
-        copy.start()
-
+def plane_sums(place_ref, refs, fields_of, sums_ref, columns=()):
     def rows_of(q, _):
         at = pl.multiple_of(q * VY, VY)
         rows = pl.ds(at, VY)
-        planes = own_planes(place_ref, own_ref, side_ref, at)
+        planes = [own_planes(place_ref, own_ref, side_ref, at) for own_ref, side_ref in refs]
         for k, column in enumerate(columns):
-            column[rows, :] = pack(place_ref, planes, k)
-        fields = [planes, [v * v for v in planes]]
-        if with_image:
-            fields.append([image_ref[p, rows, :] * v for p, v in enumerate(planes)])
-        else:
-            for p, v in enumerate(planes):
-                image_ref[p, rows, :] = v
-        for f, parts in enumerate(fields):
+            column[rows, :] = pack(place_ref, planes[0], k)
+        for f, parts in enumerate(fields_of(*planes)):
             for z, total in enumerate(window(parts, NZ)):
                 sums_ref[f * NZ + z, rows, :] = total
         return 0
 
     lax.fori_loop(0, NBY, rows_of, 0)
-    if with_image:
-        copy.wait()
+
+
+def own_kernel(place_ref, own_ref, side_ref, image_ref, image_side_ref, sums_ref, out_hbm, *rest):
+    columns, sem = rest[:-1], rest[-1]
+    copy = pltpu.make_async_copy(own_ref, out_hbm, sem)
+    copy.start()
+    plane_sums(
+        place_ref,
+        [(own_ref, side_ref), (image_ref, image_side_ref)],
+        lambda w, f: [w, [v * v for v in w], [u * v for u, v in zip(f, w)]],
+        sums_ref,
+        columns,
+    )
+    copy.wait()
 
 
 def columns_kernel(y_count, x_count, place_ref, *refs):
@@ -508,10 +508,6 @@
 LINES = (pltpu.VMEM((4, EY + VY, NX), F32),) * 3
 
 
-def image_sums_kernel(place_ref, own_sums_ref, out_ref, *lines):
-    brick_sums(2 * NZ, lambda i: (own_sums_ref[i], jnp.zeros((VY, NX), F32)), out_ref, *lines)
-
-
 def halo_sums(fields, outer_sums):
     for f, parts in enumerate(fields):
         for z, total in enumerate(window(parts, NZ)):
@@ -546,42 +542,64 @@
     return box
 
 
-def image_box_kernel(x_count, place_ref, sums_ref, image_ref, rows_ref, *refs):
+def image_values(out_ref, z, box, image):
+    mean = box[0] * (1.0 / COUNT)
+    out_ref[z] = mean
+    out_ref[NZ + z] = image - mean
+    out_ref[2 * NZ + z] = 1.0 / (box[1] * (1.0 / COUNT) - mean * mean + 1e-5)
+
+
+def image_early_kernel(x_count, place_ref, image_ref, side_ref, *refs):
+    packed, (out_ref, outer_ref, planes, sums_ref, edges, *lines) = refs[:x_count], refs[x_count:]
+    plane_sums(place_ref, [(image_ref, side_ref)], lambda f: [f, [v * v for v in f]], planes)
+    brick_sums(2 * NZ, lambda i: (planes[i], jnp.zeros((VY, NX), F32)), sums_ref, *lines)
+    for k in range(x_count):
+        table = edge_table(side_is_right(place_ref, k))
+        f = jnp.concatenate([packed[k][...], jnp.zeros((VY, NX), F32)], 0)
+        for i, field in enumerate([f, f * f]):
+            edges[2 * k + i] = split_dot(window_rows(field), table)
+
+    def plane(z, _):
+        box = [sums_ref[z], sums_ref[NZ + z]]
+        for f in range(2):
+            outer_ref[f * NZ + z] = outer_rows(box[f][:VY], box[f][NY - VY :])
+        box = add_edges(x_count, place_ref, z, box, edges, 2, 0)
+        image_values(out_ref, z, box, image_ref[pl.ds(pl.multiple_of(z * NY, NY), NY), :])
+        return 0
+
+    lax.fori_loop(0, NZ, plane, 0, unroll=2)
+
+
+def outer_rows(first, last):
+    return jnp.concatenate([first, last], 0)
+
+
+def image_late_kernel(x_count, place_ref, sums_ref, image_ref, rows_ref, *refs):
     halos, (out_ref, edges, outer_sums) = refs[:x_count], refs[x_count:]
     for k in range(x_count):
         table = edge_table(side_is_right(place_ref, k))
         f = halos[k][...]
         for i, field in enumerate([f, f * f]):
-            edges[2 * k + i] = split_dot(window_rows(field), table)
+            rows = window_rows(field)
+            edges[2 * k + i] = split_dot(outer_rows(rows[:VY], rows[NY - VY :]), table)
     f = [rows_ref[p] for p in range(EZ)]
     halo_sums([f, [v * v for v in f]], outer_sums)
     outer = split_dot(halo_part(outer_sums[...].reshape(2 * NZ * VY, NX)), near_columns())
     outer_sums[...] = outer.reshape(2 * NZ, VY, NX)
     first = iota((VY, NX), 0) < RAD
-    scale = 1.0 / COUNT
 
     def plane(z, _):
         box = []
         for f in range(2):
-            total, rows = sums_ref[f * NZ + z], outer_sums[f * NZ + z]
-            box.append(
-                jnp.concatenate(
-                    [
-                        total[:VY] + jnp.where(first, rows, 0.0),
-                        total[VY : NY - VY],
-                        total[NY - VY :] + jnp.where(first, 0.0, rows),
-                    ],
-                    0,
-                )
-            )
+            rows = outer_sums[f * NZ + z]
+            before = sums_ref[f * NZ + z, :VY, :] + jnp.where(first, rows, 0.0)
+            box.append(outer_rows(before, sums_ref[f * NZ + z, VY:, :] + jnp.where(first, 0.0, rows)))
         box = add_edges(x_count, place_ref, z, box, edges, 2, 0)
-        mean = box[0] * scale
-        out_ref[z] = mean
-        out_ref[NZ + z] = image_ref[pl.ds(pl.multiple_of(z * NY, NY), NY), :] - mean
-        out_ref[2 * NZ + z] = 1.0 / (box[1] * scale - mean * mean + 1e-5)
+        at = pl.multiple_of(z * NY, NY)
+        image_values(out_ref, z, box, outer_rows(image_ref[pl.ds(at, VY), :], image_ref[pl.ds(at + NY - VY, VY), :]))
         return 0
 
-    lax.fori_loop(0, NZ, plane, 0, unroll=2)
+    lax.fori_loop(0, NZ, plane, 0, unroll=4)
 
 
 def finish_kernel(y_count, x_count, place_ref, *refs):
@@ -589,14 +607,14 @@
     sums_ref, image_ref, own_sums_ref, rows_ref, box_ref, out_ref = refs[:6]
     columns, (image_rows, edges, image_outer, outer_sums, *lines) = refs[6 : 6 + x_count], refs[6 + x_count :]
     columns_kernel(y_count, x_count, place_ref, *halos, image_rows, *columns)
-    image_box_kernel(x_count, place_ref, sums_ref, image_ref, image_rows, *columns, box_ref, edges, image_outer)
+    image_late_kernel(x_count, place_ref, sums_ref, image_ref, image_rows, *columns, box_ref, edges, image_outer)
     warped_sums_kernel(own_sums_ref, rows_ref, image_rows, out_ref, outer_sums, *lines)
 
 
 HALF = NY // 2
 
 
-def force_kernel(x_count, place_ref, sums_ref, image_ref, own_ref, side_ref, rows_ref, *refs):
+def force_kernel(x_count, place_ref, sums_ref, image_ref, patch_ref, own_ref, side_ref, rows_ref, *refs):
     warped_halos, fixed_halos = refs[:x_count], refs[x_count : 2 * x_count]
     force_hbm, edges, force_ref, sems = refs[2 * x_count :]
     for k in range(x_count):
@@ -620,10 +638,16 @@
             own = own_ref[pl.ds(at + h, HALF), :]
             box = [sums_ref[f * NZ + z, part, :] for f in range(3)]
             box = add_edges(x_count, place_ref, z, box, edges, 4, h)
+            mean_f, image, inverse_f = [
+                jnp.concatenate([patch_ref[f * NZ + z, :VY, :], image_ref[f * NZ + z, VY:HALF, :]], 0)
+                if h == 0
+                else jnp.concatenate([image_ref[f * NZ + z, HALF : NY - VY, :], patch_ref[f * NZ + z, VY:, :]], 0)
+                for f in range(3)
+            ]
             mean_w = box[0] * scale
-            cov = box[2] * scale - image_ref[z, part, :] * mean_w
+            cov = box[2] * scale - mean_f * mean_w
             ratio = cov / (box[1] * scale - mean_w * mean_w + 1e-5)
-            half = (ratio * image_ref[2 * NZ + z, part, :]) * (image_ref[NZ + z, part, :] - ratio * (own - mean_w))
+            half = (ratio * inverse_f) * (image - ratio * (own - mean_w))
             up, down = own_ref[pl.ds(above + h, HALF), :], own_ref[pl.ds(below + h, HALF), :]
             up = jnp.where(z == NZ - 1, jnp.where(low, side_ref[part, :], 0.0), up)
             down = jnp.where(z == 0, jnp.where(low, 0.0, side_ref[(RAD - 1) * NY + h : (RAD - 1) * NY + h + HALF, :]), down)
@@ -710,35 +734,40 @@
     image_sent = rows_to_send(place, image_face, image_side, *image_packed)
     image_halos = exchange_rows(image_sent)
     weights = spread_weights(counts, mix_z)
-    image_sums, image_planes = call(
-        lambda place_ref, own_ref, side_ref, sums_ref, image_ref: own_kernel(
-            False, place_ref, own_ref, side_ref, image_ref, sums_ref
-        ),
-        (array(2 * NZ, NY, NX), array(EZ, NY, NX)),
+    image_box, image_sums = call(
+        lambda *refs: image_early_kernel(count, *refs),
+        (array(3 * NZ, NY, NX), array(2 * NZ, 2 * VY, NX)),
         place,
         image,
         image_side,
+        *image_packed,
+        scratch=(
+            pltpu.VMEM((2 * NZ, NY, NX), F32),
+            pltpu.VMEM((2 * NZ, NY, NX), F32),
+            pltpu.VMEM((2 * count, NY, NX), F32),
+        )
+        + LINES,
     )
-    image_sums = call(image_sums_kernel, array(2 * NZ, NY, NX), place, image_sums, scratch=LINES)
-    received, weights, image_sums = lax.optimization_barrier((received, weights, image_sums))
+    received, weights, image_box = lax.optimization_barrier((received, weights, image_box))
     warped, side, face = mix(flat, place, received, weights, mix_yx.reshape(SLOTS, BV, BV))
     side = exchange_planes(side)
     row_halos = exchange_rows(rows_to_send(place, face, side))
     own_sums, out, *packed = call(
-        lambda *refs: own_kernel(True, *refs),
+        own_kernel,
         (array(3 * NZ, NY, NX), array(NZ * NY, NX)) + (array(NY, NX),) * count,
         place,
         warped,
         side,
-        image_planes,
+        image,
+        image_side,
         scratch=(pltpu.SemaphoreType.DMA,),
         out_hbm=1,
     )
     rows, columns = pack_columns(place, row_halos, packed)
     columns = exchange_columns(columns)
-    image_box, box, *image_columns = call(
+    image_patch, box, *image_columns = call(
         lambda *refs: finish_kernel(len(image_halos), count, *refs),
-        (array(3 * NZ, NY, NX), array(3 * NZ, NY, NX)) + (array(EY, NX),) * count,
+        (array(3 * NZ, 2 * VY, NX), array(3 * NZ, NY, NX)) + (array(EY, NX),) * count,
         place,
         *image_halos,
         *image_packed,
@@ -748,7 +777,7 @@
         rows,
         scratch=(
             pltpu.VMEM((EZ, VY, NX), F32),
-            pltpu.VMEM((2 * count, NY, NX), F32),
+            pltpu.VMEM((2 * count, 2 * VY, NX), F32),
             pltpu.VMEM((2 * NZ, VY, NX), F32),
             pltpu.VMEM((3 * NZ, VY, NX), F32),
         )
@@ -760,6 +789,7 @@
         place,
         box,
         image_box,
+        image_patch,
         warped,
         side,
         rows,

time: 72.2 us -> 72.6 us (level)
  the two profiles are of different devices: /device:TPU:4 before, /device:TPU:14 now
where the time goes in v7:
time: 72.6 us; the launch traced here: 71.4 us
  Pallas kernels  26.6 us (37%)
  starting transfers between devices  20.3 us (28%)
  waiting for transfers between devices  13.3 us (18%)
  blocking collectives  7.21 us (10%)
  local copies, waits for them, and re-layouts  2.7 us (4%)
  between operations  0.86 us (1%)
    pallas_call x8, Pallas kernels, call(): pl.pallas_call(kernel, out_shape=outs, in_specs=[SMEM] + [VMEM] * (len(ar...  15 us
    ppermute x4, starting transfers between devices, exchange_rows(): lax.ppermute(s, 'gy', pairs)  10.8 us
    ppermute x2, waiting for transfers between devices, exchange_columns(): return [lax.ppermute(c, 'gx', pairs) for c, pairs in zip(columns, along)]  7.66 us
    all_to_all x1, blocking collectives, exchange_in_half(): lax.all_to_all(array, BRICKS, split_axis=0, concat_axis=0, tiled=True, ax...  7.21 us
    all_to_all x1, starting transfers between devices, exchange_in_half(): lax.all_to_all(array, BRICKS, split_axis=0, concat_axis=0, tiled=True, ax...  5.23 us
    pallas_call x1, Pallas kernels, mix(): pl.pallas_call(mix_kernel, out_shape=OUTER, in_specs=[SMEM, SMEM, VMEM, V...  4.81 us
    ppermute x1, waiting for transfers between devices, ask(): lax.ppermute(near, 'gy', [(i, (i + rows_gy // 2) % rows_gy) for i in rang...  3.86 us
    ppermute x1, starting transfers between devices, ask(): lax.ppermute(near, 'gy', [(i, (i + rows_gy // 2) % rows_gy) for i in rang...  2.65 us
  transfers between devices with their start and end apart: 10, of which 4 were waited for; matrix products, arithmetic and copies ran while one was open for 2% of the time, Pallas kernels for 19%

profile of v7, /device:TPU:14, one launch (start us, length us, event | category | flops | bytes accessed | tf_op | source)
XLA Modules:
  0.0 71.4 jit_solution(2684155283330694626)
XLA Ops:
  0.6 2.3 %prepare.1 = (bf16[128,8,128]{2,1,0:T(8,128)(2,1)S(1)}, s32[8,1,64]{2,1,0:T(1,128)S(1)}, s32[1,256]{1,0:T(1,128)S(1)}) custom-call(s32[1]{0:T(128)} %bitcast.3.half_ref, bf16[16,64,128]{2,1,0:T(8,128)(2,1)} %moving_hbm.1, s32[1,256]{1,0:T(1,128)} %bitcast.17, s32[1,256]{1,0:T(1,128)} %bitcast.18), custom_call_target="tpu_custom_call" | custom-call | tf_op jit(solution)/shard_map/prepare/pallas_call | solution.py:139
  2.9 2.7 %collective-permute-start = (bf16[128,8,128]{2,1,0:T(8,128)(2,1)S(1)}, bf16[128,8,128]{2,1,0:T(8,128)(2,1)S(1)}, u32[]{:S(2)}, u32[]{:S(2)}) collective-permute-start(bf16[128,8,128]{2,1,0:T(8,128)(2,1)S(1)} %get-tuple-element.30.refs_1_), channel_id=1, source_target_pairs={{0,8},{2,10},{4,12},{6,14},{8,0},{10,2},{12,4},{14,6},{1,9},{3,11}... | collective-permute-start | bytes 786440 | tf_op jit(solution)/shard_map/ppermute | solution.py:300
  5.6 7.2 %all_to_all.10.refs_0_ = s32[8,1,64]{2,1,0:T(1,128)S(1)} all-to-all(s32[8,1,64]{2,1,0:T(1,128)S(1)} %get-tuple-element.29), channel_id=1, replica_groups={{0,1,2,3,4,5,6,7},{8,9,10,11,12,13,14,15},{16,17,18,19,20,21,22,23},{24..., dimensions={0} | all-to-all | bytes 4096 | tf_op jit(solution)/shard_map/all_to_all | solution.py:292
  12.8 3.9 %collective-permute-done.refs_2_ = bf16[128,8,128]{2,1,0:T(8,128)(2,1)S(1)} collective-permute-done((bf16[128,8,128]{2,1,0:T(8,128)(2,1)S(1)}, bf16[128,8,128]{2,1,0:T(8,128)(2,1)S(1)}, u32[]{:S(2)}, u32[]{:S(2)}) %collective-permute-start) | collective-permute-done | bytes 262176 | tf_op jit(solution)/shard_map/ppermute | solution.py:300
  16.6 2.0 %pick.1 = bf16[512,8,128]{2,1,0:T(8,128)(2,1)} custom-call(s32[8,1,64]{2,1,0:T(1,128)S(1)} %all_to_all.10.refs_0_, bf16[128,8,128]{2,1,0:T(8,128)(2,1)S(1)} %get-tuple-element.30.refs_1_, bf16[128,8,128]{2,1,0:T(8,128)(2,1)S(1)} %collective-permute-done.refs_2_), custom_call_target="tpu_custom_call" | custom-call | tf_op jit(solution)/shard_map/pick/pallas_call | solution.py:170
  18.7 5.2 %all-to-all-start.1 = ((bf16[8,64,8,128]{3,2,1,0:T(8,128)(2,1)}), bf16[8,64,8,128]{3,2,1,0:T(8,128)(2,1)S(1)}, u32[]{:S(2)}, u32[]{:S(2)}) async-start(bf16[8,64,8,128]{3,2,1,0:T(8,128)(2,1)} %bitcast.7), calls=%async_computation.1 | async-start | bytes 2097152 | tf_op jit(solution)/shard_map/all_to_all | solution.py:292
  24.0 1.5 %image.1 = (f32[1024,128]{1,0:T(8,128)S(1)}, f32[256,128]{1,0:T(8,128)S(1)}, f32[16,8,128]{2,1,0:T(8,128)S(1)}) custom-call(s32[3]{0:T(128)S(1)} %pad_add_fusion.place_ref.refs_0_, bf16[16,64,128]{2,1,0:T(8,128)(2,1)} %fixed_hbm.1), custom_call_target="tpu_custom_call" | custom-call | tf_op jit(solution)/shard_map/image/pallas_call | solution.py:125
  25.7 0.1 reshape.64
  25.8 0.1 broadcast_in_dim.21
  25.9 0.1 broadcast_in_dim.22
  26.1 0.4 copy.10
  26.5 0.4 collective-permute-done.1.side_ref.refs_2_.image_side_ref
  26.9 1.0 %shard_map.86 = f32[64,128]{1,0:T(8,128)S(1)} custom-call(s32[3]{0:T(128)S(1)} %pad_add_fusion.place_ref.refs_0_, f32[1024,128]{1,0:T(8,128)S(1)} %get-tuple-element.31.own_ref.refs_1_.image_ref.refs_5_, f32[256,128]{1,0:T(8,128)S(1)} %collective-permute-done.1.side_ref.refs_2_.image_side_ref), custom_call_target="tpu_custom_call" | custom-call | tf_op jit(solution)/shard_map/pallas_call | solution.py:328
  28.0 0.6 collective-permute-start.2
  28.6 0.3 bitcast_select_fusion.mix_ref
  28.9 1.0 %spread.1.spread_ref = bf16[16,384,128]{2,1,0:T(8,128)(2,1)S(1)} custom-call(f32[2048,8]{1,0:T(8,128)S(1)} %bitcast_select_fusion.mix_ref), custom_call_target="tpu_custom_call" | custom-call | tf_op jit(solution)/shard_map/spread/pallas_call | solution.py:195
  29.9 7.7 %collective-permute-done.2.refs_3_ = f32[64,128]{1,0:T(8,128)S(1)} collective-permute-done((f32[64,128]{1,0:T(8,128)S(1)}, f32[64,128]{1,0:T(8,128)S(1)}, u32[]{:S(2)}, u32[]{:S(2)}) %collective-permute-start.2) | collective-permute-done | bytes 32800 | tf_op jit(solution)/shard_map/ppermute | solution.py:710
  37.6 3.7 %shard_map.87 = (f32[48,64,128]{2,1,0:T(8,128)S(1)}, f32[32,16,128]{2,1,0:T(8,128)S(1)}) custom-call(s32[3]{0:T(128)S(1)} %pad_add_fusion.place_ref.refs_0_, f32[1024,128]{1,0:T(8,128)S(1)} %get-tuple-element.31.own_ref.refs_1_.image_ref.refs_5_, f32[256,128]{1,0:T(8,128)S(1)} %collective-permute-done.1.side_ref.refs_2_.image_side_ref, ...), custom_call_target="tpu_custom_call" | custom-call | tf_op jit(solution)/shard_map/pallas_call | solution.py:328
  41.4 1.1 %copy-done = f32[48,64,128]{2,1,0:T(8,128)} copy-done((f32[48,64,128]{2,1,0:T(8,128)}, f32[48,64,128]{2,1,0:T(8,128)S(1)}, u32[]{:S(2)}) %copy-start) | copy-done | bytes 1572888
  42.5 0.7 copy-done.2
  43.2 4.8 %mix.1 = (f32[1024,128]{1,0:T(8,128)S(1)}, f32[256,128]{1,0:T(8,128)S(1)}, f32[16,8,128]{2,1,0:T(8,128)S(1)}) custom-call(s32[3]{0:T(128)S(1)} %pad_add_fusion.place_ref.refs_0_, s32[256]{0:T(256)S(1)} %bitcast.15, bf16[512,8,128]{2,1,0:T(8,128)(2,1)S(1)} %bitcast.14, bf16[16,384,128]{2,1,0:T(8,128)(2,1)S(1)} %spread.1.spread_ref, ...), custom_call_target="tpu_custom_call" | custom-call | tf_op jit(solution)/shard_map/mix/pallas_call | solution.py:268
  48.1 1.3 %collective-permute-done.3.side_ref.refs_2_.refs_5_ = f32[256,128]{1,0:T(8,128)S(1)} collective-permute-done((f32[256,128]{1,0:T(8,128)S(1)}, f32[256,128]{1,0:T(8,128)S(1)}, u32[]{:S(2)}, u32[]{:S(2)}) %collective-permute-start.3) | collective-permute-done | bytes 131104 | tf_op jit(solution)/shard_map/ppermute | solution.py:688
  49.4 0.6 shard_map.90
  50.0 0.4 collective-permute-start.6
  50.3 5.5 %collective-permute-start.7 = (f32[20,4,128]{2,1,0:T(4,128)S(1)}, f32[20,4,128]{2,1,0:T(4,128)S(1)}, u32[]{:S(2)}, u32[]{:S(2)}) collective-permute-start(f32[20,4,128]{2,1,0:T(4,128)S(1)} %get-tuple-element.46), channel_id=1, source_target_pairs={{2,4},{4,2},{6,8},{8,6},{10,12},{12,10},{3,5},{5,3},{7,9},{9,7},{1... | collective-permute-start | bytes 122888 | tf_op jit(solution)/shard_map/ppermute | solution.py:705
  55.9 0.6 shard_map.89
  56.5 4.9 %collective-permute-start.5 = (f32[21,4,128]{2,1,0:T(4,128)S(1)}, f32[21,4,128]{2,1,0:T(4,128)S(1)}, u32[]{:S(2)}, u32[]{:S(2)}) collective-permute-start(f32[21,4,128]{2,1,0:T(4,128)S(1)} %get-tuple-element.41), channel_id=1, source_target_pairs={{2,4},{4,2},{6,8},{8,6},{10,12},{12,10},{3,5},{5,3},{7,9},{9,7},{1... | collective-permute-start | bytes 129032 | tf_op jit(solution)/shard_map/ppermute | solution.py:705
  61.4 1.4 %shard_map.88 = (f32[48,64,128]{2,1,0:T(8,128)S(1)}, f32[1024,128]{1,0:T(8,128)}, f32[64,128]{1,0:T(8,128)S(1)}) custom-call(s32[3]{0:T(128)S(1)} %pad_add_fusion.place_ref.refs_0_, f32[1024,128]{1,0:T(8,128)S(1)} %get-tuple-element.36.own_ref.refs_4_, f32[256,128]{1,0:T(8,128)S(1)} %collective-permute-done.3.side_ref.refs_2_.refs_5_, ...), custom_call_target="tpu_custom_call" | custom-call | tf_op jit(solution)/shard_map/pallas_call | solution.py:328
  62.8 0.6 shard_map.91
  63.4 0.8 %collective-permute-start.8 = (f32[72,128]{1,0:T(8,128)S(1)}, f32[72,128]{1,0:T(8,128)S(1)}, u32[]{:S(2)}, u32[]{:S(2)}) collective-permute-start(f32[72,128]{1,0:T(8,128)S(1)} %get-tuple-element.52), channel_id=1, source_target_pairs={{0,1},{1,0},{2,3},{3,2},{4,5},{5,4},{6,7},{7,6},{8,9},{9,8},{10,11... | collective-permute-start | bytes 110600 | tf_op jit(solution)/shard_map/ppermute | solution.py:710
  64.3 4.0 %shard_map.92 = (f32[48,16,128]{2,1,0:T(8,128)S(1)}, f32[48,64,128]{2,1,0:T(8,128)S(1)}, f32[72,128]{1,0:T(8,128)S(1)}) custom-call(s32[3]{0:T(128)S(1)} %pad_add_fusion.place_ref.refs_0_, f32[21,4,128]{2,1,0:T(4,128)S(1)} %collective-permute-done.4.refs_1_, f32[21,4,128]{2,1,0:T(4,128)S(1)} %collective-permute-done.5.refs_2_, ...), custom_call_target="tpu_custom_call" | custom-call | tf_op jit(solution)/shard_map/pallas_call | solution.py:328
  68.3 3.1 %shard_map.93 = f32[3,16,64,128]{3,2,1,0:T(8,128)} custom-call(s32[3]{0:T(128)S(1)} %pad_add_fusion.place_ref.refs_0_, f32[48,64,128]{2,1,0:T(8,128)S(1)} %get-tuple-element.49.refs_1_, f32[48,64,128]{2,1,0:T(8,128)S(1)} %copy-done.1, f32[48,16,128]{2,1,0:T(8,128)S(1)} %get-tuple-element.51.refs_3_, f32[1024,128]{1,0:T(8,128)S(1)} %get-tuple-element.36.own_ref.refs_4_, ...), custom_call_target="tpu_custom_call" | custom-call | tf_op jit(solution)/shard_map/pallas_call | solution.py:328
  (22 shorter events, 0.4 us)
Async XLA Ops:
  2.9 13.7 %collective-permute-start = (bf16[128,8,128]{2,1,0:T(8,128)(2,1)S(1)}, bf16[128,8,128]{2,1,0:T(8,128)(2,1)S(1)}, u32[]{:S(2)}, u32[]{:S(2)}) collective-permute-start(bf16[128,8,128]{2,1,0:T(8,128)(2,1)S(1)} %get-tuple-element.30.refs_1_), channel_id=1, source_target_pairs={{0,8},{2,10},{4,12},{6,14},{8,0},{10,2},{12,4},{14,6},{1,9},{3,11}... | collective-permute-start | bytes 786440 | tf_op jit(solution)/shard_map/ppermute | solution.py:300
  18.6 6.9 %copy-start.5 = (s32[1,1,1,128]{3,2,1,0:T(1,128)S(1)}, s32[1,1,1,128]{3,2,1,0:T(1,128)}, u32[]{:S(2)}) copy-start(s32[1,1,1,128]{3,2,1,0:T(1,128)} %param.11) | copy-start | bytes 1540
  18.6 7.4 %copy-start.4 = (f32[1,1,1,256,8,8]{3,5,4,2,1,0:T(8,128)S(1)}, f32[1,1,1,256,8,8]{3,5,4,2,1,0:T(8,128)}, u32[]{:S(2)}) copy-start(f32[1,1,1,256,8,8]{3,5,4,2,1,0:T(8,128)} %param.13) | copy-start | bytes 196612
  18.7 24.5 %all-to-all-start.1 = ((bf16[8,64,8,128]{3,2,1,0:T(8,128)(2,1)}), bf16[8,64,8,128]{3,2,1,0:T(8,128)(2,1)S(1)}, u32[]{:S(2)}, u32[]{:S(2)}) async-start(bf16[8,64,8,128]{3,2,1,0:T(8,128)(2,1)} %bitcast.7), calls=%async_computation.1 | async-start | bytes 2097152 | tf_op jit(solution)/shard_map/all_to_all | solution.py:292
  25.5 1.4 %collective-permute-start.1 = (f32[256,128]{1,0:T(8,128)S(1)}, f32[256,128]{1,0:T(8,128)S(1)}, u32[]{:S(2)}, u32[]{:S(2)}) collective-permute-start(f32[256,128]{1,0:T(8,128)S(1)} %get-tuple-element.32), channel_id=1, source_target_pairs={{0,16},{16,0},{1,17},{17,1},{2,18},{18,2},{3,19},{19,3},{4,20},{20... | collective-permute-start | bytes 393224 | tf_op jit(solution)/shard_map/ppermute | solution.py:688
  28.0 9.6 %collective-permute-start.2 = (f32[64,128]{1,0:T(8,128)S(1)}, f32[64,128]{1,0:T(8,128)S(1)}, u32[]{:S(2)}, u32[]{:S(2)}) collective-permute-start(f32[64,128]{1,0:T(8,128)S(1)} %shard_map.86), channel_id=1, source_target_pairs={{0,1},{1,0},{2,3},{3,2},{4,5},{5,4},{6,7},{7,6},{8,9},{9,8},{10,11... | collective-permute-start | bytes 98312 | tf_op jit(solution)/shard_map/ppermute | solution.py:710
  41.3 1.1 %copy-start = (f32[48,64,128]{2,1,0:T(8,128)}, f32[48,64,128]{2,1,0:T(8,128)S(1)}, u32[]{:S(2)}) copy-start(f32[48,64,128]{2,1,0:T(8,128)S(1)} %get-tuple-element.50.refs_2_) | copy-start | bytes 4718596
  42.5 0.7 copy-start.2
  48.0 16.3 %copy-start.3 = (f32[32,16,128]{2,1,0:T(8,128)S(1)}, f32[32,16,128]{2,1,0:T(8,128)}, u32[]{:S(2)}) copy-start(f32[32,16,128]{2,1,0:T(8,128)} %copy-done.2) | copy-start | bytes 786436
  48.0 1.4 %collective-permute-start.3 = (f32[256,128]{1,0:T(8,128)S(1)}, f32[256,128]{1,0:T(8,128)S(1)}, u32[]{:S(2)}, u32[]{:S(2)}) collective-permute-start(f32[256,128]{1,0:T(8,128)S(1)} %get-tuple-element.37), channel_id=1, source_target_pairs={{0,16},{16,0},{1,17},{17,1},{2,18},{18,2},{3,19},{19,3},{4,20},{20... | collective-permute-start | bytes 393224 | tf_op jit(solution)/shard_map/ppermute | solution.py:688
  50.0 12.8 %collective-permute-start.6 = (f32[20,4,128]{2,1,0:T(4,128)S(1)}, f32[20,4,128]{2,1,0:T(4,128)S(1)}, u32[]{:S(2)}, u32[]{:S(2)}) collective-permute-start(f32[20,4,128]{2,1,0:T(4,128)S(1)} %get-tuple-element.45), channel_id=1, source_target_pairs={{0,2},{2,0},{4,6},{6,4},{8,10},{10,8},{12,14},{14,12},{1,3},{3,1},... | collective-permute-start | bytes 122888 | tf_op jit(solution)/shard_map/ppermute | solution.py:705
  50.3 12.4 %collective-permute-start.7 = (f32[20,4,128]{2,1,0:T(4,128)S(1)}, f32[20,4,128]{2,1,0:T(4,128)S(1)}, u32[]{:S(2)}, u32[]{:S(2)}) collective-permute-start(f32[20,4,128]{2,1,0:T(4,128)S(1)} %get-tuple-element.46), channel_id=1, source_target_pairs={{2,4},{4,2},{6,8},{8,6},{10,12},{12,10},{3,5},{5,3},{7,9},{9,7},{1... | collective-permute-start | bytes 122888 | tf_op jit(solution)/shard_map/ppermute | solution.py:705
  56.4 7.8 %collective-permute-start.4 = (f32[21,4,128]{2,1,0:T(4,128)S(1)}, f32[21,4,128]{2,1,0:T(4,128)S(1)}, u32[]{:S(2)}, u32[]{:S(2)}) collective-permute-start(f32[21,4,128]{2,1,0:T(4,128)S(1)} %get-tuple-element.40), channel_id=1, source_target_pairs={{0,2},{2,0},{4,6},{6,4},{8,10},{10,8},{12,14},{14,12},{1,3},{3,1},... | collective-permute-start | bytes 129032 | tf_op jit(solution)/shard_map/ppermute | solution.py:705
  56.5 7.8 %collective-permute-start.5 = (f32[21,4,128]{2,1,0:T(4,128)S(1)}, f32[21,4,128]{2,1,0:T(4,128)S(1)}, u32[]{:S(2)}, u32[]{:S(2)}) collective-permute-start(f32[21,4,128]{2,1,0:T(4,128)S(1)} %get-tuple-element.41), channel_id=1, source_target_pairs={{2,4},{4,2},{6,8},{8,6},{10,12},{12,10},{3,5},{5,3},{7,9},{9,7},{1... | collective-permute-start | bytes 129032 | tf_op jit(solution)/shard_map/ppermute | solution.py:705
  62.7 5.5 %copy-start.1 = (f32[48,64,128]{2,1,0:T(8,128)S(1)}, f32[48,64,128]{2,1,0:T(8,128)}, u32[]{:S(2)}) copy-start(f32[48,64,128]{2,1,0:T(8,128)} %copy-done) | copy-start | bytes 4718596
  63.4 4.8 %collective-permute-start.8 = (f32[72,128]{1,0:T(8,128)S(1)}, f32[72,128]{1,0:T(8,128)S(1)}, u32[]{:S(2)}, u32[]{:S(2)}) collective-permute-start(f32[72,128]{1,0:T(8,128)S(1)} %get-tuple-element.52), channel_id=1, source_target_pairs={{0,1},{1,0},{2,3},{3,2},{4,5},{5,4},{6,7},{7,6},{8,9},{9,8},{10,11... | collective-permute-start | bytes 110600 | tf_op jit(solution)/shard_map/ppermute | solution.py:710
